TPU v7x, 32 devices: a whole 2x2x4 slice. The times are simulated.
32 devices in a mesh: sweep: 2 (over core), cx: 4 (over y, x), cy: 4 (over z).
Axes of the slice: x: 2, y: 2, z: 4, core: 2. Of those that a mesh axis runs over, the one named last changes fastest.
Arguments:
- right_side: bfloat16 [8, 135, 16, 512], P('sweep', None, 'cx', 'cy'), may hold values from -6 to 6
- previous: bfloat16 [8, 135, 16, 512], P('sweep', None, 'cx', 'cy'), may hold values from -6 to 6
- diag_inverse: float32 [4, 135, 135], replicated
- face_blocks: float32 [4, 6, 135, 135], replicated
- pattern: int32 [8], P('sweep'), may hold values from 0 to 3
- live_count: int32 [8, 4, 4], P('sweep', 'cx', 'cy'), may hold values from 384 to 512, as said below
Outputs:
- solution: float32 [8, 135, 16, 512], P('sweep', None, 'cx', 'cy')
Inputs may be any that keep to these rules, and one draw needn't show every extreme that they name: In a device's band the slots are numbered i * 128 + j by the device's own cell indices; the first live_count of them hold elements. In every draw some band of some device holds 512 elements.
All inputs are finite; a program needn't handle non-finite values.
Results may differ from a plain program's by a relative error of at most 0.0003.
Values may be sent and summed in bfloat16 or wider, within the bound.
No kernel may reach another device: no remote copies, remote signals or barrier semaphores. Data moves between devices by JAX's collectives and lax.ppermute only.
A program may use at most 64 MiB of HBM per device.

v0:
```python
import jax
import jax.numpy as jnp
from jax import lax
from jax.sharding import PartitionSpec as P

PATTERNS = 4


full_precision = lax.Precision.HIGHEST


def padded(cells, sides, width):
    for axis, dim in sides:
        count = lax.axis_size(axis)
        ends = count - 1
        head = lax.slice_in_dim(cells, 0, width, axis=dim)
        tail = lax.slice_in_dim(cells, cells.shape[dim] - width, cells.shape[dim], axis=dim)
        cells = jnp.concatenate(
            [
                lax.ppermute(tail, axis, [(i, (i + 1) % count) for i in range(ends)]),
                cells,
                lax.ppermute(head, axis, [((i + 1) % count, i) for i in range(ends)]),
            ],
            axis=dim,
        )
    return cells


def passed_along(value, axis, steps):
    count = lax.axis_size(axis)
    first, last = (max(0, -steps), min(count, count - steps))
    return lax.ppermute(value, axis, [(source, source + steps) for source in range(first, last)])


def contract(blocks, fields):
    return jnp.einsum("buv,bvc->buc", blocks, fields, precision=full_precision)


def on_device(right_side, previous, diag_inverse, face_blocks, pattern, live_count):
    band_total, unknowns, across, along_y = right_side.shape
    cell_total = across * along_y
    extended = padded(previous, (("cx", 2), ("cy", 3)), 1)
    following = passed_along(previous[0], "sweep", -1)
    selector = (pattern[:, None] == jnp.arange(PATTERNS, dtype=jnp.int32)[None, :]).astype(
        jnp.float32
    )
    inverses = jnp.einsum("bp,puv->buv", selector, diag_inverse, precision=full_precision)
    couplings = jnp.einsum("bp,pfuv->bfuv", selector, face_blocks, precision=full_precision)
    transfer = -jnp.einsum("buv,bvw->buw", inverses, couplings[:, 0], precision=full_precision)
    downstream = jnp.concatenate([previous[1:], following[None]], axis=0)
    neighbours = (
        downstream,
        extended[:, :, :-2, 1:-1],
        extended[:, :, 2:, 1:-1],
        extended[:, :, 1:-1, :-2],
        extended[:, :, 1:-1, 2:],
    )
    residual_base = right_side.astype(jnp.float32).reshape(band_total, unknowns, cell_total)
    for face_index in range(5):
        neighbour_field = (
            neighbours[face_index].astype(jnp.float32).reshape(band_total, unknowns, cell_total)
        )
        residual_base = residual_base - contract(couplings[:, face_index + 1], neighbour_field)
    local_part = contract(inverses, residual_base)
    slot_index = jnp.arange(cell_total, dtype=jnp.int32)
    live_mask = (slot_index[None, :] < live_count.reshape(band_total, 1)).astype(jnp.float32)

    def advance(carry, inputs):
        current, product, still_live = carry
        offset, step_map, live_row = inputs
        current = live_row[None, :] * (
            offset + jnp.dot(step_map, current, precision=full_precision)
        )
        product = jnp.dot(step_map, product, precision=full_precision)
        still_live = still_live * live_row
        return ((current, product, still_live), (current, product, still_live))

    initial = (
        jnp.zeros((unknowns, cell_total), jnp.float32),
        jnp.eye(unknowns, dtype=jnp.float32),
        jnp.ones((cell_total,), jnp.float32),
    )
    final_carry, history = lax.scan(advance, initial, (local_part, transfer, live_mask))
    states, products, live_prefix = history
    end_state, end_map, end_live = final_carry

    def relay(segment_index, incoming):
        outgoing = (
            end_live[None, :] * jnp.dot(end_map, incoming, precision=full_precision) + end_state
        )
        return passed_along(outgoing, "sweep", 1)

    incoming = lax.fori_loop(
        0, lax.axis_size("sweep") - 1, relay, jnp.zeros((unknowns, cell_total), jnp.float32)
    )
    carried = jnp.einsum("buv,vc->buc", products, incoming, precision=full_precision)
    solution = states + live_prefix[:, None, :] * carried
    return solution.reshape(band_total, unknowns, across, along_y)


def solution(mesh):
    return jax.shard_map(
        on_device,
        mesh=mesh,
        in_specs=(
            P("sweep", None, "cx", "cy"),
            P("sweep", None, "cx", "cy"),
            P(),
            P(),
            P("sweep"),
            P("sweep", "cx", "cy"),
        ),
        out_specs=P("sweep", None, "cx", "cy"),
        check_vma=False,
    )
```

profile of v0, /device:TPU:11, one launch (start us, length us, event | category | flops | bytes accessed | tf_op | source)
XLA Modules:
  0.0 94.1 jit_solution(17032525774755919975)
XLA Ops:
  0.0 1.9 %fusion.44 = (bf16[4,135,1,128]{3,2,1,0:T(2,128)(2,1)S(1)}, bf16[4,135,1,128]{3,2,1,0:T(2,128)(2,1)S(1)}) fusion(bf16[4,135,4,128]{3,2,1,0:T(4,128)(2,1)} %param.9), kind=kLoop, calls=%fused_computation.75 | loop fusion | bytes 552960 | tf_op jit(solution)/shard_map/slice | solution.py:16
  2.6 3.1 %collective-permute-start.1 = (bf16[4,135,1,128]{3,0,2,1:T(4,128)(2,1)}, bf16[4,135,1,128]{3,0,2,1:T(4,128)(2,1)}, u32[]{:S(2)}, u32[]{:S(2)}) collective-permute-start(bf16[4,135,1,128]{3,0,2,1:T(4,128)(2,1)} %copy.33), channel_id=1, source_target_pairs={{0,4},{4,8},{8,12},{1,5},{5,9},{9,13},{2,6},{6,10},{10,14},{3,7},{... | collective-permute-start | bytes 414728 | tf_op jit(solution)/shard_map/ppermute | solution.py:20
  6.5 2.8 %collective-permute-start.2 = (bf16[4,135,1,128]{3,0,2,1:T(4,128)(2,1)}, bf16[4,135,1,128]{3,0,2,1:T(4,128)(2,1)}, u32[]{:S(2)}, u32[]{:S(2)}) collective-permute-start(bf16[4,135,1,128]{3,0,2,1:T(4,128)(2,1)} %copy.34), channel_id=1, source_target_pairs={{4,0},{8,4},{12,8},{5,1},{9,5},{13,9},{6,2},{10,6},{14,10},{7,3},{... | collective-permute-start | bytes 414728 | tf_op jit(solution)/shard_map/ppermute | solution.py:22
  10.0 3.8 %collective-permute-start = (bf16[135,4,128]{2,1,0:T(4,128)(2,1)}, bf16[135,4,128]{2,1,0:T(4,128)(2,1)}, u32[]{:S(2)}, u32[]{:S(2)}) collective-permute-start(bf16[135,4,128]{2,1,0:T(4,128)(2,1)} %slice_bitcast_fusion.6), channel_id=1, source_target_pairs={{16,0},{17,1},{18,2},{19,3},{20,4},{21,5},{22,6},{23,7},{24,8},{25... | collective-permute-start | bytes 414728 | tf_op jit(solution)/shard_map/ppermute | solution.py:32
  13.8 3.4 %fusion.38 = f32[4,6,135,135]{3,0,2,1:T(4,128)S(1)} fusion(f32[4,6,135,135]{3,0,2,1:T(4,128)S(1)} %copy-done, s32[4]{0:T(128)S(1)} %copy-done.15), kind=kOutput, calls=%fused_computation.70 | convolution fusion | flops 20995216 | bytes 3499216 | tf_op jit(solution)/shard_map/bp,pfuv->bfuv/dot_general | solution.py:48
  23.0 2.7 %copy.21 = bf16[4,135,4,128]{1,0,3,2:T(4,128)(2,1)} copy(bf16[4,135,4,128]{3,2,1,0:T(4,128)(2,1)} %param.9) | data formatting | bytes 1105920 | tf_op args[1]
  25.7 2.2 %reshape.38 = f32[4,135,512]{2,1,0:T(8,128)} reshape(bf16[4,135,4,128]{3,2,1,0:T(4,128)(2,1)} %param.8) | data formatting | bytes 1658880 | tf_op jit(solution)/shard_map/reshape | solution.py:58
  27.9 2.1 %concatenate.24 = bf16[3,135,512]{2,1,0:T(8,128)(2,1)} reshape(bf16[3,135,4,128]{3,2,1,0:T(4,128)(2,1)} %slice.53) | data formatting | bytes 829440 | tf_op jit(solution)/shard_map/concatenate | solution.py:50
  32.4 2.3 %pad_maximum_fusion.6 = (bf16[4,135,4,128]{3,2,1,0:T(4,128)(2,1)}, bf16[4,135,4,128]{3,2,1,0:T(4,128)(2,1)}) fusion(bf16[4,135,1,128]{3,2,1,0:T(2,128)(2,1)S(1)} %copy.18, bf16[4,135,4,128]{3,2,1,0:T(4,128)(2,1)S(1)} %copy-done.3, bf16[4,135,1,128]{3,2,1,0:T(2,128)(2,1)S(1)} %copy.15), kind=kLoop, calls=%fused_computation.48 | loop fusion | flops 2211840 | bytes 1935360 | tf_op jit(solution)/shard_map/concatenate | solution.py:18
  34.7 2.1 %reshape.32 = bf16[4,135,512]{2,1,0:T(8,128)(2,1)} reshape(bf16[4,135,4,128]{3,2,1,0:T(4,128)(2,1)} %get-tuple-element.151) | data formatting | bytes 1105920 | tf_op jit(solution)/shard_map/reshape | solution.py:61
  36.7 2.1 %reshape.33 = bf16[4,135,512]{2,1,0:T(8,128)(2,1)} reshape(bf16[4,135,4,128]{3,2,1,0:T(4,128)(2,1)} %get-tuple-element.150) | data formatting | bytes 1105920 | tf_op jit(solution)/shard_map/reshape | solution.py:61
  43.3 3.2 %collective-permute-start.3 = (bf16[4,135,6,1]{1,0,3,2:T(4,128)(2,1)S(1)}, bf16[4,135,6,1]{1,0,3,2:T(4,128)(2,1)S(1)}, u32[]{:S(2)}, u32[]{:S(2)}) collective-permute-start(bf16[4,135,6,1]{1,0,3,2:T(4,128)(2,1)S(1)} %get-tuple-element.149), channel_id=1, source_target_pairs={{0,1},{1,2},{2,3},{4,5},{5,6},{6,7},{8,9},{9,10},{10,11},{12,13},{... | collective-permute-start | bytes 19448 | tf_op jit(solution)/shard_map/ppermute | solution.py:20
  46.6 2.3 %collective-permute-start.4 = (bf16[4,135,6,1]{1,0,3,2:T(4,128)(2,1)S(1)}, bf16[4,135,6,1]{1,0,3,2:T(4,128)(2,1)S(1)}, u32[]{:S(2)}, u32[]{:S(2)}) collective-permute-start(bf16[4,135,6,1]{1,0,3,2:T(4,128)(2,1)S(1)} %get-tuple-element.148), channel_id=1, source_target_pairs={{1,0},{2,1},{3,2},{5,4},{6,5},{7,6},{9,8},{10,9},{11,10},{13,12},{... | collective-permute-start | bytes 19448 | tf_op jit(solution)/shard_map/ppermute | solution.py:22
  52.2 2.7 %fusion.13 = f32[4,135,512]{2,1,0:T(8,128)S(1)} fusion(f32[4,135,512]{2,1,0:T(8,128)} %fusion.24, f32[4,135,512]{2,1,0:T(8,128)} %reshape.38, bf16[1,135,512]{2,1,0:T(8,128)(2,1)} %concatenate.25, bf16[3,135,512]{2,1,0:T(8,128)(2,1)} %concatenate.24, f32[4,135,135]{2,0,1:T(4,128)} %get-tuple-element.145), kind=kOutput, calls=%fused_computation.23 | convolution fusion | flops 448727040 | bytes 4162320 | tf_op jit(solution)/shard_map/buv,bvc->buc/dot_general | solution.py:36
  56.3 1.9 %pad_maximum_fusion = (bf16[4,135,4,128]{1,0,3,2:T(4,128)(2,1)S(1)}, bf16[4,135,4,128]{1,0,3,2:T(4,128)(2,1)S(1)}) fusion(bf16[4,135,6,1]{1,0,3,2:T(4,128)(2,1)S(1)} %collective-permute-done.4, bf16[4,135,1,128]{1,0,3,2:T(4,128)(2,1)S(1)} %copy-done.7, bf16[4,135,4,128]{1,0,3,2:T(4,128)(2,1)S(1)} %copy-done.1, bf16[4,135,1,128]{1,0,3,2:T(4,128)(2,1)S(1)} %copy-done.6, ...), kind=kLoop, calls=%fused_computation.27 | loop fusion | flops 1658880 | bytes 1948320 | tf_op jit(solution)/shard_map/concatenate | solution.py:18
  60.6 2.1 %fusion.28 = f32[4,135,512]{2,1,0:T(8,128)} fusion(f32[4,135,512]{2,1,0:T(8,128)S(1)} %convolution_subtract_fusion, f32[4,135,135]{2,0,1:T(4,128)S(1)} %copy-done.5), kind=kOutput, calls=%fused_computation.54 | convolution fusion | flops 447897600 | bytes 2503440 | tf_op jit(solution)/shard_map/buv,bvc->buc/dot_general | solution.py:36
  62.8 20.5 %while.8 = (s32[]{:T(128)}, f32[135,512]{1,0:T(8,128)}, f32[135,135]{1,0:T(8,128)S(1)}, f32[512]{0:T(512)S(1)}, f32[4,135,512]{2,1,0:T(8,128)}, /*index=5*/f32[4...) while((s32[]{:T(128)}, f32[135,512]{1,0:T(8,128)}, ...), condition=%wide.region_1.2_spmd.clone, body=%wide.region_0.1_spmd.clone.sunk | while | flops 141707280 | bytes 2392984 | solution.py:83
  63.7 2.3 %bitcast_dynamic-update-slice_fusion.4 = (f32[4,135,512]{2,1,0:T(8,128)}, f32[135,512]{1,0:T(8,128)}) fusion(f32[4,135,512]{2,1,0:T(8,128)} %get-tuple-element.239, s32[]{:T(128)} %get-tuple-element.235, f32[135,512]{1,0:T(8,128)S(1)} %copy.81, pred[]{:T(512)S(6)} %compare.3, f32[4,135,135]{2,1,0:T(8,128)} %get-tuple-element.256, ...), kind=kOutput, calls=%fused_computation.2.clone.1 | convolution fusion | flops 112181760 | bytes 1254401 | tf_op jit(solution)/shard_map/while/body/eval_jaxpr/dot_general | solution.py:72
  68.9 2.2 %bitcast_dynamic-update-slice_fusion.4 = (f32[4,135,512]{2,1,0:T(8,128)}, f32[135,512]{1,0:T(8,128)}) fusion(f32[4,135,512]{2,1,0:T(8,128)} %get-tuple-element.239, s32[]{:T(128)} %get-tuple-element.235, f32[135,512]{1,0:T(8,128)S(1)} %copy.81, pred[]{:T(512)S(6)} %compare.3, f32[4,135,135]{2,1,0:T(8,128)} %get-tuple-element.256, ...), kind=kOutput, calls=%fused_computation.2.clone.1 | convolution fusion | flops 112181760 | bytes 1254401 | tf_op jit(solution)/shard_map/while/body/eval_jaxpr/dot_general | solution.py:72
  74.0 2.3 %bitcast_dynamic-update-slice_fusion.4 = (f32[4,135,512]{2,1,0:T(8,128)}, f32[135,512]{1,0:T(8,128)}) fusion(f32[4,135,512]{2,1,0:T(8,128)} %get-tuple-element.239, s32[]{:T(128)} %get-tuple-element.235, f32[135,512]{1,0:T(8,128)S(1)} %copy.81, pred[]{:T(512)S(6)} %compare.3, f32[4,135,135]{2,1,0:T(8,128)} %get-tuple-element.256, ...), kind=kOutput, calls=%fused_computation.2.clone.1 | convolution fusion | flops 112181760 | bytes 1254401 | tf_op jit(solution)/shard_map/while/body/eval_jaxpr/dot_general | solution.py:72
  79.1 2.3 %bitcast_dynamic-update-slice_fusion.4 = (f32[4,135,512]{2,1,0:T(8,128)}, f32[135,512]{1,0:T(8,128)}) fusion(f32[4,135,512]{2,1,0:T(8,128)} %get-tuple-element.239, s32[]{:T(128)} %get-tuple-element.235, f32[135,512]{1,0:T(8,128)S(1)} %copy.81, pred[]{:T(512)S(6)} %compare.3, f32[4,135,135]{2,1,0:T(8,128)} %get-tuple-element.256, ...), kind=kOutput, calls=%fused_computation.2.clone.1 | convolution fusion | flops 112181760 | bytes 1254401 | tf_op jit(solution)/shard_map/while/body/eval_jaxpr/dot_general | solution.py:72
  85.9 2.2 %collective-permute-done.5 = f32[135,512]{1,0:T(8,128)S(1)} collective-permute-done((f32[135,512]{1,0:T(8,128)S(1)}, f32[135,512]{1,0:T(8,128)S(1)}, u32[]{:S(2)}, u32[]{:S(2)}) %collective-permute-start.5) | collective-permute-done | bytes 276512 | tf_op jit(solution)/shard_map/while/body/eval_jaxpr/ppermute | solution.py:32
  88.1 3.5 %fusion.12 = f32[4,135,512]{2,1,0:T(8,128)} fusion(f32[4,135,512]{2,1,0:T(8,128)} %get-tuple-element.77, f32[4,135,135]{2,1,0:T(8,128)} %get-tuple-element.79, f32[4,512]{1,0:T(4,128)S(1)} %get-tuple-element.78, f32[135,512]{1,0:T(8,128)S(1)} %collective-permute-done.5), kind=kOutput, calls=%fused_computation.18 | convolution fusion | flops 448450560 | bytes 2788112 | tf_op jit(solution)/shard_map/buv,vc->buc/dot_general | solution.py:96
  91.5 2.6 %reshape.36 = f32[4,135,4,128]{3,2,1,0:T(4,128)} reshape(f32[4,135,512]{2,1,0:T(8,128)} %fusion.12) | data formatting | bytes 2211840 | tf_op jit(solution)/shard_map/reshape | solution.py:98
  (89 shorter events, 35.9 us)
Async XLA Ops:
  0.0 13.8 %copy-start = (f32[4,6,135,135]{3,0,2,1:T(4,128)S(1)}, f32[4,6,135,135]{3,0,2,1:T(4,128)}, u32[]{:S(2)}) copy-start(f32[4,6,135,135]{3,0,2,1:T(4,128)} %param.11) | copy-start | bytes 5248804
  0.0 9.3 %copy-start.2 = (bf16[4,135,4,128]{3,2,1,0:T(4,128)(2,1)S(1)}, bf16[4,135,4,128]{3,2,1,0:T(4,128)(2,1)}, u32[]{:S(2)}) copy-start(bf16[4,135,4,128]{3,2,1,0:T(4,128)(2,1)} %param.9) | copy-start | bytes 1658884
  0.0 13.8 %copy-start.15 = (s32[4]{0:T(128)S(1)}, s32[4]{0:T(128)}, u32[]{:S(2)}) copy-start(s32[4]{0:T(128)} %param.12) | copy-start | bytes 52
  2.6 27.4 %collective-permute-start.1 = (bf16[4,135,1,128]{3,0,2,1:T(4,128)(2,1)}, bf16[4,135,1,128]{3,0,2,1:T(4,128)(2,1)}, u32[]{:S(2)}, u32[]{:S(2)}) collective-permute-start(bf16[4,135,1,128]{3,0,2,1:T(4,128)(2,1)} %copy.33), channel_id=1, source_target_pairs={{0,4},{4,8},{8,12},{1,5},{5,9},{9,13},{2,6},{6,10},{10,14},{3,7},{... | collective-permute-start | bytes 414728 | tf_op jit(solution)/shard_map/ppermute | solution.py:20
  6.5 24.8 %collective-permute-start.2 = (bf16[4,135,1,128]{3,0,2,1:T(4,128)(2,1)}, bf16[4,135,1,128]{3,0,2,1:T(4,128)(2,1)}, u32[]{:S(2)}, u32[]{:S(2)}) collective-permute-start(bf16[4,135,1,128]{3,0,2,1:T(4,128)(2,1)} %copy.34), channel_id=1, source_target_pairs={{4,0},{8,4},{12,8},{5,1},{9,5},{13,9},{6,2},{10,6},{14,10},{7,3},{... | collective-permute-start | bytes 414728 | tf_op jit(solution)/shard_map/ppermute | solution.py:22
  10.0 40.5 %collective-permute-start = (bf16[135,4,128]{2,1,0:T(4,128)(2,1)}, bf16[135,4,128]{2,1,0:T(4,128)(2,1)}, u32[]{:S(2)}, u32[]{:S(2)}) collective-permute-start(bf16[135,4,128]{2,1,0:T(4,128)(2,1)} %slice_bitcast_fusion.6), channel_id=1, source_target_pairs={{16,0},{17,1},{18,2},{19,3},{20,4},{21,5},{22,6},{23,7},{24,8},{25... | collective-permute-start | bytes 414728 | tf_op jit(solution)/shard_map/ppermute | solution.py:32
  17.2 1.8 %copy-start.14 = (f32[4,135,135]{2,0,1:T(4,128)S(1)}, f32[4,135,135]{2,0,1:T(4,128)}, u32[]{:S(2)}) copy-start(f32[4,135,135]{2,0,1:T(4,128)} %param.10) | copy-start | bytes 874804
  19.6 0.8 copy-start.4
  19.6 2.4 %copy-start.16 = (s32[4,1,1]{0,2,1:T(1,128)S(1)}, s32[4,1,1]{0,2,1:T(1,128)}, u32[]{:S(2)}) copy-start(s32[4,1,1]{0,2,1:T(1,128)} %param.13) | copy-start | bytes 52
  30.0 2.3 %copy-start.3 = (bf16[4,135,4,128]{3,2,1,0:T(4,128)(2,1)S(1)}, bf16[4,135,4,128]{3,2,1,0:T(4,128)(2,1)}, u32[]{:S(2)}) copy-start(bf16[4,135,4,128]{3,2,1,0:T(4,128)(2,1)} %param.9) | copy-start | bytes 1658884
  42.5 6.3 %copy-start.9 = (f32[4,135,135]{2,0,1:T(4,128)S(1)}, f32[4,135,135]{2,0,1:T(4,128)}, u32[]{:S(2)}) copy-start(f32[4,135,135]{2,0,1:T(4,128)} %get-tuple-element.144) | copy-start | bytes 874804
  42.5 6.3 %copy-start.13 = (bf16[4,135,512]{2,1,0:T(8,128)(2,1)S(1)}, bf16[4,135,512]{2,1,0:T(8,128)(2,1)}, u32[]{:S(2)}) copy-start(bf16[4,135,512]{2,1,0:T(8,128)(2,1)} %reshape.32) | copy-start | bytes 1658884
  43.3 12.3 %collective-permute-start.3 = (bf16[4,135,6,1]{1,0,3,2:T(4,128)(2,1)S(1)}, bf16[4,135,6,1]{1,0,3,2:T(4,128)(2,1)S(1)}, u32[]{:S(2)}, u32[]{:S(2)}) collective-permute-start(bf16[4,135,6,1]{1,0,3,2:T(4,128)(2,1)S(1)} %get-tuple-element.149), channel_id=1, source_target_pairs={{0,1},{1,2},{2,3},{4,5},{5,6},{6,7},{8,9},{9,10},{10,11},{12,13},{... | collective-permute-start | bytes 19448 | tf_op jit(solution)/shard_map/ppermute | solution.py:20
  46.6 9.1 %collective-permute-start.4 = (bf16[4,135,6,1]{1,0,3,2:T(4,128)(2,1)S(1)}, bf16[4,135,6,1]{1,0,3,2:T(4,128)(2,1)S(1)}, u32[]{:S(2)}, u32[]{:S(2)}) collective-permute-start(bf16[4,135,6,1]{1,0,3,2:T(4,128)(2,1)S(1)} %get-tuple-element.148), channel_id=1, source_target_pairs={{1,0},{2,1},{3,2},{5,4},{6,5},{7,6},{9,8},{10,9},{11,10},{13,12},{... | collective-permute-start | bytes 19448 | tf_op jit(solution)/shard_map/ppermute | solution.py:22
  52.2 2.7 %copy-start.8 = (f32[4,135,135]{2,0,1:T(4,128)S(1)}, f32[4,135,135]{2,0,1:T(4,128)}, u32[]{:S(2)}) copy-start(f32[4,135,135]{2,0,1:T(4,128)} %get-tuple-element.143) | copy-start | bytes 874804
  52.2 2.7 %copy-start.12 = (bf16[4,135,512]{2,1,0:T(8,128)(2,1)S(1)}, bf16[4,135,512]{2,1,0:T(8,128)(2,1)}, u32[]{:S(2)}) copy-start(bf16[4,135,512]{2,1,0:T(8,128)(2,1)} %reshape.33) | copy-start | bytes 1658884
  54.9 1.2 %copy-start.1 = (bf16[4,135,4,128]{1,0,3,2:T(4,128)(2,1)S(1)}, bf16[4,135,4,128]{1,0,3,2:T(4,128)(2,1)}, u32[]{:S(2)}) copy-start(bf16[4,135,4,128]{1,0,3,2:T(4,128)(2,1)} %copy.21) | copy-start | bytes 1658884
  54.9 1.3 %copy-start.6 = (bf16[4,135,1,128]{1,0,3,2:T(4,128)(2,1)S(1)}, bf16[4,135,1,128]{1,0,3,2:T(4,128)(2,1)}, u32[]{:S(2)}) copy-start(bf16[4,135,1,128]{1,0,3,2:T(4,128)(2,1)} %copy.20) | copy-start | bytes 414724
  54.9 1.3 %copy-start.7 = (bf16[4,135,1,128]{1,0,3,2:T(4,128)(2,1)S(1)}, bf16[4,135,1,128]{1,0,3,2:T(4,128)(2,1)}, u32[]{:S(2)}) copy-start(bf16[4,135,1,128]{1,0,3,2:T(4,128)(2,1)} %copy.22) | copy-start | bytes 414724
  55.6 2.6 %copy-start.11 = (f32[4,135,135]{2,0,1:T(4,128)S(1)}, f32[4,135,135]{2,0,1:T(4,128)}, u32[]{:S(2)}) copy-start(f32[4,135,135]{2,0,1:T(4,128)} %get-tuple-element.142) | copy-start | bytes 874804
  58.2 1.2 %copy-start.10 = (f32[4,135,135]{2,0,1:T(4,128)S(1)}, f32[4,135,135]{2,0,1:T(4,128)}, u32[]{:S(2)}) copy-start(f32[4,135,135]{2,0,1:T(4,128)} %get-tuple-element.141) | copy-start | bytes 874804
  59.4 1.2 %copy-start.5 = (f32[4,135,135]{2,0,1:T(4,128)S(1)}, f32[4,135,135]{2,0,1:T(4,128)}, u32[]{:S(2)}) copy-start(f32[4,135,135]{2,0,1:T(4,128)} %copy-done.4) | copy-start | bytes 874804
  84.6 3.5 %collective-permute-start.5 = (f32[135,512]{1,0:T(8,128)S(1)}, f32[135,512]{1,0:T(8,128)S(1)}, u32[]{:S(2)}, u32[]{:S(2)}) collective-permute-start(f32[135,512]{1,0:T(8,128)S(1)} %fusion.14), channel_id=1, source_target_pairs={{0,16},{1,17},{2,18},{3,19},{4,20},{5,21},{6,22},{7,23},{8,24},{9,... | collective-permute-start | bytes 829448 | tf_op jit(solution)/shard_map/while/body/eval_jaxpr/ppermute | solution.py:32
where the time goes:
time: 95.3 us; the launch traced here: 94.1 us
  matrix products  36.4 us (38%)
  local copies, waits for them, and re-layouts  33.6 us (35%)
  starting transfers between devices  16.5 us (17%)
  other arithmetic  5.16 us (5%)
  waiting for transfers between devices  2.17 us (2%)
    dot_general x6, matrix products, contract(): return jnp.einsum('buv,bvc->buc', blocks, fields, precision=full_precision)  9.56 us
    dot_general x4, matrix products, advance(): jnp.dot(step_map, current, precision=full_precision)  9.05 us
    dot_general x4, matrix products, advance(): product = jnp.dot(step_map, product, precision=full_precision)  7.34 us
    ppermute x2, starting transfers between devices, padded(): lax.ppermute(tail, axis, [(i, (i + 1) % count) for i in range(ends)])  6.31 us
    unnamed x37, local copies, waits for them, and re-layouts  5.64 us
    ppermute x2, starting transfers between devices, passed_along(): lax.ppermute(value, axis, [(source, source + steps) for source in range(f...  5.09 us
    ppermute x2, starting transfers between devices, padded(): lax.ppermute(head, axis, [((i + 1) % count, i) for i in range(ends)])  5.06 us
    concatenate x3, other arithmetic, padded(): jnp.concatenate([lax.ppermute(tail, axis, [(i, (i + 1) % count) for i in...  5.04 us
  transfers between devices with their start and end apart: 6, of which 1 were waited for; matrix products, arithmetic and copies ran while one was open for 39% of the time, Pallas kernels for 0%

commit v1 on v0

v1 whole, which is shorter than its diff:
```python
import functools

import jax
import jax.numpy as jnp
from jax import lax
from jax.experimental import pallas as pl
from jax.experimental.pallas import tpu as pltpu
from jax.sharding import PartitionSpec as P

F32, BF16 = jnp.float32, jnp.bfloat16
VMEM = pl.BlockSpec(memory_space=pltpu.VMEM)
SMEM = pl.BlockSpec(memory_space=pltpu.SMEM)


def rounded(count, unit):
    return (count + unit - 1) // unit * unit


def padded_rows(count):
    return rounded(count, 16)


def product(left, right):
    return jnp.dot(left, right, preferred_element_type=F32)


def halves(value):
    high = value.astype(BF16)
    return high, (value - high.astype(F32)).astype(BF16)


def store_halves(ref, value):
    count = value.shape[0]
    start = padded_rows(count)
    high, low = halves(value)
    ref[0:count, :] = high
    ref[start : start + count, :] = low


def apply(stacked, right, count):
    both = product(stacked, right)
    start = padded_rows(count)
    return both[0:count] + both[start : start + count]


def apply_halves(stacked, right, count):
    high, low = right
    rest = product(stacked[0 : padded_rows(count)], low)
    return apply(stacked, high, count) + rest[0:count]


def lane_blocks(ref, start, count, across):
    return [ref[pl.ds(start + i, count, stride=across), :] for i in range(across)]


def pack_kernel(bands, count, across, prev, face_even, face_odd, side_even, side_odd, first, wide, rows_even, rows_odd):
    along = prev.shape[-1]
    odd_x = lax.axis_index("cx") % 2 == 1
    odd_y = lax.axis_index("cy") % 2 == 1
    wide[...] = prev[...].astype(F32)
    first[...] = prev[0 : count * across, :]
    row = lax.broadcasted_iota(jnp.int32, (8, along), 0)
    lane = lax.broadcasted_iota(jnp.int32, (8, along), 1)
    last = along - 1
    even_lane, odd_lane = jnp.where(odd_y, 0, last), jnp.where(odd_y, last, 0)
    chosen = jnp.where(row == 0, even_lane, odd_lane)
    pick = jnp.where(lane == chosen, 1.0, 0.0).astype(BF16)
    for z in range(bands):
        blocks = lane_blocks(wide, z * count * across, count, across)
        low, high = blocks[0], blocks[-1]
        face_even[z] = jnp.where(odd_x, low, high).astype(BF16)
        face_odd[z] = jnp.where(odd_x, high, low).astype(BF16)
        for i in range(across):
            found = lax.dot_general(
                pick, blocks[i].astype(BF16), (((1,), (1,)), ((), ())), preferred_element_type=F32
            )
            at = z * across + i
            rows_even[at : at + 1, :] = found[0:1]
            rows_odd[at : at + 1, :] = found[1:2]
    side_even[...] = rows_even[...].astype(BF16)
    side_odd[...] = rows_odd[...].astype(BF16)


def local_kernel(
    bands, count, across, pattern, right, prev, follow, side_even, side_odd, faces, inverses,
    base, reach, across_maps, inverse_maps, step_maps, wide, wide_right, wide_follow, sides, work, reach_work,
):
    along = prev.shape[-1]
    block = count * across
    odd_y = lax.axis_index("cy") % 2 == 1
    has_next = lax.axis_index("sweep") < lax.axis_size("sweep") - 1
    wide[...] = prev[...].astype(F32)
    wide_right[...] = right[...].astype(F32)
    wide_follow[...] = jnp.where(has_next, follow[...].astype(F32), 0.0)
    even, odd = side_even[...].astype(F32), side_odd[...].astype(F32)
    total = bands * across
    sides[0:total, 0:count] = jnp.where(odd_y, even, odd)
    sides[total : 2 * total, 0:count] = jnp.where(odd_y, odd, even)
    columns = sides[...].T
    lane = lax.broadcasted_iota(jnp.int32, (count, along), 1)
    fields = []
    for z in range(bands):
        fields.append(lane_blocks(wide, z * block, count, across))
    fields.append(lane_blocks(wide_follow, 0, count, across))

    def join(blocks):
        return jnp.concatenate(blocks, axis=1).astype(BF16)

    for z in range(bands):
        which = pattern[z]
        mine = fields[z]
        behind, ahead = [], []
        for i in range(across):
            at = z * across + i
            behind.append(
                jnp.where(lane == 0, columns[0:count, at : at + 1], pltpu.roll(mine[i], 1, axis=1))
            )
            at = at + total
            ahead.append(
                jnp.where(
                    lane == along - 1, columns[0:count, at : at + 1], pltpu.roll(mine[i], along - 1, axis=1)
                )
            )
        sums = jnp.concatenate(lane_blocks(wide_right, z * block, count, across), axis=1)
        whole = join(mine)
        for face, field in ((1, join(fields[z + 1])), (4, join(behind)), (5, join(ahead))):
            store_halves(work, faces[face, :, which, :])
            sums = sums - apply(work[...], field, count)
        base[z] = sums
        for place in range(2):
            store_halves(across_maps.at[z, place], faces[2 + place, :, which, :])
        edge = (across - 1) * along
        base[z, :, along:] = base[z, :, along:] - apply(across_maps[z, 0], whole[:, :edge], count)
        base[z, :, :edge] = base[z, :, :edge] - apply(across_maps[z, 1], whole[:, along:], count)
        inverse = inverses[:, which, :]
        store_halves(inverse_maps.at[z], inverse)
        step = -apply_halves(inverse_maps[z], halves(faces[0, :, which, :]), count)
        store_halves(step_maps.at[z], step)
    reach[bands - 1] = inverse_maps[bands - 1]
    reach_work[...] = step_maps[bands - 1]
    start = padded_rows(count)
    for z in range(bands - 2, -1, -1):
        parts = (inverse_maps[z, 0:count, :], inverse_maps[z, start : start + count, :])
        store_halves(reach.at[z], apply_halves(reach_work[...], parts, count))
        if z > 0:
            parts = (step_maps[z, 0:count, :], step_maps[z, start : start + count, :])
            store_halves(reach_work, apply_halves(reach_work[...], parts, count))


def edge_kernel(bands, count, across, live, base, reach, across_maps, face_even, face_odd, last, high, low):
    cells = base.shape[-1]
    along = cells // across
    odd_x = lax.axis_index("cx") % 2 == 1
    slot = lax.broadcasted_iota(jnp.int32, (count, cells), 1)
    edge = cells - along
    shortest = live[bands - 1]
    sums = None
    for z in range(bands - 1, -1, -1):
        even, odd = face_even[z].astype(F32), face_odd[z].astype(F32)
        minus = jnp.where(odd_x, even, odd).astype(BF16)
        plus = jnp.where(odd_x, odd, even).astype(BF16)
        rows = base[z]
        rows = jnp.concatenate(
            [
                rows[:, :along] - apply(across_maps[z, 0], minus, count),
                rows[:, along:edge],
                rows[:, edge:] - apply(across_maps[z, 1], plus, count),
            ],
            axis=1,
        )
        parts = halves(rows)
        high[z], low[z] = parts
        shortest = jnp.minimum(shortest, live[z])
        kept = slot < shortest
        parts = halves(jnp.where(kept, rows, 0.0))
        term = apply_halves(reach[z], parts, count)
        sums = term if sums is None else sums + term
    last[...] = sums


def sweep_kernel(bands, count, live, high, low, inverse_maps, step_maps, states, chains):
    cells = high.shape[-1]
    slot = lax.broadcasted_iota(jnp.int32, (count, cells), 1)
    current = None
    start = padded_rows(count)
    for z in range(bands):
        value = apply_halves(inverse_maps[z], (high[z], low[z]), count)
        if z > 0:
            value = value + apply_halves(step_maps[z], halves(current), count)
        current = jnp.where(slot < live[z], value, 0.0)
        states[z] = current
    chains[0] = step_maps[0]
    for z in range(1, bands):
        parts = (chains[z - 1, 0:count, :], chains[z - 1, start : start + count, :])
        store_halves(chains.at[z], apply_halves(step_maps[z], parts, count))


def finish_kernel(bands, count, across, live, states, chains, incoming, out):
    cells = incoming.shape[-1]
    along = cells // across
    slot = lax.broadcasted_iota(jnp.int32, (count, cells), 1)
    parts = halves(jnp.where(lax.axis_index("sweep") > 0, incoming[...], 0.0))
    shortest = live[0]
    for z in range(bands):
        shortest = jnp.minimum(shortest, live[z])
        moved = apply_halves(chains[z], parts, count)
        value = states[z] + jnp.where(slot < shortest, moved, 0.0)
        for i in range(across):
            out[pl.ds(z * count * across + i, count, stride=across), :] = value[:, i * along : (i + 1) * along]


def call(kernel, out, specs, scratch=(), flops=0, moved=0):
    return pl.pallas_call(
        kernel,
        out_shape=out,
        in_specs=specs,
        out_specs=jax.tree.map(lambda _: VMEM, out),
        scratch_shapes=scratch,
        cost_estimate=pl.CostEstimate(flops=flops, bytes_accessed=moved, transcendentals=0),
        compiler_params=pltpu.CompilerParams(vmem_limit_bytes=40 * 2**20),
    )


def swapped(value, axis, first):
    pairs = []
    for left in range(first, lax.axis_size(axis) - 1, 2):
        pairs += [(left, left + 1), (left + 1, left)]
    return lax.ppermute(value, axis, pairs)


def passed_along(value, axis, steps):
    count = lax.axis_size(axis)
    if count == 2:
        return swapped(value, axis, 0)
    first, last = (max(0, -steps), min(count, count - steps))
    return lax.ppermute(value, axis, [(source, source + steps) for source in range(first, last)])


def on_device(right_side, previous, diag_inverse, face_blocks, pattern, live_count):
    bands, count, across, along = right_side.shape
    cells, rows = across * along, bands * count * across
    pads = 2 * padded_rows(count)
    shape = jax.ShapeDtypeStruct
    right = right_side.reshape(rows, along)
    prev = previous.reshape(rows, along)
    faces = face_blocks.transpose(1, 2, 0, 3)
    inverses = diag_inverse.transpose(1, 0, 2)
    live = live_count.reshape(bands)
    face = shape((bands, count, along), BF16)
    side = shape((bands * across, count), BF16)
    side_rows = pltpu.VMEM((bands * across, count), F32)
    face_even, face_odd, side_even, side_odd, first = call(
        functools.partial(pack_kernel, bands, count, across),
        (face, face, side, side, shape((count * across, along), BF16)),
        [VMEM],
        [pltpu.VMEM((rows, along), F32), side_rows, side_rows],
        moved=rows * along * 4,
    )(prev)
    face_even = swapped(face_even, "cx", 0)
    face_odd = swapped(face_odd, "cx", 1)
    side_even = swapped(side_even, "cy", 0)
    side_odd = swapped(side_odd, "cy", 1)
    follow = passed_along(first, "sweep", -1)
    matrix = shape((bands, pads, count), BF16)
    base, reach, across_maps, inverse_maps, step_maps = call(
        functools.partial(local_kernel, bands, count, across),
        (shape((bands, count, cells), F32), matrix, shape((bands, 2, pads, count), BF16), matrix, matrix),
        [SMEM] + [VMEM] * 7,
        [
            pltpu.VMEM((rows, along), F32),
            pltpu.VMEM((rows, along), F32),
            pltpu.VMEM((count * across, along), F32),
            pltpu.VMEM((rounded(2 * bands * across, 128), rounded(count, 128)), F32),
            pltpu.VMEM((pads, count), BF16),
            pltpu.VMEM((pads, count), BF16),
        ],
        flops=bands * 10 * count * count * cells * 2,
        moved=8 * 2**20,
    )(pattern, right, prev, follow, side_even, side_odd, faces, inverses)
    last, high, low = call(
        functools.partial(edge_kernel, bands, count, across),
        (shape((count, cells), F32), shape((bands, count, cells), BF16), shape((bands, count, cells), BF16)),
        [SMEM] + [VMEM] * 5,
        flops=bands * 5 * count * count * cells * 2,
        moved=4 * 2**20,
    )(live, base, reach, across_maps, face_even, face_odd)
    states, chains = call(
        functools.partial(sweep_kernel, bands, count),
        (shape((bands, count, cells), F32), matrix),
        [SMEM] + [VMEM] * 4,
        flops=bands * 6 * count * count * cells * 2,
        moved=4 * 2**20,
    )(live, high, low, inverse_maps, step_maps)
    incoming = passed_along(last, "sweep", 1)
    if lax.axis_size("sweep") > 2:
        start = padded_rows(count)
        end_map = chains[-1, 0:count].astype(F32) + chains[-1, start : start + count].astype(F32)
        slot = jnp.arange(cells, dtype=jnp.int32)
        kept = (slot < jnp.min(live)).astype(F32)

        def relay(_, arriving):
            product = jnp.dot(end_map, arriving, precision=lax.Precision.HIGHEST)
            return passed_along(last + kept[None, :] * product, "sweep", 1)

        incoming = lax.fori_loop(0, lax.axis_size("sweep") - 2, relay, incoming)
    out = call(
        functools.partial(finish_kernel, bands, count, across),
        shape((rows, along), F32),
        [SMEM] + [VMEM] * 3,
        flops=bands * 3 * count * count * cells * 2,
        moved=3 * 2**20,
    )(live, states, chains, incoming)
    return out.reshape(bands, count, across, along)


def solution(mesh):
    return jax.shard_map(
        on_device,
        mesh=mesh,
        in_specs=(
            P("sweep", None, "cx", "cy"),
            P("sweep", None, "cx", "cy"),
            P(),
            P(),
            P("sweep"),
            P("sweep", "cx", "cy"),
        ),
        out_specs=P("sweep", None, "cx", "cy"),
        check_vma=False,
    )
```

time: 95.3 us -> 41.3 us (0.43)
  matrix products: 36.4 us -> 0 us
  local copies, waits for them, and re-layouts: 33.6 us -> 5.75 us
  Pallas kernels: 0 us -> 22.2 us
  other arithmetic: 5.16 us -> 0 us
  starting transfers between devices: 16.5 us -> 11.5 us
  waiting for transfers between devices: 2.17 us -> 1.03 us
    dot_general x19 -> x0, matrix products: 36.4 us -> none  [the longest x6 9.56 us: contract(): return jnp.einsum('buv,bvc->buc', blocks, fields, precision=full_precision)]
    pallas_call x0 -> x5, Pallas kernels: none -> 22.2 us  [the longest x1 15.5 us: on_device(): call(functools.partial(local_kernel, bands, count, across), (shape((bands...]
    reshape x4 -> x0, local copies, waits for them, and re-layouts: 8.95 us -> none  [the longest x2 4.14 us: on_device(): neighbours[face_index].astype(jnp.float32)]
    ppermute x4 -> x0, local copies, waits for them, and re-layouts: 6 us -> none  [the longest x2 3.02 us: padded(): lax.ppermute(tail, axis, [(i, (i + 1) % count) for i in range(ends)])]
    concatenate x3 -> x0, other arithmetic: 5.04 us -> none  [padded(): jnp.concatenate([lax.ppermute(tail, axis, [(i, (i + 1) % count) for i in...]
    ppermute x6, starting transfers between devices: 16.5 us -> 11.5 us  [swapped(): return lax.ppermute(value, axis, pairs)]
    while x8 -> x0, local copies, waits for them, and re-layouts: 3.87 us -> none
    concatenate x2 -> x0, local copies, waits for them, and re-layouts: 3.78 us -> none  [on_device(): downstream = jnp.concatenate([previous[1:], following[None]], axis=0)]
  transfers between devices with their start and end apart: 6 -> 6, of which waited for: 1 -> 1; matrix products, arithmetic and copies ran while one was open for 39% -> 0% of each run, Pallas kernels for 0% -> 43%
where the time goes in v1:
time: 41.3 us; the launch traced here: 40.6 us
  Pallas kernels  22.2 us (54%)
  starting transfers between devices  11.5 us (28%)
  local copies, waits for them, and re-layouts  5.75 us (14%)
  waiting for transfers between devices  1.03 us (2%)
    pallas_call x1, Pallas kernels, on_device(): call(functools.partial(local_kernel, bands, count, across), (shape((bands...  15.5 us
    ppermute x6, starting transfers between devices, swapped(): return lax.ppermute(value, axis, pairs)  11.5 us
    unnamed x12, local copies, waits for them, and re-layouts  5.75 us
    pallas_call x1, Pallas kernels, on_device(): call(functools.partial(finish_kernel, bands, count, across), shape((rows,...  2.18 us
    pallas_call x1, Pallas kernels, on_device(): call(functools.partial(sweep_kernel, bands, count), (shape((bands, count,...  2.11 us
    pallas_call x1, Pallas kernels, on_device(): call(functools.partial(edge_kernel, bands, count, across), (shape((count,...  2.05 us
    ppermute x6, waiting for transfers between devices, swapped(): return lax.ppermute(value, axis, pairs)  1.03 us
  transfers between devices with their start and end apart: 6, of which 1 were waited for; matrix products, arithmetic and copies ran while one was open for 0% of the time, Pallas kernels for 43%

profile of v1, /device:TPU:11, one launch (start us, length us, event | category | flops | bytes accessed | tf_op | source)
XLA Modules:
  0.0 40.6 jit_solution(17703507405261580971)
XLA Ops:
  0.0 1.0 %copy-done.1 = bf16[4,135,4,128]{3,2,1,0:T(4,128)(2,1)S(1)} copy-done((bf16[4,135,4,128]{3,2,1,0:T(4,128)(2,1)S(1)}, bf16[4,135,4,128]{3,2,1,0:T(4,128)(2,1)}, u32[]{:S(2)}) %copy-start.1) | copy-done | bytes 552984
  1.1 0.4 %shard_map.64 = (bf16[4,135,128]{2,1,0:T(8,128)(2,1)S(1)}, bf16[4,135,128]{2,1,0:T(8,128)(2,1)S(1)}, bf16[16,135]{1,0:T(8,128)(2,1)S(1)}, bf16[16,135]{1,0:T(8,128)(2,1)S(1)}, bf16[540,128]{1,0:T(8,128)(2,1)S(1)}) custom-call(bf16[2160,128]{1,0:T(8,128)(2,1)S(1)} %bitcast.7), custom_call_target="tpu_custom_call" | custom-call | bytes 1105920 | tf_op jit(solution)/shard_map/pallas_call | solution.py:252
  1.5 0.7 %collective-permute-start = (bf16[540,128]{1,0:T(8,128)(2,1)S(1)}, bf16[540,128]{1,0:T(8,128)(2,1)S(1)}, u32[]{:S(2)}, u32[]{:S(2)}) collective-permute-start(bf16[540,128]{1,0:T(8,128)(2,1)S(1)} %get-tuple-element.20), channel_id=1, source_target_pairs={{0,16},{16,0},{1,17},{17,1},{2,18},{18,2},{3,19},{19,3},{4,20},{20... | collective-permute-start | bytes 414728 | tf_op jit(solution)/shard_map/ppermute | solution.py:228
  2.2 0.3 collective-permute-start.3
  2.5 4.1 %collective-permute-start.4 = (bf16[4,135,128]{2,1,0:T(8,128)(2,1)S(1)}, bf16[4,135,128]{2,1,0:T(8,128)(2,1)S(1)}, u32[]{:S(2)}, u32[]{:S(2)}) collective-permute-start(bf16[4,135,128]{2,1,0:T(8,128)(2,1)S(1)} %get-tuple-element.27), channel_id=1, source_target_pairs={{4,8},{8,4},{5,9},{9,5},{6,10},{10,6},{7,11},{11,7},{20,24},{24,20... | collective-permute-start | bytes 414728 | tf_op jit(solution)/shard_map/ppermute | solution.py:228
  6.6 0.2 collective-permute-start.1
  6.8 4.3 %collective-permute-start.2 = (bf16[16,135]{1,0:T(8,128)(2,1)S(1)}, bf16[16,135]{1,0:T(8,128)(2,1)S(1)}, u32[]{:S(2)}, u32[]{:S(2)}) collective-permute-start(bf16[16,135]{1,0:T(8,128)(2,1)S(1)} %get-tuple-element.22), channel_id=1, source_target_pairs={{1,2},{2,1},{5,6},{6,5},{9,10},{10,9},{13,14},{14,13},{17,18},{18,... | collective-permute-start | bytes 12968 | tf_op jit(solution)/shard_map/ppermute | solution.py:228
  11.1 0.0 collective-permute-done.1.side_even
  11.1 1.0 %collective-permute-done.2.side_odd = bf16[16,135]{1,0:T(8,128)(2,1)S(1)} collective-permute-done((bf16[16,135]{1,0:T(8,128)(2,1)S(1)}, bf16[16,135]{1,0:T(8,128)(2,1)S(1)}, u32[]{:S(2)}, u32[]{:S(2)}) %collective-permute-start.2) | collective-permute-done | bytes 4352 | tf_op jit(solution)/shard_map/ppermute | solution.py:228
  12.2 0.0 collective-permute-done.follow
  12.2 0.0 copy-start
  12.2 1.9 %copy-done = f32[4,6,135,135]{3,0,2,1:T(4,128)S(1)} copy-done((f32[4,6,135,135]{3,0,2,1:T(4,128)S(1)}, f32[4,6,135,135]{3,0,2,1:T(4,128)}, u32[]{:S(2)}) %copy-start) | copy-done | bytes 1749624
  14.1 1.0 %copy-done.2 = bf16[4,135,4,128]{3,2,1,0:T(4,128)(2,1)S(1)} copy-done((bf16[4,135,4,128]{3,2,1,0:T(4,128)(2,1)S(1)}, bf16[4,135,4,128]{3,2,1,0:T(4,128)(2,1)}, u32[]{:S(2)}) %copy-start.2) | copy-done | bytes 552984
  15.1 1.0 %copy-done.3 = f32[4,135,135]{2,0,1:T(4,128)S(1)} copy-done((f32[4,135,135]{2,0,1:T(4,128)S(1)}, f32[4,135,135]{2,0,1:T(4,128)}, u32[]{:S(2)}) %copy-start.3) | copy-done | bytes 291624
  16.2 0.7 %copy-done.5 = s32[4]{0:T(128)S(1)} copy-done((s32[4]{0:T(128)S(1)}, s32[4]{0:T(128)}, u32[]{:S(2)}) %copy-start.5) | copy-done | bytes 40
  16.9 15.5 %shard_map.65 = (f32[4,135,512]{2,1,0:T(8,128)S(1)}, bf16[4,288,135]{2,1,0:T(8,128)(2,1)S(1)}, bf16[4,2,288,135]{3,2,1,0:T(8,128)(2,1)S(1)}, bf16[4,288,135]{2,1,0:T(8,128)(2,1)S(1)}, bf16[4,288,135]{2,1,0:T(8,128)(2,1)S(1)}) custom-call(s32[4]{0:T(128)S(1)} %copy-done.5, bf16[2160,128]{1,0:T(8,128)(2,1)S(1)} %bitcast.9, bf16[2160,128]{1,0:T(8,128)(2,1)S(1)} %bitcast.8, ...), custom_call_target="tpu_custom_call" | custom-call | flops 746496000 | bytes 8388608 | tf_op jit(solution)/shard_map/pallas_call | solution.py:265
  32.3 0.0 collective-permute-done.3.face_even
  32.3 0.0 collective-permute-done.4.face_odd
  32.3 0.0 copy-done.4
  32.4 2.0 %shard_map.66 = (f32[135,512]{1,0:T(8,128)S(1)}, bf16[4,135,512]{2,1,0:T(8,128)(2,1)S(1)}, bf16[4,135,512]{2,1,0:T(8,128)(2,1)S(1)}) custom-call(s32[4]{0:T(128)S(1)} %bitcast.11, f32[4,135,512]{2,1,0:T(8,128)S(1)} %get-tuple-element.23.base, bf16[4,288,135]{2,1,0:T(8,128)(2,1)S(1)} %get-tuple-element.24.reach, ...), custom_call_target="tpu_custom_call" | custom-call | flops 373248000 | bytes 4194304 | tf_op jit(solution)/shard_map/pallas_call | solution.py:280
  34.4 1.8 %collective-permute-start.5 = (f32[135,512]{1,0:T(8,128)S(1)}, f32[135,512]{1,0:T(8,128)S(1)}, u32[]{:S(2)}, u32[]{:S(2)}) collective-permute-start(f32[135,512]{1,0:T(8,128)S(1)} %get-tuple-element.34), channel_id=1, source_target_pairs={{0,16},{16,0},{1,17},{17,1},{2,18},{18,2},{3,19},{19,3},{4,20},{20... | collective-permute-start | bytes 829448 | tf_op jit(solution)/shard_map/ppermute | solution.py:228
  36.3 2.1 %shard_map.67 = (f32[4,135,512]{2,1,0:T(8,128)S(1)}, bf16[4,288,135]{2,1,0:T(8,128)(2,1)S(1)}) custom-call(s32[4]{0:T(128)S(1)} %bitcast.12, bf16[4,135,512]{2,1,0:T(8,128)(2,1)S(1)} %get-tuple-element.28.high, bf16[4,135,512]{2,1,0:T(8,128)(2,1)S(1)} %get-tuple-element.29.low, bf16[4,288,135]{2,1,0:T(8,128)(2,1)S(1)} %get-tuple-element.30.inverse_maps, ...), custom_call_target="tpu_custom_call" | custom-call | flops 447897600 | bytes 4194304 | tf_op jit(solution)/shard_map/pallas_call | solution.py:287
  38.4 0.0 collective-permute-done.5.incoming
  38.4 2.2 %shard_map.68 = f32[2160,128]{1,0:T(8,128)} custom-call(s32[4]{0:T(128)S(1)} %bitcast.13, f32[4,135,512]{2,1,0:T(8,128)S(1)} %get-tuple-element.32.states, bf16[4,288,135]{2,1,0:T(8,128)(2,1)S(1)} %get-tuple-element.33.chains, f32[135,512]{1,0:T(8,128)S(1)} %collective-permute-done.5.incoming), custom_call_target="tpu_custom_call" | custom-call | flops 223948800 | bytes 3145728 | tf_op jit(solution)/shard_map/pallas_call | solution.py:306
  (5 shorter events, 0.0 us)
Async XLA Ops:
  0.0 1.1 %copy-start.1 = (bf16[4,135,4,128]{3,2,1,0:T(4,128)(2,1)S(1)}, bf16[4,135,4,128]{3,2,1,0:T(4,128)(2,1)}, u32[]{:S(2)}) copy-start(bf16[4,135,4,128]{3,2,1,0:T(4,128)(2,1)} %param.7) | copy-start | bytes 1658884
  1.5 10.7 %collective-permute-start = (bf16[540,128]{1,0:T(8,128)(2,1)S(1)}, bf16[540,128]{1,0:T(8,128)(2,1)S(1)}, u32[]{:S(2)}, u32[]{:S(2)}) collective-permute-start(bf16[540,128]{1,0:T(8,128)(2,1)S(1)} %get-tuple-element.20), channel_id=1, source_target_pairs={{0,16},{16,0},{1,17},{17,1},{2,18},{18,2},{3,19},{19,3},{4,20},{20... | collective-permute-start | bytes 414728 | tf_op jit(solution)/shard_map/ppermute | solution.py:228
  2.2 30.1 %collective-permute-start.3 = (bf16[4,135,128]{2,1,0:T(8,128)(2,1)S(1)}, bf16[4,135,128]{2,1,0:T(8,128)(2,1)S(1)}, u32[]{:S(2)}, u32[]{:S(2)}) collective-permute-start(bf16[4,135,128]{2,1,0:T(8,128)(2,1)S(1)} %get-tuple-element.26), channel_id=1, source_target_pairs={{0,4},{4,0},{8,12},{12,8},{1,5},{5,1},{9,13},{13,9},{2,6},{6,2},{1... | collective-permute-start | bytes 414728 | tf_op jit(solution)/shard_map/ppermute | solution.py:228
  2.5 29.8 %collective-permute-start.4 = (bf16[4,135,128]{2,1,0:T(8,128)(2,1)S(1)}, bf16[4,135,128]{2,1,0:T(8,128)(2,1)S(1)}, u32[]{:S(2)}, u32[]{:S(2)}) collective-permute-start(bf16[4,135,128]{2,1,0:T(8,128)(2,1)S(1)} %get-tuple-element.27), channel_id=1, source_target_pairs={{4,8},{8,4},{5,9},{9,5},{6,10},{10,6},{7,11},{11,7},{20,24},{24,20... | collective-permute-start | bytes 414728 | tf_op jit(solution)/shard_map/ppermute | solution.py:228
  6.6 4.6 %collective-permute-start.1 = (bf16[16,135]{1,0:T(8,128)(2,1)S(1)}, bf16[16,135]{1,0:T(8,128)(2,1)S(1)}, u32[]{:S(2)}, u32[]{:S(2)}) collective-permute-start(bf16[16,135]{1,0:T(8,128)(2,1)S(1)} %get-tuple-element.21), channel_id=1, source_target_pairs={{0,1},{1,0},{2,3},{3,2},{4,5},{5,4},{6,7},{7,6},{8,9},{9,8},{10,11... | collective-permute-start | bytes 12968 | tf_op jit(solution)/shard_map/ppermute | solution.py:228
  6.8 5.4 %collective-permute-start.2 = (bf16[16,135]{1,0:T(8,128)(2,1)S(1)}, bf16[16,135]{1,0:T(8,128)(2,1)S(1)}, u32[]{:S(2)}, u32[]{:S(2)}) collective-permute-start(bf16[16,135]{1,0:T(8,128)(2,1)S(1)} %get-tuple-element.22), channel_id=1, source_target_pairs={{1,2},{2,1},{5,6},{6,5},{9,10},{10,9},{13,14},{14,13},{17,18},{18,... | collective-permute-start | bytes 12968 | tf_op jit(solution)/shard_map/ppermute | solution.py:228
  12.2 1.9 %copy-start = (f32[4,6,135,135]{3,0,2,1:T(4,128)S(1)}, f32[4,6,135,135]{3,0,2,1:T(4,128)}, u32[]{:S(2)}) copy-start(f32[4,6,135,135]{3,0,2,1:T(4,128)} %param.9) | copy-start | bytes 5248804
  14.1 1.1 %copy-start.2 = (bf16[4,135,4,128]{3,2,1,0:T(4,128)(2,1)S(1)}, bf16[4,135,4,128]{3,2,1,0:T(4,128)(2,1)}, u32[]{:S(2)}) copy-start(bf16[4,135,4,128]{3,2,1,0:T(4,128)(2,1)} %param.6) | copy-start | bytes 1658884
  15.1 1.1 %copy-start.3 = (f32[4,135,135]{2,0,1:T(4,128)S(1)}, f32[4,135,135]{2,0,1:T(4,128)}, u32[]{:S(2)}) copy-start(f32[4,135,135]{2,0,1:T(4,128)} %param.8) | copy-start | bytes 874804
  16.2 0.7 %copy-start.5 = (s32[4]{0:T(128)S(1)}, s32[4]{0:T(128)}, u32[]{:S(2)}) copy-start(s32[4]{0:T(128)} %pattern.1) | copy-start | bytes 52
  16.9 15.5 %copy-start.4 = (s32[4,1,1]{0,2,1:T(1,128)S(1)}, s32[4,1,1]{0,2,1:T(1,128)}, u32[]{:S(2)}) copy-start(s32[4,1,1]{0,2,1:T(1,128)} %param.11) | copy-start | bytes 52
  34.4 4.0 %collective-permute-start.5 = (f32[135,512]{1,0:T(8,128)S(1)}, f32[135,512]{1,0:T(8,128)S(1)}, u32[]{:S(2)}, u32[]{:S(2)}) collective-permute-start(f32[135,512]{1,0:T(8,128)S(1)} %get-tuple-element.34), channel_id=1, source_target_pairs={{0,16},{16,0},{1,17},{17,1},{2,18},{18,2},{3,19},{19,3},{4,20},{20... | collective-permute-start | bytes 829448 | tf_op jit(solution)/shard_map/ppermute | solution.py:228

commit v2 on v1

v2 whole, which is shorter than its diff:
```python
import functools

import jax
import jax.numpy as jnp
from jax import lax
from jax.experimental import pallas as pl
from jax.experimental.pallas import tpu as pltpu
from jax.sharding import PartitionSpec as P

F32, BF16 = jnp.float32, jnp.bfloat16
VMEM = pl.BlockSpec(memory_space=pltpu.VMEM)
HBM = pl.BlockSpec(memory_space=pltpu.HBM)


def rounded(count, unit):
    return (count + unit - 1) // unit * unit


def padded_rows(count):
    return rounded(count, 16)


def product(left, right):
    return jnp.dot(left, right, preferred_element_type=F32)


def halves(value):
    high = value.astype(BF16)
    return high, (value - high.astype(F32)).astype(BF16)


def store_halves(ref, value):
    count = value.shape[0]
    start = padded_rows(count)
    high, low = halves(value)
    ref[0:count, :] = high
    ref[start : start + count, :] = low


def apply(stacked, right, count):
    both = product(stacked, right)
    start = padded_rows(count)
    return both[0:count] + both[start : start + count]


def apply_halves(stacked, right, count):
    high, low = right
    rest = product(stacked[0 : padded_rows(count)], low)
    return apply(stacked, high, count) + rest[0:count]


def lane_blocks(ref, start, count, across):
    return [ref[pl.ds(start + i, count, stride=across), :] for i in range(across)]


def chunks(rows):
    return 2 if rows % 32 == 0 else 1


def start_copies(source, target, sems, first=0):
    rows = source.shape[0]
    size = rows // chunks(rows)
    copies = []
    for at in range(chunks(rows)):
        window = pl.ds(at * size, size)
        copies.append(pltpu.make_async_copy(source.at[window], target.at[window], sems.at[first + at]))
        copies[-1].start()
    return copies


def pack_kernel(
    bands, count, across, prev, kept, face_even, face_odd, side_even, side_odd, first, wide, rows_even, rows_odd, sems
):
    along = prev.shape[-1]
    rows = prev.shape[0]
    copies = start_copies(prev, kept, sems)
    odd_x = lax.axis_index("cx") % 2 == 1
    odd_y = lax.axis_index("cy") % 2 == 1
    row = lax.broadcasted_iota(jnp.int32, (8, along), 0)
    lane = lax.broadcasted_iota(jnp.int32, (8, along), 1)
    last = along - 1
    even_lane, odd_lane = jnp.where(odd_y, 0, last), jnp.where(odd_y, last, 0)
    chosen = jnp.where(row == 0, even_lane, odd_lane)
    pick = jnp.where(lane == chosen, 1.0, 0.0).astype(BF16)
    size = rows // len(copies)
    done = 0
    for z in range(bands):
        while done * size < (z + 1) * count * across:
            copies[done].wait()
            window = pl.ds(done * size, size)
            wide[window, :] = kept[window, :].astype(F32)
            done += 1
        blocks = lane_blocks(wide, z * count * across, count, across)
        low, high = blocks[0], blocks[-1]
        face_even[z] = jnp.where(odd_x, low, high).astype(BF16)
        face_odd[z] = jnp.where(odd_x, high, low).astype(BF16)
        for i in range(across):
            found = lax.dot_general(
                pick, blocks[i].astype(BF16), (((1,), (1,)), ((), ())), preferred_element_type=F32
            )
            at = z * across + i
            rows_even[at : at + 1, :] = found[0:1]
            rows_odd[at : at + 1, :] = found[1:2]
    first[...] = kept[0 : count * across, :]
    side_even[...] = rows_even[...].astype(BF16)
    side_odd[...] = rows_odd[...].astype(BF16)


def parts(ref, count):
    start = padded_rows(count)
    return ref[0:count, :], ref[start : start + count, :]


def combine(out, left, right, count):
    store_halves(out, apply_halves(left[...], parts(right, count), count))


def matrix_kernel(
    bands, count, pattern_far, live_far, faces, inverses, right,
    right_kept, maps, inverse_maps, step_maps, reach, edge_reach, chains, masks,
    faces_here, inverses_here, pool, pattern, live, sems,
):
    cells = masks.shape[-1]
    copies = [pltpu.make_async_copy(inverses, inverses_here, sems.at[0])]
    order = (0, 2, 3, 1, 4, 5)
    for face in order:
        copies.append(pltpu.make_async_copy(faces.at[face], faces_here.at[face], sems.at[1 + face]))
    copies.append(pltpu.make_async_copy(right, right_kept, sems.at[7]))
    small = [
        pltpu.make_async_copy(pattern_far, pattern, sems.at[8]),
        pltpu.make_async_copy(live_far, live, sems.at[9]),
    ]
    for copy in small + copies:
        copy.start()
    for copy in small:
        copy.wait()
    slot = lax.broadcasted_iota(jnp.int32, (1, cells), 1)
    counts = [live[z] for z in range(bands)]
    before, after = counts[0], counts[bands - 1]
    for z in range(bands):
        before = jnp.minimum(before, counts[z])
        after = jnp.minimum(after, counts[bands - 1 - z])
        for row, limit in ((z, counts[z]), (2 * bands - 1 - z, after), (2 * bands + z, before)):
            masks[row : row + 1, :] = jnp.where(slot < limit, 1.0, 0.0)
    which = [pattern[z] for z in range(bands)]
    copies[0].wait()
    for z in range(bands):
        store_halves(inverse_maps.at[z], inverses_here[:, which[z], :])
    copies[1].wait()
    for z in range(bands):
        upstream = halves(faces_here[0, :, which[z], :])
        store_halves(step_maps.at[z], -apply_halves(inverse_maps[z], upstream, count))
    spare = [0]

    def fresh():
        spare[0] += 1
        return pool.at[spare[0] - 1]

    def solve(low, high, top):
        if high - low == 1:
            return {low: inverse_maps.at[low]}, step_maps.at[low]
        middle = (low + high) // 2
        near, near_step = solve(low, middle, False)
        found, far_step = solve(middle, high, False)
        for z, ref in near.items():
            target = reach.at[z] if top else fresh()
            combine(target, far_step, ref, count)
            found[z] = target
        step = None
        if not top:
            step = fresh()
            combine(step, far_step, near_step, count)
        if top:
            for z in range(middle, high):
                reach[z] = found[z][...]
        return found, step

    solve(0, bands, True)
    for place, face in enumerate(order[1:]):
        copies[2 + place].wait()
        for z in range(bands):
            ref = maps.at[z, face - 1]
            store_halves(ref, faces_here[face, :, which[z], :])
            if place < 2:
                combine(edge_reach.at[z, place], reach.at[z], ref, count)
    chains[0] = step_maps[0]
    for z in range(1, bands):
        combine(chains.at[z], step_maps.at[z], chains.at[z - 1], count)
    copies[-1].wait()


def local_kernel(
    bands, count, across, right, prev, follow, side_even, side_odd, maps, reach, masks,
    base, partial, wide, wide_right, wide_follow, sides,
):
    along = prev.shape[-1]
    block = count * across
    odd_y = lax.axis_index("cy") % 2 == 1
    has_next = lax.axis_index("sweep") < lax.axis_size("sweep") - 1
    wide[...] = prev[...].astype(F32)
    wide_right[...] = right[...].astype(F32)
    wide_follow[...] = jnp.where(has_next, follow[...].astype(F32), 0.0)
    even, odd = side_even[...].astype(F32), side_odd[...].astype(F32)
    total = bands * across
    sides[0:total, 0:count] = jnp.where(odd_y, even, odd)
    sides[total : 2 * total, 0:count] = jnp.where(odd_y, odd, even)
    columns = sides[...].T
    lane = lax.broadcasted_iota(jnp.int32, (count, along), 1)
    fields = []
    for z in range(bands):
        fields.append(lane_blocks(wide, z * block, count, across))
    fields.append(lane_blocks(wide_follow, 0, count, across))

    def join(blocks):
        return jnp.concatenate(blocks, axis=1).astype(BF16)

    edge = (across - 1) * along
    sums = None
    for z in range(bands):
        mine = fields[z]
        behind, ahead = [], []
        for i in range(across):
            at = z * across + i
            column = columns[0:count, at : at + 1]
            behind.append(jnp.where(lane == 0, column, pltpu.roll(mine[i], 1, axis=1)))
            column = columns[0:count, at + total : at + total + 1]
            ahead.append(jnp.where(lane == along - 1, column, pltpu.roll(mine[i], along - 1, axis=1)))
        whole = join(mine)
        full = apply(maps[z, 0], join(fields[z + 1]), count)
        full = full + apply(maps[z, 3], join(behind), count)
        full = full + apply(maps[z, 4], join(ahead), count)
        minus = apply(maps[z, 1], whole[:, :edge], count)
        plus = apply(maps[z, 2], whole[:, along:], count)
        own = lane_blocks(wide_right, z * block, count, across)
        rows = []
        for i in range(across):
            value = own[i] - full[:, i * along : (i + 1) * along]
            if i > 0:
                value = value - minus[:, (i - 1) * along : i * along]
            if i < across - 1:
                value = value - plus[:, i * along : (i + 1) * along]
            rows.append(value)
        rows = jnp.concatenate(rows, axis=1)
        base[z] = rows
        term = apply_halves(reach[z], halves(rows * masks[bands + z : bands + z + 1, :]), count)
        sums = term if sums is None else sums + term
    partial[...] = sums


def edges_of(face_even, face_odd, z):
    odd_x = lax.axis_index("cx") % 2 == 1
    even, odd = face_even[z].astype(F32), face_odd[z].astype(F32)
    return jnp.where(odd_x, even, odd), jnp.where(odd_x, odd, even)


def edge_kernel(bands, count, across, partial, edge_reach, masks, face_even, face_odd, last):
    cells = partial.shape[-1]
    along = cells // across
    edge = cells - along
    first, final = partial[:, :along], partial[:, edge:]
    for z in range(bands):
        minus, plus = edges_of(face_even, face_odd, z)
        mask = masks[bands + z : bands + z + 1, :]
        first = first - apply(edge_reach[z, 0], (minus * mask[:, :along]).astype(BF16), count)
        final = final - apply(edge_reach[z, 1], (plus * mask[:, edge:]).astype(BF16), count)
    last[:, :along] = first
    last[:, along:edge] = partial[:, along:edge]
    last[:, edge:] = final


def sweep_kernel(bands, count, across, base, masks, maps, inverse_maps, step_maps, face_even, face_odd, states):
    cells = base.shape[-1]
    along = cells // across
    edge = cells - along
    shares = []
    for z in range(bands):
        minus, plus = edges_of(face_even, face_odd, z)
        rows = base[z]
        rows = jnp.concatenate(
            [
                rows[:, :along] - apply(maps[z, 1], minus.astype(BF16), count),
                rows[:, along:edge],
                rows[:, edge:] - apply(maps[z, 2], plus.astype(BF16), count),
            ],
            axis=1,
        )
        shares.append(apply_halves(inverse_maps[z], halves(rows), count))
    current = None
    for z in range(bands):
        value = shares[z]
        if z > 0:
            value = value + apply_halves(step_maps[z], halves(current), count)
        current = value * masks[z : z + 1, :]
        states[z] = current


def finish_kernel(bands, count, across, masks, states, chains, incoming, out, staged, sems):
    cells = incoming.shape[-1]
    along = cells // across
    rows = staged.shape[0]
    right = halves(jnp.where(lax.axis_index("sweep") > 0, incoming[...], 0.0))
    size = rows // chunks(rows)
    copies = []
    for z in range(bands):
        moved = apply_halves(chains[z], right, count)
        value = states[z] + moved * masks[2 * bands + z : 2 * bands + z + 1, :]
        for i in range(across):
            staged[pl.ds(z * count * across + i, count, stride=across), :] = value[:, i * along : (i + 1) * along]
        while (len(copies) + 1) * size <= (z + 1) * count * across:
            at = len(copies)
            window = pl.ds(at * size, size)
            copies.append(pltpu.make_async_copy(staged.at[window], out.at[window], sems.at[at]))
            copies[-1].start()
    for copy in copies:
        copy.wait()


def call(kernel, out, specs, scratch=(), flops=0, moved=0, out_specs=None):
    return pl.pallas_call(
        kernel,
        out_shape=out,
        in_specs=specs,
        out_specs=out_specs or jax.tree.map(lambda _: VMEM, out),
        scratch_shapes=scratch,
        cost_estimate=pl.CostEstimate(flops=flops, bytes_accessed=moved, transcendentals=0),
        compiler_params=pltpu.CompilerParams(vmem_limit_bytes=32 * 2**20),
    )


def in_hbm(value):
    return pltpu.with_memory_space_constraint(value, pltpu.HBM)


def swapped(value, axis, first):
    pairs = []
    for left in range(first, lax.axis_size(axis) - 1, 2):
        pairs += [(left, left + 1), (left + 1, left)]
    return lax.ppermute(value, axis, pairs)


def passed_along(value, axis, steps):
    count = lax.axis_size(axis)
    if count == 2:
        return swapped(value, axis, 0)
    first, last = (max(0, -steps), min(count, count - steps))
    return lax.ppermute(value, axis, [(source, source + steps) for source in range(first, last)])


def on_device(right_side, previous, diag_inverse, face_blocks, pattern, live_count):
    bands, count, across, along = right_side.shape
    cells, rows = across * along, bands * count * across
    pads = 2 * padded_rows(count)
    shape = jax.ShapeDtypeStruct
    right = in_hbm(right_side.reshape(rows, along))
    prev = in_hbm(previous.reshape(rows, along))
    faces = in_hbm(face_blocks.transpose(1, 2, 0, 3))
    inverses = in_hbm(diag_inverse.transpose(1, 0, 2))
    live = in_hbm(live_count.reshape(bands))
    pattern = in_hbm(pattern)
    face = shape((bands, count, along), BF16)
    side = shape((bands * across, count), BF16)
    field = shape((rows, along), BF16)
    side_rows = pltpu.VMEM((bands * across, count), F32)
    wide = pltpu.VMEM((rows, along), F32)
    kept, face_even, face_odd, side_even, side_odd, first = call(
        functools.partial(pack_kernel, bands, count, across),
        (field, face, face, side, side, shape((count * across, along), BF16)),
        [HBM],
        [wide, side_rows, side_rows, pltpu.SemaphoreType.DMA((2,))],
        moved=rows * along * 4,
    )(prev)
    face_even = swapped(face_even, "cx", 0)
    face_odd = swapped(face_odd, "cx", 1)
    side_even = swapped(side_even, "cy", 0)
    side_odd = swapped(side_odd, "cy", 1)
    follow = passed_along(first, "sweep", -1)
    matrix = shape((bands, pads, count), BF16)
    step_flops = count * count * cells * 2
    right_kept, maps, inverse_maps, step_maps, reach, edge_reach, chains, masks = call(
        functools.partial(matrix_kernel, bands, count),
        (
            field,
            shape((bands, 5, pads, count), BF16),
            matrix,
            matrix,
            matrix,
            shape((bands, 2, pads, count), BF16),
            matrix,
            shape((3 * bands, cells), F32),
        ),
        [HBM] * 5,
        [
            pltpu.VMEM(faces.shape, F32),
            pltpu.VMEM(inverses.shape, F32),
            pltpu.VMEM((4 * bands, pads, count), BF16),
            pltpu.SMEM((bands,), jnp.int32),
            pltpu.SMEM((bands,), jnp.int32),
            pltpu.SemaphoreType.DMA((10,)),
        ],
        flops=bands * 5 * step_flops,
        moved=4 * 2**20,
    )(pattern, live, faces, inverses, right)
    base, partial = call(
        functools.partial(local_kernel, bands, count, across),
        (shape((bands, count, cells), F32), shape((count, cells), F32)),
        [VMEM] * 8,
        [
            wide,
            wide,
            pltpu.VMEM((count * across, along), F32),
            pltpu.VMEM((rounded(2 * bands * across, 128), rounded(count, 128)), F32),
        ],
        flops=bands * 13 * step_flops,
        moved=2**20,
    )(right_kept, kept, follow, side_even, side_odd, maps, reach, masks)
    last = call(
        functools.partial(edge_kernel, bands, count, across),
        shape((count, cells), F32),
        [VMEM] * 5,
        flops=bands * step_flops,
        moved=2**20,
    )(partial, edge_reach, masks, face_even, face_odd)
    states = call(
        functools.partial(sweep_kernel, bands, count, across),
        shape((bands, count, cells), F32),
        [VMEM] * 7,
        flops=bands * 7 * step_flops,
        moved=2**20,
    )(base, masks, maps, inverse_maps, step_maps, face_even, face_odd)
    incoming = passed_along(last, "sweep", 1)
    if lax.axis_size("sweep") > 2:
        start = padded_rows(count)
        end_map = chains[-1, 0:count].astype(F32) + chains[-1, start : start + count].astype(F32)
        slot = jnp.arange(cells, dtype=jnp.int32)
        kept = (slot < jnp.min(live_count)).astype(F32)

        def relay(_, arriving):
            product = jnp.dot(end_map, arriving, precision=lax.Precision.HIGHEST)
            return passed_along(last + kept[None, :] * product, "sweep", 1)

        incoming = lax.fori_loop(0, lax.axis_size("sweep") - 2, relay, incoming)
    out = call(
        functools.partial(finish_kernel, bands, count, across),
        shape((rows, along), F32),
        [VMEM] * 4,
        [wide, pltpu.SemaphoreType.DMA((2,))],
        flops=bands * 3 * step_flops,
        moved=2**20,
        out_specs=HBM,
    )(masks, states, chains, incoming)
    return out.reshape(bands, count, across, along)


def solution(mesh):
    return jax.shard_map(
        on_device,
        mesh=mesh,
        in_specs=(
            P("sweep", None, "cx", "cy"),
            P("sweep", None, "cx", "cy"),
            P(),
            P(),
            P("sweep"),
            P("sweep", "cx", "cy"),
        ),
        out_specs=P("sweep", None, "cx", "cy"),
        check_vma=False,
    )
```

time: 41.3 us -> 35.9 us (0.87); the launches traced: 40.6 us -> 35.8 us
  local copies, waits for them, and re-layouts: 5.75 us -> 0 us
  Pallas kernels: 22.2 us -> 24.6 us
  waiting for transfers between devices: 1.03 us -> 0.02 us
  starting transfers between devices: 11.5 us -> 10.9 us
    pallas_call x3 -> x4, Pallas kernels: 4.6 us -> 20 us  [the longest x1 15.9 us: on_device(): call(functools.partial(matrix_kernel, bands, count), (field, shape((bands...]
    pallas_call x1, Pallas kernels: 15.5 us -> 2.97 us  [on_device(): call(functools.partial(local_kernel, bands, count, across), (shape((bands...]
    unnamed x12 -> x0, local copies, waits for them, and re-layouts: 5.75 us -> none
    ppermute x6, waiting for transfers between devices: 1.03 us -> 0.02 us  [swapped(): return lax.ppermute(value, axis, pairs)]
    ppermute x6, starting transfers between devices: 11.5 us -> 10.9 us  [swapped(): return lax.ppermute(value, axis, pairs)]
    pallas_call x1, Pallas kernels: 2.18 us -> 1.65 us  [on_device(): call(functools.partial(finish_kernel, bands, count, across), shape((rows,...]
  transfers between devices with their start and end apart: 6 -> 6, of which waited for: 1 -> 0; matrix products, arithmetic and copies ran while one was open for 0% -> 0% of each run, Pallas kernels for 43% -> 58%
where the time goes in v2:
time: 35.9 us; the launch traced here: 35.8 us
  Pallas kernels  24.6 us (69%)
  starting transfers between devices  10.9 us (30%)
    pallas_call x1, Pallas kernels, on_device(): call(functools.partial(matrix_kernel, bands, count), (field, shape((bands...  15.9 us
    ppermute x6, starting transfers between devices, swapped(): return lax.ppermute(value, axis, pairs)  10.9 us
    pallas_call x1, Pallas kernels, on_device(): call(functools.partial(local_kernel, bands, count, across), (shape((bands...  2.97 us
    pallas_call x1, Pallas kernels, on_device(): call(functools.partial(sweep_kernel, bands, count, across), shape((bands,...  2.09 us
    pallas_call x1, Pallas kernels, on_device(): call(functools.partial(finish_kernel, bands, count, across), shape((rows,...  1.65 us
    pallas_call x1, Pallas kernels, on_device(): call(functools.partial(pack_kernel, bands, count, across), (field, face,...  1.53 us
  transfers between devices with their start and end apart: 6, of which 0 were waited for; matrix products, arithmetic and copies ran while one was open for 0% of the time, Pallas kernels for 58%

profile of v2, /device:TPU:11, one launch (start us, length us, event | category | flops | bytes accessed | tf_op | source)
XLA Modules:
  0.0 35.8 jit_solution(885416697994119539)
XLA Ops:
  0.0 1.5 %shard_map.65 = (bf16[2160,128]{1,0:T(8,128)(2,1)S(1)}, bf16[4,135,128]{2,1,0:T(8,128)(2,1)S(1)}, bf16[4,135,128]{2,1,0:T(8,128)(2,1)S(1)}, bf16[16,135]{1,0:T(8...) custom-call(bf16[2160,128]{1,0:T(8,128)(2,1)} %bitcast.7), custom_call_target="tpu_custom_call" | custom-call | bytes 1105920 | tf_op jit(solution)/shard_map/pallas_call | solution.py:365
  1.5 0.7 %collective-permute-start = (bf16[540,128]{1,0:T(8,128)(2,1)S(1)}, bf16[540,128]{1,0:T(8,128)(2,1)S(1)}, u32[]{:S(2)}, u32[]{:S(2)}) collective-permute-start(bf16[540,128]{1,0:T(8,128)(2,1)S(1)} %get-tuple-element.24), channel_id=1, source_target_pairs={{0,16},{16,0},{1,17},{17,1},{2,18},{18,2},{3,19},{19,3},{4,20},{20... | collective-permute-start | bytes 414728 | tf_op jit(solution)/shard_map/ppermute | solution.py:338
  2.3 0.3 collective-permute-start.3
  2.5 4.1 %collective-permute-start.4 = (bf16[4,135,128]{2,1,0:T(8,128)(2,1)S(1)}, bf16[4,135,128]{2,1,0:T(8,128)(2,1)S(1)}, u32[]{:S(2)}, u32[]{:S(2)}) collective-permute-start(bf16[4,135,128]{2,1,0:T(8,128)(2,1)S(1)} %get-tuple-element.33), channel_id=1, source_target_pairs={{4,8},{8,4},{5,9},{9,5},{6,10},{10,6},{7,11},{11,7},{20,24},{24,20... | collective-permute-start | bytes 414728 | tf_op jit(solution)/shard_map/ppermute | solution.py:338
  6.6 0.2 collective-permute-start.1
  6.8 4.3 %collective-permute-start.2 = (bf16[16,135]{1,0:T(8,128)(2,1)S(1)}, bf16[16,135]{1,0:T(8,128)(2,1)S(1)}, u32[]{:S(2)}, u32[]{:S(2)}) collective-permute-start(bf16[16,135]{1,0:T(8,128)(2,1)S(1)} %get-tuple-element.26), channel_id=1, source_target_pairs={{1,2},{2,1},{5,6},{6,5},{9,10},{10,9},{13,14},{14,13},{17,18},{18,... | collective-permute-start | bytes 12968 | tf_op jit(solution)/shard_map/ppermute | solution.py:338
  11.2 15.9 %shard_map.64 = (bf16[2160,128]{1,0:T(8,128)(2,1)S(1)}, bf16[4,5,288,135]{3,2,1,0:T(8,128)(2,1)S(1)}, bf16[4,288,135]{2,1,0:T(8,128)(2,1)S(1)}, bf16[4,288,135]{...) custom-call(s32[4]{0:T(128)} %pattern_far.1, ...), custom_call_target="tpu_custom_call" | custom-call | flops 373248000 | bytes 4194304 | tf_op jit(solution)/shard_map/pallas_call | solution.py:379
  27.1 0.0 collective-permute-done.1.side_even
  27.1 0.0 collective-permute-done.2.side_odd
  27.1 0.0 collective-permute-done.follow
  27.1 3.0 %shard_map.66 = (f32[4,135,512]{2,1,0:T(8,128)S(1)}, f32[135,512]{1,0:T(8,128)S(1)}) custom-call(bf16[2160,128]{1,0:T(8,128)(2,1)S(1)} %get-tuple-element.22.right, bf16[2160,128]{1,0:T(8,128)(2,1)S(1)} %get-tuple-element.23.prev, bf16[540,128]{1,0:T(8,128)(2,1)S(1)} %collective-permute-done.follow, bf16[16,135]{1,0:T(8,128)(2,1)S(1)} %collective-permute-done.1.side_even, ...), custom_call_target="tpu_custom_call" | custom-call | flops 970444800 | bytes 1048576 | tf_op jit(solution)/shard_map/pallas_call | solution.py:403
  30.1 0.0 collective-permute-done.3.face_even
  30.1 0.0 collective-permute-done.4.face_odd
  30.1 0.5 %shard_map.68 = f32[135,512]{1,0:T(8,128)S(1)} custom-call(f32[135,512]{1,0:T(8,128)S(1)} %get-tuple-element.35.partial, bf16[4,2,288,135]{3,2,1,0:T(8,128)(2,1)S(1)} %get-tuple-element.36.edge_reach, f32[12,512]{1,0:T(8,128)S(1)} %get-tuple-element.21.masks, bf16[4,135,128]{2,1,0:T(8,128)(2,1)S(1)} %collective-permute-done.3.face_even, ...), custom_call_target="tpu_custom_call" | custom-call | flops 74649600 | bytes 1048576 | tf_op jit(solution)/shard_map/pallas_call | solution.py:416
  30.6 1.3 %collective-permute-start.5 = (f32[135,512]{1,0:T(8,128)S(1)}, f32[135,512]{1,0:T(8,128)S(1)}, u32[]{:S(2)}, u32[]{:S(2)}) collective-permute-start(f32[135,512]{1,0:T(8,128)S(1)} %shard_map.68), channel_id=1, source_target_pairs={{0,16},{16,0},{1,17},{17,1},{2,18},{18,2},{3,19},{19,3},{4,20},{20... | collective-permute-start | bytes 829448 | tf_op jit(solution)/shard_map/ppermute | solution.py:338
  31.8 2.1 %shard_map.67.states = f32[4,135,512]{2,1,0:T(8,128)S(1)} custom-call(f32[4,135,512]{2,1,0:T(8,128)S(1)} %get-tuple-element.29.base, f32[12,512]{1,0:T(8,128)S(1)} %get-tuple-element.21.masks, bf16[4,5,288,135]{3,2,1,0:T(8,128)(2,1)S(1)} %get-tuple-element.27.maps, bf16[4,288,135]{2,1,0:T(8,128)(2,1)S(1)} %get-tuple-element.30.inverse_maps, ...), custom_call_target="tpu_custom_call" | custom-call | flops 522547200 | bytes 1048576 | tf_op jit(solution)/shard_map/pallas_call | solution.py:423
  33.9 0.0 collective-permute-done.5.incoming
  33.9 1.7 %shard_map.69 = f32[2160,128]{1,0:T(8,128)} custom-call(f32[12,512]{1,0:T(8,128)S(1)} %get-tuple-element.21.masks, f32[4,135,512]{2,1,0:T(8,128)S(1)} %shard_map.67.states, bf16[4,288,135]{2,1,0:T(8,128)(2,1)S(1)} %get-tuple-element.34.chains, f32[135,512]{1,0:T(8,128)S(1)} %collective-permute-done.5.incoming), custom_call_target="tpu_custom_call" | custom-call | flops 223948800 | bytes 1048576 | tf_op jit(solution)/shard_map/pallas_call | solution.py:442
Async XLA Ops:
  1.5 25.5 %collective-permute-start = (bf16[540,128]{1,0:T(8,128)(2,1)S(1)}, bf16[540,128]{1,0:T(8,128)(2,1)S(1)}, u32[]{:S(2)}, u32[]{:S(2)}) collective-permute-start(bf16[540,128]{1,0:T(8,128)(2,1)S(1)} %get-tuple-element.24), channel_id=1, source_target_pairs={{0,16},{16,0},{1,17},{17,1},{2,18},{18,2},{3,19},{19,3},{4,20},{20... | collective-permute-start | bytes 414728 | tf_op jit(solution)/shard_map/ppermute | solution.py:338
  2.3 27.8 %collective-permute-start.3 = (bf16[4,135,128]{2,1,0:T(8,128)(2,1)S(1)}, bf16[4,135,128]{2,1,0:T(8,128)(2,1)S(1)}, u32[]{:S(2)}, u32[]{:S(2)}) collective-permute-start(bf16[4,135,128]{2,1,0:T(8,128)(2,1)S(1)} %get-tuple-element.32), channel_id=1, source_target_pairs={{0,4},{4,0},{8,12},{12,8},{1,5},{5,1},{9,13},{13,9},{2,6},{6,2},{1... | collective-permute-start | bytes 414728 | tf_op jit(solution)/shard_map/ppermute | solution.py:338
  2.5 27.5 %collective-permute-start.4 = (bf16[4,135,128]{2,1,0:T(8,128)(2,1)S(1)}, bf16[4,135,128]{2,1,0:T(8,128)(2,1)S(1)}, u32[]{:S(2)}, u32[]{:S(2)}) collective-permute-start(bf16[4,135,128]{2,1,0:T(8,128)(2,1)S(1)} %get-tuple-element.33), channel_id=1, source_target_pairs={{4,8},{8,4},{5,9},{9,5},{6,10},{10,6},{7,11},{11,7},{20,24},{24,20... | collective-permute-start | bytes 414728 | tf_op jit(solution)/shard_map/ppermute | solution.py:338
  6.6 20.5 %collective-permute-start.1 = (bf16[16,135]{1,0:T(8,128)(2,1)S(1)}, bf16[16,135]{1,0:T(8,128)(2,1)S(1)}, u32[]{:S(2)}, u32[]{:S(2)}) collective-permute-start(bf16[16,135]{1,0:T(8,128)(2,1)S(1)} %get-tuple-element.25), channel_id=1, source_target_pairs={{0,1},{1,0},{2,3},{3,2},{4,5},{5,4},{6,7},{7,6},{8,9},{9,8},{10,11... | collective-permute-start | bytes 12968 | tf_op jit(solution)/shard_map/ppermute | solution.py:338
  6.8 20.2 %collective-permute-start.2 = (bf16[16,135]{1,0:T(8,128)(2,1)S(1)}, bf16[16,135]{1,0:T(8,128)(2,1)S(1)}, u32[]{:S(2)}, u32[]{:S(2)}) collective-permute-start(bf16[16,135]{1,0:T(8,128)(2,1)S(1)} %get-tuple-element.26), channel_id=1, source_target_pairs={{1,2},{2,1},{5,6},{6,5},{9,10},{10,9},{13,14},{14,13},{17,18},{18,... | collective-permute-start | bytes 12968 | tf_op jit(solution)/shard_map/ppermute | solution.py:338
  30.6 3.4 %collective-permute-start.5 = (f32[135,512]{1,0:T(8,128)S(1)}, f32[135,512]{1,0:T(8,128)S(1)}, u32[]{:S(2)}, u32[]{:S(2)}) collective-permute-start(f32[135,512]{1,0:T(8,128)S(1)} %shard_map.68), channel_id=1, source_target_pairs={{0,16},{16,0},{1,17},{17,1},{2,18},{18,2},{3,19},{19,3},{4,20},{20... | collective-permute-start | bytes 829448 | tf_op jit(solution)/shard_map/ppermute | solution.py:338

commit v3 on v2

--- a/solution.py
+++ b/solution.py
@@ -30,23 +30,23 @@
 
 
 def store_halves(ref, value):
-    count = value.shape[0]
-    start = padded_rows(count)
     high, low = halves(value)
-    ref[0:count, :] = high
-    ref[start : start + count, :] = low
-
-
-def apply(stacked, right, count):
-    both = product(stacked, right)
-    start = padded_rows(count)
-    return both[0:count] + both[start : start + count]
-
-
-def apply_halves(stacked, right, count):
+    start = value.shape[0]
+    ref[0:start, :] = high
+    ref[start : 2 * start, :] = low
+
+
+def apply(stacked, right, rows):
+    both = product(stacked[:, : right.shape[0]], right)
+    start = stacked.shape[0] // 2
+    return both[0:rows] + both[start : start + rows]
+
+
+def apply_halves(stacked, right, rows):
     high, low = right
-    rest = product(stacked[0 : padded_rows(count)], low)
-    return apply(stacked, high, count) + rest[0:count]
+    start = stacked.shape[0] // 2
+    rest = product(stacked[0:start, : low.shape[0]], low)
+    return apply(stacked, high, rows) + rest[0:rows]
 
 
 def lane_blocks(ref, start, count, across):
@@ -107,18 +107,18 @@
 
 
 def parts(ref, count):
-    start = padded_rows(count)
+    start = ref.shape[0] // 2
     return ref[0:count, :], ref[start : start + count, :]
 
 
 def combine(out, left, right, count):
-    store_halves(out, apply_halves(left[...], parts(right, count), count))
+    store_halves(out, apply_halves(left[...], parts(right, count), out.shape[0] // 2))
 
 
 def matrix_kernel(
     bands, count, pattern_far, live_far, faces, inverses, right,
     right_kept, maps, inverse_maps, step_maps, reach, edge_reach, chains, masks,
-    faces_here, inverses_here, pool, pattern, live, sems,
+    faces_here, inverses_here, pool, staged, pattern, live, sems,
 ):
     cells = masks.shape[-1]
     copies = [pltpu.make_async_copy(inverses, inverses_here, sems.at[0])]
@@ -134,6 +134,15 @@
         copy.start()
     for copy in small:
         copy.wait()
+    staged[...] = jnp.zeros(staged.shape, F32)
+    taken = [0]
+
+    def selected(source, band):
+        ref = staged.at[taken[0]]
+        taken[0] += 1
+        ref[0:count, 0:count] = source[:, which[band], :]
+        return ref[...]
+
     slot = lax.broadcasted_iota(jnp.int32, (1, cells), 1)
     counts = [live[z] for z in range(bands)]
     before, after = counts[0], counts[bands - 1]
@@ -145,11 +154,12 @@
     which = [pattern[z] for z in range(bands)]
     copies[0].wait()
     for z in range(bands):
-        store_halves(inverse_maps.at[z], inverses_here[:, which[z], :])
+        store_halves(inverse_maps.at[z], selected(inverses_here, z))
     copies[1].wait()
     for z in range(bands):
-        upstream = halves(faces_here[0, :, which[z], :])
-        store_halves(step_maps.at[z], -apply_halves(inverse_maps[z], upstream, count))
+        high, low = halves(selected(faces_here.at[0], z))
+        upstream = high[0:count], low[0:count]
+        store_halves(step_maps.at[z], -apply_halves(inverse_maps[z], upstream, high.shape[0]))
     spare = [0]
 
     def fresh():
@@ -180,7 +190,7 @@
         copies[2 + place].wait()
         for z in range(bands):
             ref = maps.at[z, face - 1]
-            store_halves(ref, faces_here[face, :, which[z], :])
+            store_halves(ref, selected(faces_here.at[face], z))
             if place < 2:
                 combine(edge_reach.at[z, place], reach.at[z], ref, count)
     chains[0] = step_maps[0]
@@ -349,7 +359,7 @@
 def on_device(right_side, previous, diag_inverse, face_blocks, pattern, live_count):
     bands, count, across, along = right_side.shape
     cells, rows = across * along, bands * count * across
-    pads = 2 * padded_rows(count)
+    pads, wide_count = 2 * padded_rows(count), rounded(count, 128)
     shape = jax.ShapeDtypeStruct
     right = in_hbm(right_side.reshape(rows, along))
     prev = in_hbm(previous.reshape(rows, along))
@@ -374,17 +384,17 @@
     side_even = swapped(side_even, "cy", 0)
     side_odd = swapped(side_odd, "cy", 1)
     follow = passed_along(first, "sweep", -1)
-    matrix = shape((bands, pads, count), BF16)
+    matrix = shape((bands, pads, wide_count), BF16)
     step_flops = count * count * cells * 2
     right_kept, maps, inverse_maps, step_maps, reach, edge_reach, chains, masks = call(
         functools.partial(matrix_kernel, bands, count),
         (
             field,
-            shape((bands, 5, pads, count), BF16),
+            shape((bands, 5, pads, wide_count), BF16),
             matrix,
             matrix,
             matrix,
-            shape((bands, 2, pads, count), BF16),
+            shape((bands, 2, pads, wide_count), BF16),
             matrix,
             shape((3 * bands, cells), F32),
         ),
@@ -392,7 +402,8 @@
         [
             pltpu.VMEM(faces.shape, F32),
             pltpu.VMEM(inverses.shape, F32),
-            pltpu.VMEM((4 * bands, pads, count), BF16),
+            pltpu.VMEM((4 * bands, pads, wide_count), BF16),
+            pltpu.VMEM((7 * bands, pads // 2, wide_count), F32),
             pltpu.SMEM((bands,), jnp.int32),
             pltpu.SMEM((bands,), jnp.int32),
             pltpu.SemaphoreType.DMA((10,)),
@@ -430,7 +441,7 @@
     incoming = passed_along(last, "sweep", 1)
     if lax.axis_size("sweep") > 2:
         start = padded_rows(count)
-        end_map = chains[-1, 0:count].astype(F32) + chains[-1, start : start + count].astype(F32)
+        end_map = chains[-1, 0:count, 0:count].astype(F32) + chains[-1, start : start + count, 0:count].astype(F32)
         slot = jnp.arange(cells, dtype=jnp.int32)
         kept = (slot < jnp.min(live_count)).astype(F32)
 

time: 35.9 us -> 25.1 us (0.70)
  Pallas kernels: 24.6 us -> 13.9 us
    pallas_call x1, Pallas kernels: 15.9 us -> 5.2 us  [on_device(): call(functools.partial(matrix_kernel, bands, count), (field, shape((bands...]
  transfers between devices with their start and end apart: 6 -> 6, of which waited for: 0 -> 0; matrix products, arithmetic and copies ran while one was open for 0% -> 0% of each run, Pallas kernels for 58% -> 41%
where the time goes in v3:
time: 25.1 us; the launch traced here: 24.9 us
  Pallas kernels  13.9 us (55%)
  starting transfers between devices  10.9 us (43%)
    ppermute x6, starting transfers between devices, swapped(): return lax.ppermute(value, axis, pairs)  10.9 us
    pallas_call x1, Pallas kernels, on_device(): call(functools.partial(matrix_kernel, bands, count), (field, shape((bands...  5.2 us
    pallas_call x1, Pallas kernels, on_device(): call(functools.partial(local_kernel, bands, count, across), (shape((bands...  2.97 us
    pallas_call x1, Pallas kernels, on_device(): call(functools.partial(sweep_kernel, bands, count, across), shape((bands,...  2.09 us
    pallas_call x1, Pallas kernels, on_device(): call(functools.partial(finish_kernel, bands, count, across), shape((rows,...  1.65 us
    pallas_call x1, Pallas kernels, on_device(): call(functools.partial(pack_kernel, bands, count, across), (field, face,...  1.53 us
  transfers between devices with their start and end apart: 6, of which 0 were waited for; matrix products, arithmetic and copies ran while one was open for 0% of the time, Pallas kernels for 41%

profile of v3, /device:TPU:11, one launch (start us, length us, event | category | flops | bytes accessed | tf_op | source)
XLA Modules:
  0.0 24.9 jit_solution(6323629646673980159)
XLA Ops:
  0.0 1.5 %shard_map.65 = (bf16[2160,128]{1,0:T(8,128)(2,1)S(1)}, bf16[4,135,128]{2,1,0:T(8,128)(2,1)S(1)}, bf16[4,135,128]{2,1,0:T(8,128)(2,1)S(1)}, bf16[16,135]{1,0:T(8...) custom-call(bf16[2160,128]{1,0:T(8,128)(2,1)} %bitcast.7), custom_call_target="tpu_custom_call" | custom-call | bytes 1105920 | tf_op jit(solution)/shard_map/pallas_call | solution.py:375
  1.5 0.7 %collective-permute-start = (bf16[540,128]{1,0:T(8,128)(2,1)S(1)}, bf16[540,128]{1,0:T(8,128)(2,1)S(1)}, u32[]{:S(2)}, u32[]{:S(2)}) collective-permute-start(bf16[540,128]{1,0:T(8,128)(2,1)S(1)} %get-tuple-element.24), channel_id=1, source_target_pairs={{0,16},{16,0},{1,17},{17,1},{2,18},{18,2},{3,19},{19,3},{4,20},{20... | collective-permute-start | bytes 414728 | tf_op jit(solution)/shard_map/ppermute | solution.py:348
  2.3 0.3 %collective-permute-start.3 = (bf16[4,135,128]{2,1,0:T(8,128)(2,1)S(1)}, bf16[4,135,128]{2,1,0:T(8,128)(2,1)S(1)}, u32[]{:S(2)}, u32[]{:S(2)}) collective-permute-start(bf16[4,135,128]{2,1,0:T(8,128)(2,1)S(1)} %get-tuple-element.32), channel_id=1, source_target_pairs={{0,4},{4,0},{8,12},{12,8},{1,5},{5,1},{9,13},{13,9},{2,6},{6,2},{1... | collective-permute-start | bytes 414728 | tf_op jit(solution)/shard_map/ppermute | solution.py:348
  2.5 4.1 %collective-permute-start.4 = (bf16[4,135,128]{2,1,0:T(8,128)(2,1)S(1)}, bf16[4,135,128]{2,1,0:T(8,128)(2,1)S(1)}, u32[]{:S(2)}, u32[]{:S(2)}) collective-permute-start(bf16[4,135,128]{2,1,0:T(8,128)(2,1)S(1)} %get-tuple-element.33), channel_id=1, source_target_pairs={{4,8},{8,4},{5,9},{9,5},{6,10},{10,6},{7,11},{11,7},{20,24},{24,20... | collective-permute-start | bytes 414728 | tf_op jit(solution)/shard_map/ppermute | solution.py:348
  6.6 0.2 collective-permute-start.1
  6.8 4.3 %collective-permute-start.2 = (bf16[16,135]{1,0:T(8,128)(2,1)S(1)}, bf16[16,135]{1,0:T(8,128)(2,1)S(1)}, u32[]{:S(2)}, u32[]{:S(2)}) collective-permute-start(bf16[16,135]{1,0:T(8,128)(2,1)S(1)} %get-tuple-element.26), channel_id=1, source_target_pairs={{1,2},{2,1},{5,6},{6,5},{9,10},{10,9},{13,14},{14,13},{17,18},{18,... | collective-permute-start | bytes 12968 | tf_op jit(solution)/shard_map/ppermute | solution.py:348
  11.2 5.2 %shard_map.64 = (bf16[2160,128]{1,0:T(8,128)(2,1)S(1)}, bf16[4,5,288,256]{3,2,1,0:T(8,128)(2,1)S(1)}, bf16[4,288,256]{2,1,0:T(8,128)(2,1)S(1)}, bf16[4,288,256]{...) custom-call(s32[4]{0:T(128)} %pattern_far.1, ...), custom_call_target="tpu_custom_call" | custom-call | flops 373248000 | bytes 4194304 | tf_op jit(solution)/shard_map/pallas_call | solution.py:389
  16.4 0.0 collective-permute-done.1.side_even
  16.4 0.0 collective-permute-done.2.side_odd
  16.4 0.0 collective-permute-done.follow
  16.4 3.0 %shard_map.66 = (f32[4,135,512]{2,1,0:T(8,128)S(1)}, f32[135,512]{1,0:T(8,128)S(1)}) custom-call(bf16[2160,128]{1,0:T(8,128)(2,1)S(1)} %get-tuple-element.22.right, bf16[2160,128]{1,0:T(8,128)(2,1)S(1)} %get-tuple-element.23.prev, bf16[540,128]{1,0:T(8,128)(2,1)S(1)} %collective-permute-done.follow, bf16[16,135]{1,0:T(8,128)(2,1)S(1)} %collective-permute-done.1.side_even, ...), custom_call_target="tpu_custom_call" | custom-call | flops 970444800 | bytes 1048576 | tf_op jit(solution)/shard_map/pallas_call | solution.py:414
  19.4 0.0 collective-permute-done.3.face_even
  19.4 0.0 collective-permute-done.4.face_odd
  19.4 0.5 %shard_map.68 = f32[135,512]{1,0:T(8,128)S(1)} custom-call(f32[135,512]{1,0:T(8,128)S(1)} %get-tuple-element.35.partial, bf16[4,2,288,256]{3,2,1,0:T(8,128)(2,1)S(1)} %get-tuple-element.36.edge_reach, f32[12,512]{1,0:T(8,128)S(1)} %get-tuple-element.21.masks, bf16[4,135,128]{2,1,0:T(8,128)(2,1)S(1)} %collective-permute-done.3.face_even, ...), custom_call_target="tpu_custom_call" | custom-call | flops 74649600 | bytes 1048576 | tf_op jit(solution)/shard_map/pallas_call | solution.py:427
  19.9 1.2 %collective-permute-start.5 = (f32[135,512]{1,0:T(8,128)S(1)}, f32[135,512]{1,0:T(8,128)S(1)}, u32[]{:S(2)}, u32[]{:S(2)}) collective-permute-start(f32[135,512]{1,0:T(8,128)S(1)} %shard_map.68), channel_id=1, source_target_pairs={{0,16},{16,0},{1,17},{17,1},{2,18},{18,2},{3,19},{19,3},{4,20},{20... | collective-permute-start | bytes 829448 | tf_op jit(solution)/shard_map/ppermute | solution.py:348
  21.1 2.1 %shard_map.67.states = f32[4,135,512]{2,1,0:T(8,128)S(1)} custom-call(f32[4,135,512]{2,1,0:T(8,128)S(1)} %get-tuple-element.29.base, f32[12,512]{1,0:T(8,128)S(1)} %get-tuple-element.21.masks, bf16[4,5,288,256]{3,2,1,0:T(8,128)(2,1)S(1)} %get-tuple-element.27.maps, bf16[4,288,256]{2,1,0:T(8,128)(2,1)S(1)} %get-tuple-element.30.inverse_maps, ...), custom_call_target="tpu_custom_call" | custom-call | flops 522547200 | bytes 1048576 | tf_op jit(solution)/shard_map/pallas_call | solution.py:434
  23.2 0.0 collective-permute-done.5.incoming
  23.2 1.7 %shard_map.69 = f32[2160,128]{1,0:T(8,128)} custom-call(f32[12,512]{1,0:T(8,128)S(1)} %get-tuple-element.21.masks, f32[4,135,512]{2,1,0:T(8,128)S(1)} %shard_map.67.states, bf16[4,288,256]{2,1,0:T(8,128)(2,1)S(1)} %get-tuple-element.34.chains, f32[135,512]{1,0:T(8,128)S(1)} %collective-permute-done.5.incoming), custom_call_target="tpu_custom_call" | custom-call | flops 223948800 | bytes 1048576 | tf_op jit(solution)/shard_map/pallas_call | solution.py:453
Async XLA Ops:
  1.5 14.9 %collective-permute-start = (bf16[540,128]{1,0:T(8,128)(2,1)S(1)}, bf16[540,128]{1,0:T(8,128)(2,1)S(1)}, u32[]{:S(2)}, u32[]{:S(2)}) collective-permute-start(bf16[540,128]{1,0:T(8,128)(2,1)S(1)} %get-tuple-element.24), channel_id=1, source_target_pairs={{0,16},{16,0},{1,17},{17,1},{2,18},{18,2},{3,19},{19,3},{4,20},{20... | collective-permute-start | bytes 414728 | tf_op jit(solution)/shard_map/ppermute | solution.py:348
  2.3 17.1 %collective-permute-start.3 = (bf16[4,135,128]{2,1,0:T(8,128)(2,1)S(1)}, bf16[4,135,128]{2,1,0:T(8,128)(2,1)S(1)}, u32[]{:S(2)}, u32[]{:S(2)}) collective-permute-start(bf16[4,135,128]{2,1,0:T(8,128)(2,1)S(1)} %get-tuple-element.32), channel_id=1, source_target_pairs={{0,4},{4,0},{8,12},{12,8},{1,5},{5,1},{9,13},{13,9},{2,6},{6,2},{1... | collective-permute-start | bytes 414728 | tf_op jit(solution)/shard_map/ppermute | solution.py:348
  2.5 16.9 %collective-permute-start.4 = (bf16[4,135,128]{2,1,0:T(8,128)(2,1)S(1)}, bf16[4,135,128]{2,1,0:T(8,128)(2,1)S(1)}, u32[]{:S(2)}, u32[]{:S(2)}) collective-permute-start(bf16[4,135,128]{2,1,0:T(8,128)(2,1)S(1)} %get-tuple-element.33), channel_id=1, source_target_pairs={{4,8},{8,4},{5,9},{9,5},{6,10},{10,6},{7,11},{11,7},{20,24},{24,20... | collective-permute-start | bytes 414728 | tf_op jit(solution)/shard_map/ppermute | solution.py:348
  6.6 9.8 %collective-permute-start.1 = (bf16[16,135]{1,0:T(8,128)(2,1)S(1)}, bf16[16,135]{1,0:T(8,128)(2,1)S(1)}, u32[]{:S(2)}, u32[]{:S(2)}) collective-permute-start(bf16[16,135]{1,0:T(8,128)(2,1)S(1)} %get-tuple-element.25), channel_id=1, source_target_pairs={{0,1},{1,0},{2,3},{3,2},{4,5},{5,4},{6,7},{7,6},{8,9},{9,8},{10,11... | collective-permute-start | bytes 12968 | tf_op jit(solution)/shard_map/ppermute | solution.py:348
  6.8 9.5 %collective-permute-start.2 = (bf16[16,135]{1,0:T(8,128)(2,1)S(1)}, bf16[16,135]{1,0:T(8,128)(2,1)S(1)}, u32[]{:S(2)}, u32[]{:S(2)}) collective-permute-start(bf16[16,135]{1,0:T(8,128)(2,1)S(1)} %get-tuple-element.26), channel_id=1, source_target_pairs={{1,2},{2,1},{5,6},{6,5},{9,10},{10,9},{13,14},{14,13},{17,18},{18,... | collective-permute-start | bytes 12968 | tf_op jit(solution)/shard_map/ppermute | solution.py:348
  19.9 3.4 %collective-permute-start.5 = (f32[135,512]{1,0:T(8,128)S(1)}, f32[135,512]{1,0:T(8,128)S(1)}, u32[]{:S(2)}, u32[]{:S(2)}) collective-permute-start(f32[135,512]{1,0:T(8,128)S(1)} %shard_map.68), channel_id=1, source_target_pairs={{0,16},{16,0},{1,17},{17,1},{2,18},{18,2},{3,19},{19,3},{4,20},{20... | collective-permute-start | bytes 829448 | tf_op jit(solution)/shard_map/ppermute | solution.py:348

commit v4 on v3

v4 whole, which is shorter than its diff:
```python
import functools

import jax
import jax.numpy as jnp
from jax import lax
from jax.experimental import pallas as pl
from jax.experimental.pallas import tpu as pltpu
from jax.sharding import PartitionSpec as P


F32, BF16 = jnp.float32, jnp.bfloat16
VMEM = pl.BlockSpec(memory_space=pltpu.VMEM)
HBM = pl.BlockSpec(memory_space=pltpu.HBM)


def rounded(count, unit):
    return (count + unit - 1) // unit * unit


def padded_rows(count):
    return rounded(count, 16)


def product(left, right):
    return jnp.dot(left, right, preferred_element_type=F32)


def halves(value):
    high = value.astype(BF16)
    return high, (value - high.astype(F32)).astype(BF16)


def store_halves(ref, value):
    high, low = halves(value)
    start = value.shape[0]
    ref[0:start, :] = high
    ref[start : 2 * start, :] = low


def apply(stacked, right, rows):
    both = product(stacked[:, : right.shape[0]], right)
    start = stacked.shape[0] // 2
    return both[0:rows] + both[start : start + rows]


def apply_halves(stacked, right, rows):
    high, low = right
    start = stacked.shape[0] // 2
    rest = product(stacked[0:start, : low.shape[0]], low)
    return apply(stacked, high, rows) + rest[0:rows]


def lane_blocks(ref, start, count, across):
    return [ref[pl.ds(start + i, count, stride=across), :] for i in range(across)]


def rest_rows(count):
    return rounded(count, 8)


def rest_of(value, head, count):
    piece = value[head:]
    row = lax.broadcasted_iota(jnp.int32, piece.shape, 0)
    return jnp.where(row < count - head, piece, 0.0)


def stacked_rests(pieces, head):
    used = sum(piece.shape[0] for piece in pieces)
    return jnp.concatenate(list(pieces) + [jnp.zeros((head - used, pieces[0].shape[1]), F32)], axis=0)


def chunks(rows):
    return 2 if rows % 32 == 0 else 1


def start_copies(source, target, sems, first=0):
    rows = source.shape[0]
    size = rows // chunks(rows)
    copies = []
    for at in range(chunks(rows)):
        window = pl.ds(at * size, size)
        copies.append(pltpu.make_async_copy(source.at[window], target.at[window], sems.at[first + at]))
        copies[-1].start()
    return copies


def select_block(main, tail, firsts, which, rows, patterns, staged):
    staged[:, 0 : tail.shape[-1]] = tail[pl.ds(firsts[1] + which, rows, stride=patterns), :]
    return jnp.concatenate([main[pl.ds(firsts[0] + which, rows, stride=patterns), :], staged[...]], axis=1)


def pack_kernel(
    bands, count, across, prev, pattern_far, live_far, faces, inverses,
    kept, face_even, face_odd, side_even, side_odd, first, inverse_maps, upstream_maps, masks,
    wide, rows_even, rows_odd, main, tail, inverse_main, inverse_tail, staged, pattern, live, sems,
):
    along = prev.shape[-1]
    rows = prev.shape[0]
    copies = start_copies(prev, kept, sems)
    room, patterns, lanes = main.shape
    ragged = count - lanes
    small = [
        pltpu.make_async_copy(pattern_far, pattern, sems.at[2]),
        pltpu.make_async_copy(live_far, live, sems.at[3]),
    ]
    large = [
        pltpu.make_async_copy(
            inverses.at[:, :, pl.ds(0, lanes)], inverse_main.at[pl.ds(0, count)], sems.at[4]
        ),
        pltpu.make_async_copy(
            inverses.at[:, :, pl.ds(lanes, ragged)], inverse_tail.at[pl.ds(0, count)], sems.at[5]
        ),
        pltpu.make_async_copy(faces.at[0, :, :, pl.ds(0, lanes)], main.at[pl.ds(0, count)], sems.at[6]),
        pltpu.make_async_copy(faces.at[0, :, :, pl.ds(lanes, ragged)], tail.at[pl.ds(0, count)], sems.at[7]),
    ]
    for copy in small + large:
        copy.start()
    staged[...] = jnp.zeros(staged.shape, F32)
    wide[rows:, :] = jnp.zeros((wide.shape[0] - rows, along), F32)
    odd_x = lax.axis_index("cx") % 2 == 1
    odd_y = lax.axis_index("cy") % 2 == 1
    row = lax.broadcasted_iota(jnp.int32, (8, along), 0)
    lane = lax.broadcasted_iota(jnp.int32, (8, along), 1)
    last = along - 1
    even_lane, odd_lane = jnp.where(odd_y, 0, last), jnp.where(odd_y, last, 0)
    chosen = jnp.where(row == 0, even_lane, odd_lane)
    pick = jnp.where(lane == chosen, 1.0, 0.0).astype(BF16)
    size = rows // len(copies)
    done = 0
    for z in range(bands):
        while done * size < min(rows, ((z + 1) * count + 8) * across):
            copies[done].wait()
            window = pl.ds(done * size, size)
            wide[window, :] = kept[window, :].astype(F32)
            done += 1
        blocks = lane_blocks(wide, z * count * across, rest_rows(count), across)
        low, high = blocks[0], blocks[-1]
        face_even[z] = jnp.where(odd_x, low, high).astype(BF16)
        face_odd[z] = jnp.where(odd_x, high, low).astype(BF16)
        for i in range(across):
            found = lax.dot_general(
                pick, blocks[i][0:count].astype(BF16), (((1,), (1,)), ((), ())), preferred_element_type=F32
            )
            at = z * across + i
            rows_even[at : at + 1, :] = found[0:1]
            rows_odd[at : at + 1, :] = found[1:2]
    first[...] = kept[0 : count * across, :]
    side_even[...] = rows_even[...].astype(BF16)
    side_odd[...] = rows_odd[...].astype(BF16)
    for copy in small:
        copy.wait()
    slot = lax.broadcasted_iota(jnp.int32, (1, masks.shape[-1]), 1)
    counts = [live[z] for z in range(bands)]
    before, after = counts[0], counts[bands - 1]
    for z in range(bands):
        before = jnp.minimum(before, counts[z])
        after = jnp.minimum(after, counts[bands - 1 - z])
        for row, limit in ((z, counts[z]), (2 * bands - 1 - z, after), (2 * bands + z, before)):
            masks[row : row + 1, :] = jnp.where(slot < limit, 1.0, 0.0)
    for copy in large:
        copy.wait()
    high_rows = padded_rows(count)
    views = [
        (inverse_main.reshape(room * patterns, lanes), inverse_tail.reshape(room * patterns, ragged), inverse_maps),
        (main.reshape(room * patterns, lanes), tail.reshape(room * patterns, ragged), upstream_maps),
    ]
    for at, (near, rest, target) in enumerate(views):
        for z in range(bands):
            value = select_block(near, rest, (0, 0), pattern[z], high_rows, patterns, staged.at[at * bands + z])
            store_halves(target.at[z], value)


def parts(ref, count):
    start = ref.shape[0] // 2
    return ref[0:count, :], ref[start : start + count, :]


def combine(out, left, right, count):
    store_halves(out, apply_halves(left[...], parts(right, count), out.shape[0] // 2))


def matrix_kernel(
    bands, count, pattern_far, faces, right, inverse_maps, upstream_maps,
    right_kept, maps, step_maps, reach, chains,
    main, tail, pool, staged, pattern, sems,
):
    patterns, lanes = main.shape[1:]
    ragged = count - lanes
    high_rows = padded_rows(count)
    room = tail.shape[1]
    used = tail.shape[0]
    copies = [pltpu.make_async_copy(pattern_far, pattern, sems.at[0])]
    for at in range(used):
        source = faces.at[at + 1]
        copies.append(
            pltpu.make_async_copy(
                source.at[:, :, pl.ds(0, lanes)], main.at[pl.ds(at * count, count)], sems.at[1 + 2 * at]
            )
        )
        copies.append(
            pltpu.make_async_copy(
                source.at[:, :, pl.ds(lanes, ragged)], tail.at[at, pl.ds(0, count)], sems.at[2 + 2 * at]
            )
        )
    copies.append(pltpu.make_async_copy(right, right_kept, sems.at[1 + 2 * used]))
    for copy in copies:
        copy.start()
    staged[...] = jnp.zeros(staged.shape, F32)
    main_rows = main.reshape(main.shape[0] * patterns, lanes)
    tail_rows = tail.reshape(used * room * patterns, ragged)

    def selected(band, face):
        at = face - 1
        firsts = (at * count * patterns, at * room * patterns)
        return select_block(
            main_rows, tail_rows, firsts, pattern[band], high_rows, patterns, staged.at[at * bands + band]
        )

    for z in range(bands):
        upstream = parts(upstream_maps.at[z], count)
        store_halves(step_maps.at[z], -apply_halves(inverse_maps[z], upstream, high_rows))
    spare = [0]

    def fresh():
        spare[0] += 1
        return pool.at[spare[0] - 1]

    def solve(low, high, top):
        if high - low == 1:
            return {low: inverse_maps.at[low]}, step_maps.at[low]
        middle = (low + high) // 2
        near, near_step = solve(low, middle, False)
        found, far_step = solve(middle, high, False)
        for z, ref in near.items():
            found[z] = fresh()
            combine(found[z], far_step, ref, count)
        step = None
        if not top:
            step = fresh()
            combine(step, far_step, near_step, count)
        return found, step

    full_reach, _ = solve(0, bands, True)
    chains[0] = step_maps[0]
    for z in range(1, bands):
        combine(chains.at[z], step_maps.at[z], chains.at[z - 1], count)

    def put(ref, tile, value):
        high, low = halves(value)
        window = pl.ds(tile * lanes, lanes)
        ref[0:high_rows, window] = high
        ref[high_rows : 2 * high_rows, window] = low

    rests = [None] * bands
    total = maps.shape[2] // lanes - 1

    for copy in copies:
        copy.wait()

    def take(face):
        for z in range(bands):
            value = selected(z, face)
            put(maps.at[z], face - 1, value[:, :lanes])
            rest = pltpu.roll(value[:, lanes:], 8 * (face - 1), axis=1)
            rests[z] = rest if rests[z] is None else rests[z] + rest

    for face in range(1, used + 1):
        take(face)
    reach_rest = None
    for z in range(bands):
        put(maps.at[z], total, rests[z])
        natural = full_reach[z]
        reach[:, pl.ds(z * lanes, lanes)] = natural[:, 0:lanes]
        rest = natural[0:high_rows, lanes:].astype(F32) + natural[high_rows:, lanes:].astype(F32)
        rest = pltpu.roll(rest, 8 * z, axis=1)
        reach_rest = rest if reach_rest is None else reach_rest + rest
    put(reach, bands, reach_rest)


def local_kernel(
    bands, count, across, right, prev, follow, side_even, side_odd, face_even, face_odd, maps, reach, masks,
    base, last_band, wide, wide_right, wide_follow, sides, stacks, high_stack, low_stack,
):
    along = prev.shape[-1]
    rows = prev.shape[0]
    block = count * across
    deep = rest_rows(count)
    head = count // 128 * 128
    odd_y = lax.axis_index("cy") % 2 == 1
    has_next = lax.axis_index("sweep") < lax.axis_size("sweep") - 1
    wide[0:rows, :] = prev[...].astype(F32)
    wide_right[0:rows, :] = right[...].astype(F32)
    wide_follow[0:block, :] = jnp.where(has_next, follow[...].astype(F32), 0.0)
    even, odd = side_even[...].astype(F32), side_odd[...].astype(F32)
    total = bands * across
    sides[0:total, 0:count] = jnp.where(odd_y, even, odd)
    sides[total : 2 * total, 0:count] = jnp.where(odd_y, odd, even)
    columns = sides[...].T
    lane = lax.broadcasted_iota(jnp.int32, (deep, along), 1)
    heads, rests = [], []
    for z in range(bands + 1):
        blocks = lane_blocks(*((wide, z * block) if z < bands else (wide_follow, 0)), deep, across)
        heads.append([value[0:head].astype(BF16) for value in blocks])
        rests.append([rest_of(value, head, count) for value in blocks])
        if z == bands:
            continue
        for i, value in enumerate(blocks):
            window = pl.ds(i * along, along)
            at = z * across + i
            column = columns[0:deep, at : at + 1]
            behind = jnp.where(lane == 0, column, pltpu.roll(value, 1, axis=1))
            column = columns[0:deep, at + total : at + total + 1]
            ahead = jnp.where(lane == along - 1, column, pltpu.roll(value, along - 1, axis=1))
            stacks[z, 3 * head : 4 * head, window] = behind[0:head].astype(BF16)
            stacks[z, 4 * head : 5 * head, window] = ahead[0:head].astype(BF16)
            rests[z][i] = (rests[z][i], rest_of(behind, head, count), rest_of(ahead, head, count))
    final_rests = []
    for z in range(bands):
        minus, plus = edges_of(face_even, face_odd, z)
        for i in range(across):
            window = pl.ds(i * along, along)
            first, last = i == 0, i == across - 1
            stacks[z, 0:head, window] = heads[z + 1][i]
            stacks[z, head : 2 * head, window] = minus[0:head].astype(BF16) if first else heads[z][i - 1]
            stacks[z, 2 * head : 3 * head, window] = plus[0:head].astype(BF16) if last else heads[z][i + 1]
            _, behind, ahead = rests[z][i]
            pieces = [
                rests[z + 1][i][0] if z + 1 < bands else rests[z + 1][i],
                rest_of(minus, head, count) if first else rests[z][i - 1][0],
                rest_of(plus, head, count) if last else rests[z][i + 1][0],
                behind,
                ahead,
            ]
            stacks[z, 5 * head : 6 * head, window] = stacked_rests(pieces, head).astype(BF16)
        drop = apply(maps[z], stacks[z], deep)
        value = jnp.concatenate(lane_blocks(wide_right, z * block, deep, across), axis=1) - drop
        base[z] = value[0:count]
        value = value * masks[bands + z : bands + z + 1, :]
        high, low = halves(value[0:head])
        high_stack[z * head : (z + 1) * head, :] = high
        low_stack[z * head : (z + 1) * head, :] = low
        final_rests.append(rest_of(value, head, count))
    high, low = halves(stacked_rests(final_rests, head))
    high_stack[bands * head :, :] = high
    low_stack[bands * head :, :] = low
    last_band[...] = apply_halves(reach[...], (high_stack[...], low_stack[...]), count)


def edges_of(face_even, face_odd, z):
    odd_x = lax.axis_index("cx") % 2 == 1
    even, odd = face_even[z].astype(F32), face_odd[z].astype(F32)
    return jnp.where(odd_x, even, odd), jnp.where(odd_x, odd, even)


def sweep_kernel(bands, count, base, masks, inverse_maps, step_maps, states):
    shares = [apply_halves(inverse_maps[z], halves(base[z]), count) for z in range(bands)]
    current = None
    for z in range(bands):
        value = shares[z]
        if z > 0:
            value = value + apply_halves(step_maps[z], halves(current), count)
        current = value * masks[z : z + 1, :]
        states[z] = current


def finish_kernel(bands, count, across, masks, states, chains, incoming, out, staged, sems):
    cells = incoming.shape[-1]
    along = cells // across
    rows = staged.shape[0]
    right = halves(jnp.where(lax.axis_index("sweep") > 0, incoming[...], 0.0))
    size = rows // chunks(rows)
    copies = []
    for z in range(bands):
        moved = apply_halves(chains[z], right, count)
        value = states[z] + moved * masks[2 * bands + z : 2 * bands + z + 1, :]
        for i in range(across):
            staged[pl.ds(z * count * across + i, count, stride=across), :] = value[:, i * along : (i + 1) * along]
        while (len(copies) + 1) * size <= (z + 1) * count * across:
            at = len(copies)
            window = pl.ds(at * size, size)
            copies.append(pltpu.make_async_copy(staged.at[window], out.at[window], sems.at[at]))
            copies[-1].start()
    for copy in copies:
        copy.wait()


def call(kernel, out, specs, scratch=(), flops=0, moved=0, out_specs=None):
    return pl.pallas_call(
        kernel,
        out_shape=out,
        in_specs=specs,
        out_specs=out_specs or jax.tree.map(lambda _: VMEM, out),
        scratch_shapes=scratch,
        cost_estimate=pl.CostEstimate(flops=flops, bytes_accessed=moved, transcendentals=0),
        compiler_params=pltpu.CompilerParams(vmem_limit_bytes=32 * 2**20),
    )


def in_hbm(value):
    return pltpu.with_memory_space_constraint(value, pltpu.HBM)


def swapped(value, axis, first):
    pairs = []
    for left in range(first, lax.axis_size(axis) - 1, 2):
        pairs += [(left, left + 1), (left + 1, left)]
    return lax.ppermute(value, axis, pairs)


def passed_along(value, axis, steps):
    count = lax.axis_size(axis)
    if count == 2:
        return swapped(value, axis, 0)
    first, last = (max(0, -steps), min(count, count - steps))
    return lax.ppermute(value, axis, [(source, source + steps) for source in range(first, last)])


def on_device(right_side, previous, diag_inverse, face_blocks, pattern, live_count):
    bands, count, across, along = right_side.shape
    cells, rows = across * along, bands * count * across
    pads, wide_count = 2 * padded_rows(count), rounded(count, 128)
    shape = jax.ShapeDtypeStruct
    patterns, face_total = face_blocks.shape[:2]
    lanes = count // 128 * 128
    right = in_hbm(right_side.reshape(rows, along))
    prev = in_hbm(previous.reshape(rows, along))
    faces = in_hbm(face_blocks.transpose(1, 2, 0, 3))
    inverses = in_hbm(diag_inverse.transpose(1, 0, 2))
    live = in_hbm(live_count.reshape(bands))
    pattern = in_hbm(pattern)
    deep = rest_rows(count)
    face = shape((bands, deep, along), BF16)
    side = shape((bands * across, count), BF16)
    field = shape((rows, along), BF16)
    side_rows = pltpu.VMEM((bands * across, count), F32)
    filled = pltpu.VMEM((rows + 8 * across, along), F32)
    wide = pltpu.VMEM((rows, along), F32)
    matrix = shape((bands, pads, wide_count), BF16)
    block_room = [
        pltpu.VMEM((count + 16, patterns, lanes), F32),
        pltpu.VMEM((count + 16, patterns, count - lanes), F32),
    ]
    small_room = pltpu.SMEM((bands,), jnp.int32)
    (
        kept, face_even, face_odd, side_even, side_odd, first, inverse_maps, upstream_maps, masks
    ) = call(
        functools.partial(pack_kernel, bands, count, across),
        (
            field,
            face,
            face,
            side,
            side,
            shape((count * across, along), BF16),
            matrix,
            matrix,
            shape((3 * bands, cells), F32),
        ),
        [HBM] * 5,
        [filled, side_rows, side_rows]
        + block_room * 2
        + [pltpu.VMEM((2 * bands, pads // 2, lanes), F32), small_room, small_room, pltpu.SemaphoreType.DMA((8,))],
        moved=rows * along * 4,
    )(prev, pattern, live, faces, inverses)
    side_even = swapped(side_even, "cy", 0)
    side_odd = swapped(side_odd, "cy", 1)
    follow = passed_along(first, "sweep", -1)
    face_odd = swapped(face_odd, "cx", 1)
    face_even = swapped(face_even, "cx", 0)
    step_flops = count * count * cells * 2
    used = face_total - 1
    right_kept, maps, step_maps, reach, chains = call(
        functools.partial(matrix_kernel, bands, count),
        (
            field,
            shape((bands, pads, face_total * lanes), BF16),
            matrix,
            shape((pads, (bands + 1) * lanes), BF16),
            matrix,
        ),
        [HBM, HBM, HBM, VMEM, VMEM],
        [
            pltpu.VMEM((used * count + 16, patterns, lanes), F32),
            pltpu.VMEM((used, count + 16, patterns, count - lanes), F32),
            pltpu.VMEM((4 * bands, pads, wide_count), BF16),
            pltpu.VMEM((used * bands, pads // 2, lanes), F32),
            small_room,
            pltpu.SemaphoreType.DMA((2 * used + 2,)),
        ],
        flops=bands * 5 * step_flops,
        moved=4 * 2**20,
    )(pattern, faces, right, inverse_maps, upstream_maps)
    base, last = call(
        functools.partial(local_kernel, bands, count, across),
        (shape((bands, count, cells), F32), shape((count, cells), F32)),
        [VMEM] * 10,
        [
            filled,
            filled,
            pltpu.VMEM(((count + 8) * across, along), F32),
            pltpu.VMEM((rounded(2 * bands * across, 128), rounded(count, 128)), F32),
            pltpu.VMEM((bands, face_total * lanes, cells), BF16),
            pltpu.VMEM(((bands + 1) * lanes, cells), BF16),
            pltpu.VMEM(((bands + 1) * lanes, cells), BF16),
        ],
        flops=bands * 13 * step_flops,
        moved=2**20,
    )(right_kept, kept, follow, side_even, side_odd, face_even, face_odd, maps, reach, masks)
    states = call(
        functools.partial(sweep_kernel, bands, count),
        shape((bands, count, cells), F32),
        [VMEM] * 4,
        flops=bands * 7 * step_flops,
        moved=2**20,
    )(base, masks, inverse_maps, step_maps)
    incoming = passed_along(last, "sweep", 1)
    if lax.axis_size("sweep") > 2:
        start = padded_rows(count)
        end_map = chains[-1, 0:count, 0:count].astype(F32) + chains[-1, start : start + count, 0:count].astype(F32)
        slot = jnp.arange(cells, dtype=jnp.int32)
        kept = (slot < jnp.min(live_count)).astype(F32)

        def relay(_, arriving):
            product = jnp.dot(end_map, arriving, precision=lax.Precision.HIGHEST)
            return passed_along(last + kept[None, :] * product, "sweep", 1)

        incoming = lax.fori_loop(0, lax.axis_size("sweep") - 2, relay, incoming)
    out = call(
        functools.partial(finish_kernel, bands, count, across),
        shape((rows, along), F32),
        [VMEM] * 4,
        [wide, pltpu.SemaphoreType.DMA((2,))],
        flops=bands * 3 * step_flops,
        moved=2**20,
        out_specs=HBM,
    )(masks, states, chains, incoming)
    return out.reshape(bands, count, across, along)


def solution(mesh):
    return jax.shard_map(
        on_device,
        mesh=mesh,
        in_specs=(
            P("sweep", None, "cx", "cy"),
            P("sweep", None, "cx", "cy"),
            P(),
            P(),
            P("sweep"),
            P("sweep", "cx", "cy"),
        ),
        out_specs=P("sweep", None, "cx", "cy"),
        check_vma=False,
    )
```

time: 25.1 us -> 21.4 us (0.85)
  Pallas kernels: 13.9 us -> 10.2 us
    pallas_call x1, Pallas kernels: 5.2 us -> 3.38 us  [on_device(): call(functools.partial(matrix_kernel, bands, count), (field, shape((bands...]
    pallas_call x2 -> x1, Pallas kernels: 2.56 us -> 1.26 us  [on_device(): call(functools.partial(sweep_kernel, bands, count), shape((bands, count,...]
    pallas_call x1, Pallas kernels: 2.97 us -> 2.03 us  [on_device(): call(functools.partial(local_kernel, bands, count, across), (shape((bands...]
    pallas_call x1, Pallas kernels: 1.53 us -> 1.9 us  [on_device(): call(functools.partial(pack_kernel, bands, count, across), (field, face,...]
  transfers between devices with their start and end apart: 6 -> 6, of which waited for: 0 -> 0; matrix products, arithmetic and copies ran while one was open for 0% -> 0% of each run, Pallas kernels for 41% -> 22%
where the time goes in v4:
time: 21.4 us; the launch traced here: 21.2 us
  starting transfers between devices  10.9 us (51%)
  Pallas kernels  10.2 us (48%)
    ppermute x6, starting transfers between devices, swapped(): return lax.ppermute(value, axis, pairs)  10.9 us
    pallas_call x1, Pallas kernels, on_device(): call(functools.partial(matrix_kernel, bands, count), (field, shape((bands...  3.38 us
    pallas_call x1, Pallas kernels, on_device(): call(functools.partial(local_kernel, bands, count, across), (shape((bands...  2.03 us
    pallas_call x1, Pallas kernels, on_device(): call(functools.partial(pack_kernel, bands, count, across), (field, face,...  1.9 us
    pallas_call x1, Pallas kernels, on_device(): call(functools.partial(finish_kernel, bands, count, across), shape((rows,...  1.67 us
    pallas_call x1, Pallas kernels, on_device(): call(functools.partial(sweep_kernel, bands, count), shape((bands, count,...  1.26 us
  transfers between devices with their start and end apart: 6, of which 0 were waited for; matrix products, arithmetic and copies ran while one was open for 0% of the time, Pallas kernels for 22%

profile of v4, /device:TPU:11, one launch (start us, length us, event | category | flops | bytes accessed | tf_op | source)
XLA Modules:
  0.0 21.2 jit_solution(16832126403858938890)
XLA Ops:
  0.0 1.9 %shard_map.64 = (bf16[2160,128]{1,0:T(8,128)(2,1)S(1)}, bf16[4,136,128]{2,1,0:T(8,128)(2,1)S(1)}, bf16[4,136,128]{2,1,0:T(8,128)(2,1)S(1)}, bf16[16,135]{1,0:T(8...) custom-call(bf16[2160,128]{1,0:T(8,128)(2,1)} %bitcast.8, ...), custom_call_target="tpu_custom_call" | custom-call | bytes 1105920 | tf_op jit(solution)/shard_map/pallas_call | solution.py:446
  1.9 0.3 %collective-permute-start.3 = (bf16[4,136,128]{2,1,0:T(8,128)(2,1)S(1)}, bf16[4,136,128]{2,1,0:T(8,128)(2,1)S(1)}, u32[]{:S(2)}, u32[]{:S(2)}) collective-permute-start(bf16[4,136,128]{2,1,0:T(8,128)(2,1)S(1)} %get-tuple-element.29), channel_id=1, source_target_pairs={{0,4},{4,0},{8,12},{12,8},{1,5},{5,1},{9,13},{13,9},{2,6},{6,2},{1... | collective-permute-start | bytes 417800 | tf_op jit(solution)/shard_map/ppermute | solution.py:407
  2.2 4.1 %collective-permute-start.4 = (bf16[4,136,128]{2,1,0:T(8,128)(2,1)S(1)}, bf16[4,136,128]{2,1,0:T(8,128)(2,1)S(1)}, u32[]{:S(2)}, u32[]{:S(2)}) collective-permute-start(bf16[4,136,128]{2,1,0:T(8,128)(2,1)S(1)} %get-tuple-element.30), channel_id=1, source_target_pairs={{4,8},{8,4},{5,9},{9,5},{6,10},{10,6},{7,11},{11,7},{20,24},{24,20... | collective-permute-start | bytes 417800 | tf_op jit(solution)/shard_map/ppermute | solution.py:407
  6.3 1.3 %collective-permute-start = (bf16[540,128]{1,0:T(8,128)(2,1)S(1)}, bf16[540,128]{1,0:T(8,128)(2,1)S(1)}, u32[]{:S(2)}, u32[]{:S(2)}) collective-permute-start(bf16[540,128]{1,0:T(8,128)(2,1)S(1)} %get-tuple-element.26), channel_id=1, source_target_pairs={{0,16},{16,0},{1,17},{17,1},{2,18},{18,2},{3,19},{19,3},{4,20},{20... | collective-permute-start | bytes 414728 | tf_op jit(solution)/shard_map/ppermute | solution.py:407
  7.6 0.2 collective-permute-start.1
  7.8 4.3 %collective-permute-start.2 = (bf16[16,135]{1,0:T(8,128)(2,1)S(1)}, bf16[16,135]{1,0:T(8,128)(2,1)S(1)}, u32[]{:S(2)}, u32[]{:S(2)}) collective-permute-start(bf16[16,135]{1,0:T(8,128)(2,1)S(1)} %get-tuple-element.28), channel_id=1, source_target_pairs={{1,2},{2,1},{5,6},{6,5},{9,10},{10,9},{13,14},{14,13},{17,18},{18,... | collective-permute-start | bytes 12968 | tf_op jit(solution)/shard_map/ppermute | solution.py:407
  12.1 3.4 %shard_map.65 = (bf16[2160,128]{1,0:T(8,128)(2,1)S(1)}, bf16[4,288,768]{2,1,0:T(8,128)(2,1)S(1)}, bf16[4,288,256]{2,1,0:T(8,128)(2,1)S(1)}, bf16[288,640]{1,0:T(8,128)(2,1)S(1)}, bf16[4,288,256]{2,1,0:T(8,128)(2,1)S(1)}) custom-call(s32[4]{0:T(128)} %pattern_far.3, f32[6,135,4,135]{3,2,1,0:T(4,128)} %bitcast.7, bf16[2160,128]{1,0:T(8,128)(2,1)} %bitcast.10, ...), custom_call_target="tpu_custom_call" | custom-call | flops 373248000 | bytes 4194304 | tf_op jit(solution)/shard_map/pallas_call | solution.py:472
  15.5 0.0 collective-permute-done.1.side_even
  15.5 0.0 collective-permute-done.2.side_odd
  15.5 0.0 collective-permute-done.follow
  15.5 0.0 collective-permute-done.3.face_even
  15.5 0.0 collective-permute-done.4.face_odd
  15.5 2.0 %shard_map.66 = (f32[4,135,512]{2,1,0:T(8,128)S(1)}, f32[135,512]{1,0:T(8,128)S(1)}) custom-call(bf16[2160,128]{1,0:T(8,128)(2,1)S(1)} %get-tuple-element.24.right, bf16[2160,128]{1,0:T(8,128)(2,1)S(1)} %get-tuple-element.25.prev, bf16[540,128]{1,0:T(8,128)(2,1)S(1)} %collective-permute-done.follow, bf16[16,135]{1,0:T(8,128)(2,1)S(1)} %collective-permute-done.1.side_even, ...), custom_call_target="tpu_custom_call" | custom-call | flops 970444800 | bytes 1048576 | tf_op jit(solution)/shard_map/pallas_call | solution.py:493
  17.6 0.7 %collective-permute-start.5 = (f32[135,512]{1,0:T(8,128)S(1)}, f32[135,512]{1,0:T(8,128)S(1)}, u32[]{:S(2)}, u32[]{:S(2)}) collective-permute-start(f32[135,512]{1,0:T(8,128)S(1)} %get-tuple-element.36), channel_id=1, source_target_pairs={{0,16},{16,0},{1,17},{17,1},{2,18},{18,2},{3,19},{19,3},{4,20},{20... | collective-permute-start | bytes 829448 | tf_op jit(solution)/shard_map/ppermute | solution.py:407
  18.3 1.3 %shard_map.67.states = f32[4,135,512]{2,1,0:T(8,128)S(1)} custom-call(f32[4,135,512]{2,1,0:T(8,128)S(1)} %get-tuple-element.33.base, f32[12,512]{1,0:T(8,128)S(1)} %get-tuple-element.21.masks, bf16[4,288,256]{2,1,0:T(8,128)(2,1)S(1)} %get-tuple-element.22.inverse_maps, bf16[4,288,256]{2,1,0:T(8,128)(2,1)S(1)} %get-tuple-element.34.step_maps), custom_call_target="tpu_custom_call" | custom-call | flops 522547200 | bytes 1048576 | tf_op jit(solution)/shard_map/pallas_call | solution.py:509
  19.6 0.0 collective-permute-done.5.incoming
  19.6 1.7 %shard_map.68 = f32[2160,128]{1,0:T(8,128)} custom-call(f32[12,512]{1,0:T(8,128)S(1)} %get-tuple-element.21.masks, f32[4,135,512]{2,1,0:T(8,128)S(1)} %shard_map.67.states, bf16[4,288,256]{2,1,0:T(8,128)(2,1)S(1)} %get-tuple-element.35.chains, f32[135,512]{1,0:T(8,128)S(1)} %collective-permute-done.5.incoming), custom_call_target="tpu_custom_call" | custom-call | flops 223948800 | bytes 1048576 | tf_op jit(solution)/shard_map/pallas_call | solution.py:528
Async XLA Ops:
  1.9 13.6 %collective-permute-start.3 = (bf16[4,136,128]{2,1,0:T(8,128)(2,1)S(1)}, bf16[4,136,128]{2,1,0:T(8,128)(2,1)S(1)}, u32[]{:S(2)}, u32[]{:S(2)}) collective-permute-start(bf16[4,136,128]{2,1,0:T(8,128)(2,1)S(1)} %get-tuple-element.29), channel_id=1, source_target_pairs={{0,4},{4,0},{8,12},{12,8},{1,5},{5,1},{9,13},{13,9},{2,6},{6,2},{1... | collective-permute-start | bytes 417800 | tf_op jit(solution)/shard_map/ppermute | solution.py:407
  2.2 13.3 %collective-permute-start.4 = (bf16[4,136,128]{2,1,0:T(8,128)(2,1)S(1)}, bf16[4,136,128]{2,1,0:T(8,128)(2,1)S(1)}, u32[]{:S(2)}, u32[]{:S(2)}) collective-permute-start(bf16[4,136,128]{2,1,0:T(8,128)(2,1)S(1)} %get-tuple-element.30), channel_id=1, source_target_pairs={{4,8},{8,4},{5,9},{9,5},{6,10},{10,6},{7,11},{11,7},{20,24},{24,20... | collective-permute-start | bytes 417800 | tf_op jit(solution)/shard_map/ppermute | solution.py:407
  6.3 9.2 %collective-permute-start = (bf16[540,128]{1,0:T(8,128)(2,1)S(1)}, bf16[540,128]{1,0:T(8,128)(2,1)S(1)}, u32[]{:S(2)}, u32[]{:S(2)}) collective-permute-start(bf16[540,128]{1,0:T(8,128)(2,1)S(1)} %get-tuple-element.26), channel_id=1, source_target_pairs={{0,16},{16,0},{1,17},{17,1},{2,18},{18,2},{3,19},{19,3},{4,20},{20... | collective-permute-start | bytes 414728 | tf_op jit(solution)/shard_map/ppermute | solution.py:407
  7.6 7.9 %collective-permute-start.1 = (bf16[16,135]{1,0:T(8,128)(2,1)S(1)}, bf16[16,135]{1,0:T(8,128)(2,1)S(1)}, u32[]{:S(2)}, u32[]{:S(2)}) collective-permute-start(bf16[16,135]{1,0:T(8,128)(2,1)S(1)} %get-tuple-element.27), channel_id=1, source_target_pairs={{0,1},{1,0},{2,3},{3,2},{4,5},{5,4},{6,7},{7,6},{8,9},{9,8},{10,11... | collective-permute-start | bytes 12968 | tf_op jit(solution)/shard_map/ppermute | solution.py:407
  7.8 7.7 %collective-permute-start.2 = (bf16[16,135]{1,0:T(8,128)(2,1)S(1)}, bf16[16,135]{1,0:T(8,128)(2,1)S(1)}, u32[]{:S(2)}, u32[]{:S(2)}) collective-permute-start(bf16[16,135]{1,0:T(8,128)(2,1)S(1)} %get-tuple-element.28), channel_id=1, source_target_pairs={{1,2},{2,1},{5,6},{6,5},{9,10},{10,9},{13,14},{14,13},{17,18},{18,... | collective-permute-start | bytes 12968 | tf_op jit(solution)/shard_map/ppermute | solution.py:407
  17.6 2.0 %collective-permute-start.5 = (f32[135,512]{1,0:T(8,128)S(1)}, f32[135,512]{1,0:T(8,128)S(1)}, u32[]{:S(2)}, u32[]{:S(2)}) collective-permute-start(f32[135,512]{1,0:T(8,128)S(1)} %get-tuple-element.36), channel_id=1, source_target_pairs={{0,16},{16,0},{1,17},{17,1},{2,18},{18,2},{3,19},{19,3},{4,20},{20... | collective-permute-start | bytes 829448 | tf_op jit(solution)/shard_map/ppermute | solution.py:407

commit v5 on v4

--- a/solution.py
+++ b/solution.py
@@ -254,41 +254,49 @@
     rests = [None] * bands
     total = maps.shape[2] // lanes - 1
 
-    for copy in copies:
-        copy.wait()
+    copies[0].wait()
 
     def take(face):
+        for copy in copies[2 * face - 1 : 2 * face + 1]:
+            copy.wait()
         for z in range(bands):
             value = selected(z, face)
             put(maps.at[z], face - 1, value[:, :lanes])
             rest = pltpu.roll(value[:, lanes:], 8 * (face - 1), axis=1)
             rests[z] = rest if rests[z] is None else rests[z] + rest
 
-    for face in range(1, used + 1):
-        take(face)
     reach_rest = None
     for z in range(bands):
-        put(maps.at[z], total, rests[z])
         natural = full_reach[z]
         reach[:, pl.ds(z * lanes, lanes)] = natural[:, 0:lanes]
         rest = natural[0:high_rows, lanes:].astype(F32) + natural[high_rows:, lanes:].astype(F32)
         rest = pltpu.roll(rest, 8 * z, axis=1)
         reach_rest = rest if reach_rest is None else reach_rest + rest
     put(reach, bands, reach_rest)
+    for face in range(1, used + 1):
+        take(face)
+    for z in range(bands):
+        put(maps.at[z], total, rests[z])
+    copies[-1].wait()
 
 
 def local_kernel(
     bands, count, across, right, prev, follow, side_even, side_odd, face_even, face_odd, maps, reach, masks,
-    base, last_band, wide, wide_right, wide_follow, sides, stacks, high_stack, low_stack,
+    base, last_band, heads, rests, wide, wide_right, wide_follow, sides, shifted, rest_stacks, high_stack, low_stack,
 ):
-    along = prev.shape[-1]
-    rows = prev.shape[0]
+    rows, along = right.shape
     block = count * across
     deep = rest_rows(count)
     head = count // 128 * 128
+    edge = (across - 1) * along
     odd_y = lax.axis_index("cy") % 2 == 1
     has_next = lax.axis_index("sweep") < lax.axis_size("sweep") - 1
     wide[0:rows, :] = prev[...].astype(F32)
+    for z in range(bands):
+        for i, value in enumerate(lane_blocks(wide, z * block, deep, across)):
+            window = pl.ds(i * along, along)
+            heads[z, :, window] = value[0:head].astype(BF16)
+            rests[z, :, window] = rest_of(value, head, count)
     wide_right[0:rows, :] = right[...].astype(F32)
     wide_follow[0:block, :] = jnp.where(has_next, follow[...].astype(F32), 0.0)
     even, odd = side_even[...].astype(F32), side_odd[...].astype(F32)
@@ -297,42 +305,45 @@
     sides[total : 2 * total, 0:count] = jnp.where(odd_y, odd, even)
     columns = sides[...].T
     lane = lax.broadcasted_iota(jnp.int32, (deep, along), 1)
-    heads, rests = [], []
-    for z in range(bands + 1):
-        blocks = lane_blocks(*((wide, z * block) if z < bands else (wide_follow, 0)), deep, across)
-        heads.append([value[0:head].astype(BF16) for value in blocks])
-        rests.append([rest_of(value, head, count) for value in blocks])
-        if z == bands:
-            continue
-        for i, value in enumerate(blocks):
-            window = pl.ds(i * along, along)
+    beyond = lane_blocks(wide_follow, 0, deep, across)
+    beyond_head = jnp.concatenate([value[0:head].astype(BF16) for value in beyond], axis=1)
+    beyond_rest = jnp.concatenate([rest_of(value, head, count) for value in beyond], axis=1)
+    final_rests = []
+    for z in range(bands):
+        minus, plus = edges_of(face_even, face_odd, z)
+        behind_rests, ahead_rests = [], []
+        for i in range(across):
+            window = slice(i * along, (i + 1) * along)
+            value = jnp.concatenate([heads[z, :, window].astype(F32), rests[z, :, window]], axis=0)
             at = z * across + i
             column = columns[0:deep, at : at + 1]
             behind = jnp.where(lane == 0, column, pltpu.roll(value, 1, axis=1))
             column = columns[0:deep, at + total : at + total + 1]
             ahead = jnp.where(lane == along - 1, column, pltpu.roll(value, along - 1, axis=1))
-            stacks[z, 3 * head : 4 * head, window] = behind[0:head].astype(BF16)
-            stacks[z, 4 * head : 5 * head, window] = ahead[0:head].astype(BF16)
-            rests[z][i] = (rests[z][i], rest_of(behind, head, count), rest_of(ahead, head, count))
-    final_rests = []
-    for z in range(bands):
-        minus, plus = edges_of(face_even, face_odd, z)
-        for i in range(across):
-            window = pl.ds(i * along, along)
-            first, last = i == 0, i == across - 1
-            stacks[z, 0:head, window] = heads[z + 1][i]
-            stacks[z, head : 2 * head, window] = minus[0:head].astype(BF16) if first else heads[z][i - 1]
-            stacks[z, 2 * head : 3 * head, window] = plus[0:head].astype(BF16) if last else heads[z][i + 1]
-            _, behind, ahead = rests[z][i]
-            pieces = [
-                rests[z + 1][i][0] if z + 1 < bands else rests[z + 1][i],
-                rest_of(minus, head, count) if first else rests[z][i - 1][0],
-                rest_of(plus, head, count) if last else rests[z][i + 1][0],
-                behind,
-                ahead,
-            ]
-            stacks[z, 5 * head : 6 * head, window] = stacked_rests(pieces, head).astype(BF16)
-        drop = apply(maps[z], stacks[z], deep)
+            shifted[z, 0:head, window] = behind[0:head].astype(BF16)
+            shifted[z, head:, window] = ahead[0:head].astype(BF16)
+            behind_rests.append(rest_of(behind, head, count))
+            ahead_rests.append(rest_of(ahead, head, count))
+        own, own_rest = heads[z], rests[z]
+        pieces = [
+            rests[z + 1] if z + 1 < bands else beyond_rest,
+            jnp.concatenate([rest_of(minus, head, count), own_rest[:, :edge]], axis=1),
+            jnp.concatenate([own_rest[:, along:], rest_of(plus, head, count)], axis=1),
+            jnp.concatenate(behind_rests, axis=1),
+            jnp.concatenate(ahead_rests, axis=1),
+        ]
+        rest_stacks[z] = stacked_rests(pieces, head).astype(BF16)
+        fields = jnp.concatenate(
+            [
+                heads[z + 1] if z + 1 < bands else beyond_head,
+                jnp.concatenate([minus[0:head].astype(BF16), own[:, :edge]], axis=1),
+                jnp.concatenate([own[:, along:], plus[0:head].astype(BF16)], axis=1),
+                shifted[z],
+                rest_stacks[z],
+            ],
+            axis=0,
+        )
+        drop = apply(maps[z], fields, deep)
         value = jnp.concatenate(lane_blocks(wide_right, z * block, deep, across), axis=1) - drop
         base[z] = value[0:count]
         value = value * masks[bands + z : bands + z + 1, :]
@@ -368,18 +379,19 @@
     along = cells // across
     rows = staged.shape[0]
     right = halves(jnp.where(lax.axis_index("sweep") > 0, incoming[...], 0.0))
-    size = rows // chunks(rows)
     copies = []
+    sent = 0
     for z in range(bands):
         moved = apply_halves(chains[z], right, count)
         value = states[z] + moved * masks[2 * bands + z : 2 * bands + z + 1, :]
         for i in range(across):
             staged[pl.ds(z * count * across + i, count, stride=across), :] = value[:, i * along : (i + 1) * along]
-        while (len(copies) + 1) * size <= (z + 1) * count * across:
-            at = len(copies)
-            window = pl.ds(at * size, size)
-            copies.append(pltpu.make_async_copy(staged.at[window], out.at[window], sems.at[at]))
-            copies[-1].start()
+        ready = (z + 1) * count * across
+        ready = rows if ready == rows else ready // 8 * 8
+        window = pl.ds(sent, ready - sent)
+        copies.append(pltpu.make_async_copy(staged.at[window], out.at[window], sems.at[z]))
+        copies[-1].start()
+        sent = ready
     for copy in copies:
         copy.wait()
 
@@ -495,11 +507,14 @@
         (shape((bands, count, cells), F32), shape((count, cells), F32)),
         [VMEM] * 10,
         [
+            pltpu.VMEM((bands, lanes, cells), BF16),
+            pltpu.VMEM((bands, deep - lanes, cells), F32),
             filled,
             filled,
             pltpu.VMEM(((count + 8) * across, along), F32),
             pltpu.VMEM((rounded(2 * bands * across, 128), rounded(count, 128)), F32),
-            pltpu.VMEM((bands, face_total * lanes, cells), BF16),
+            pltpu.VMEM((bands, 2 * lanes, cells), BF16),
+            pltpu.VMEM((bands, lanes, cells), BF16),
             pltpu.VMEM(((bands + 1) * lanes, cells), BF16),
             pltpu.VMEM(((bands + 1) * lanes, cells), BF16),
         ],
@@ -529,7 +544,7 @@
         functools.partial(finish_kernel, bands, count, across),
         shape((rows, along), F32),
         [VMEM] * 4,
-        [wide, pltpu.SemaphoreType.DMA((2,))],
+        [wide, pltpu.SemaphoreType.DMA((bands,))],
         flops=bands * 3 * step_flops,
         moved=2**20,
         out_specs=HBM,

time: 21.4 us -> 20.4 us (0.953)
  Pallas kernels: 10.2 us -> 9.24 us
    pallas_call x1, Pallas kernels: 3.38 us -> 2.74 us  [on_device(): call(functools.partial(matrix_kernel, bands, count), (field, shape((bands...]
    pallas_call x1, Pallas kernels: 1.67 us -> 1.41 us  [on_device(): call(functools.partial(finish_kernel, bands, count, across), shape((rows,...]
  transfers between devices with their start and end apart: 6 -> 6, of which waited for: 0 -> 0; matrix products, arithmetic and copies ran while one was open for 0% -> 0% of each run, Pallas kernels for 22% -> 20%
where the time goes in v5:
time: 20.4 us; the launch traced here: 20.2 us
  starting transfers between devices  10.9 us (53%)
  Pallas kernels  9.24 us (45%)
    ppermute x6, starting transfers between devices, swapped(): return lax.ppermute(value, axis, pairs)  10.9 us
    pallas_call x1, Pallas kernels, on_device(): call(functools.partial(matrix_kernel, bands, count), (field, shape((bands...  2.74 us
    pallas_call x1, Pallas kernels, on_device(): call(functools.partial(local_kernel, bands, count, across), (shape((bands...  1.92 us
    pallas_call x1, Pallas kernels, on_device(): call(functools.partial(pack_kernel, bands, count, across), (field, face,...  1.9 us
    pallas_call x1, Pallas kernels, on_device(): call(functools.partial(finish_kernel, bands, count, across), shape((rows,...  1.41 us
    pallas_call x1, Pallas kernels, on_device(): call(functools.partial(sweep_kernel, bands, count), shape((bands, count,...  1.27 us
  transfers between devices with their start and end apart: 6, of which 0 were waited for; matrix products, arithmetic and copies ran while one was open for 0% of the time, Pallas kernels for 20%

profile of v5, /device:TPU:11, one launch (start us, length us, event | category | flops | bytes accessed | tf_op | source)
XLA Modules:
  0.0 20.2 jit_solution(2444869587343960718)
XLA Ops:
  0.0 1.9 %shard_map.64 = (bf16[2160,128]{1,0:T(8,128)(2,1)S(1)}, bf16[4,136,128]{2,1,0:T(8,128)(2,1)S(1)}, bf16[4,136,128]{2,1,0:T(8,128)(2,1)S(1)}, bf16[16,135]{1,0:T(8...) custom-call(bf16[2160,128]{1,0:T(8,128)(2,1)} %bitcast.8, ...), custom_call_target="tpu_custom_call" | custom-call | bytes 1105920 | tf_op jit(solution)/shard_map/pallas_call | solution.py:458
  1.9 0.3 %collective-permute-start.3 = (bf16[4,136,128]{2,1,0:T(8,128)(2,1)S(1)}, bf16[4,136,128]{2,1,0:T(8,128)(2,1)S(1)}, u32[]{:S(2)}, u32[]{:S(2)}) collective-permute-start(bf16[4,136,128]{2,1,0:T(8,128)(2,1)S(1)} %get-tuple-element.29), channel_id=1, source_target_pairs={{0,4},{4,0},{8,12},{12,8},{1,5},{5,1},{9,13},{13,9},{2,6},{6,2},{1... | collective-permute-start | bytes 417800 | tf_op jit(solution)/shard_map/ppermute | solution.py:419
  2.2 4.1 %collective-permute-start.4 = (bf16[4,136,128]{2,1,0:T(8,128)(2,1)S(1)}, bf16[4,136,128]{2,1,0:T(8,128)(2,1)S(1)}, u32[]{:S(2)}, u32[]{:S(2)}) collective-permute-start(bf16[4,136,128]{2,1,0:T(8,128)(2,1)S(1)} %get-tuple-element.30), channel_id=1, source_target_pairs={{4,8},{8,4},{5,9},{9,5},{6,10},{10,6},{7,11},{11,7},{20,24},{24,20... | collective-permute-start | bytes 417800 | tf_op jit(solution)/shard_map/ppermute | solution.py:419
  6.3 1.3 %collective-permute-start = (bf16[540,128]{1,0:T(8,128)(2,1)S(1)}, bf16[540,128]{1,0:T(8,128)(2,1)S(1)}, u32[]{:S(2)}, u32[]{:S(2)}) collective-permute-start(bf16[540,128]{1,0:T(8,128)(2,1)S(1)} %get-tuple-element.26), channel_id=1, source_target_pairs={{0,16},{16,0},{1,17},{17,1},{2,18},{18,2},{3,19},{19,3},{4,20},{20... | collective-permute-start | bytes 414728 | tf_op jit(solution)/shard_map/ppermute | solution.py:419
  7.6 0.2 collective-permute-start.1
  7.8 4.3 %collective-permute-start.2 = (bf16[16,135]{1,0:T(8,128)(2,1)S(1)}, bf16[16,135]{1,0:T(8,128)(2,1)S(1)}, u32[]{:S(2)}, u32[]{:S(2)}) collective-permute-start(bf16[16,135]{1,0:T(8,128)(2,1)S(1)} %get-tuple-element.28), channel_id=1, source_target_pairs={{1,2},{2,1},{5,6},{6,5},{9,10},{10,9},{13,14},{14,13},{17,18},{18,... | collective-permute-start | bytes 12968 | tf_op jit(solution)/shard_map/ppermute | solution.py:419
  12.1 2.7 %shard_map.65 = (bf16[2160,128]{1,0:T(8,128)(2,1)S(1)}, bf16[4,288,768]{2,1,0:T(8,128)(2,1)S(1)}, bf16[4,288,256]{2,1,0:T(8,128)(2,1)S(1)}, bf16[288,640]{1,0:T(8,128)(2,1)S(1)}, bf16[4,288,256]{2,1,0:T(8,128)(2,1)S(1)}) custom-call(s32[4]{0:T(128)} %pattern_far.3, f32[6,135,4,135]{3,2,1,0:T(4,128)} %bitcast.7, bf16[2160,128]{1,0:T(8,128)(2,1)} %bitcast.10, ...), custom_call_target="tpu_custom_call" | custom-call | flops 373248000 | bytes 4194304 | tf_op jit(solution)/shard_map/pallas_call | solution.py:484
  14.8 0.0 collective-permute-done.1.side_even
  14.9 0.0 collective-permute-done.2.side_odd
  14.9 0.0 collective-permute-done.follow
  14.9 0.0 collective-permute-done.3.face_even
  14.9 0.0 collective-permute-done.4.face_odd
  14.9 1.9 %shard_map.66 = (f32[4,135,512]{2,1,0:T(8,128)S(1)}, f32[135,512]{1,0:T(8,128)S(1)}) custom-call(bf16[2160,128]{1,0:T(8,128)(2,1)S(1)} %get-tuple-element.24.right, bf16[2160,128]{1,0:T(8,128)(2,1)S(1)} %get-tuple-element.25.prev, bf16[540,128]{1,0:T(8,128)(2,1)S(1)} %collective-permute-done.follow, bf16[16,135]{1,0:T(8,128)(2,1)S(1)} %collective-permute-done.1.side_even, ...), custom_call_target="tpu_custom_call" | custom-call | flops 970444800 | bytes 1048576 | tf_op jit(solution)/shard_map/pallas_call | solution.py:505
  16.8 0.7 %collective-permute-start.5 = (f32[135,512]{1,0:T(8,128)S(1)}, f32[135,512]{1,0:T(8,128)S(1)}, u32[]{:S(2)}, u32[]{:S(2)}) collective-permute-start(f32[135,512]{1,0:T(8,128)S(1)} %get-tuple-element.36), channel_id=1, source_target_pairs={{0,16},{16,0},{1,17},{17,1},{2,18},{18,2},{3,19},{19,3},{4,20},{20... | collective-permute-start | bytes 829448 | tf_op jit(solution)/shard_map/ppermute | solution.py:419
  17.5 1.3 %shard_map.67.states = f32[4,135,512]{2,1,0:T(8,128)S(1)} custom-call(f32[4,135,512]{2,1,0:T(8,128)S(1)} %get-tuple-element.33.base, f32[12,512]{1,0:T(8,128)S(1)} %get-tuple-element.21.masks, bf16[4,288,256]{2,1,0:T(8,128)(2,1)S(1)} %get-tuple-element.22.inverse_maps, bf16[4,288,256]{2,1,0:T(8,128)(2,1)S(1)} %get-tuple-element.34.step_maps), custom_call_target="tpu_custom_call" | custom-call | flops 522547200 | bytes 1048576 | tf_op jit(solution)/shard_map/pallas_call | solution.py:524
  18.8 0.0 collective-permute-done.5.incoming
  18.8 1.4 %shard_map.68 = f32[2160,128]{1,0:T(8,128)} custom-call(f32[12,512]{1,0:T(8,128)S(1)} %get-tuple-element.21.masks, f32[4,135,512]{2,1,0:T(8,128)S(1)} %shard_map.67.states, bf16[4,288,256]{2,1,0:T(8,128)(2,1)S(1)} %get-tuple-element.35.chains, f32[135,512]{1,0:T(8,128)S(1)} %collective-permute-done.5.incoming), custom_call_target="tpu_custom_call" | custom-call | flops 223948800 | bytes 1048576 | tf_op jit(solution)/shard_map/pallas_call | solution.py:543
Async XLA Ops:
  1.9 13.0 %collective-permute-start.3 = (bf16[4,136,128]{2,1,0:T(8,128)(2,1)S(1)}, bf16[4,136,128]{2,1,0:T(8,128)(2,1)S(1)}, u32[]{:S(2)}, u32[]{:S(2)}) collective-permute-start(bf16[4,136,128]{2,1,0:T(8,128)(2,1)S(1)} %get-tuple-element.29), channel_id=1, source_target_pairs={{0,4},{4,0},{8,12},{12,8},{1,5},{5,1},{9,13},{13,9},{2,6},{6,2},{1... | collective-permute-start | bytes 417800 | tf_op jit(solution)/shard_map/ppermute | solution.py:419
  2.2 12.7 %collective-permute-start.4 = (bf16[4,136,128]{2,1,0:T(8,128)(2,1)S(1)}, bf16[4,136,128]{2,1,0:T(8,128)(2,1)S(1)}, u32[]{:S(2)}, u32[]{:S(2)}) collective-permute-start(bf16[4,136,128]{2,1,0:T(8,128)(2,1)S(1)} %get-tuple-element.30), channel_id=1, source_target_pairs={{4,8},{8,4},{5,9},{9,5},{6,10},{10,6},{7,11},{11,7},{20,24},{24,20... | collective-permute-start | bytes 417800 | tf_op jit(solution)/shard_map/ppermute | solution.py:419
  6.3 8.6 %collective-permute-start = (bf16[540,128]{1,0:T(8,128)(2,1)S(1)}, bf16[540,128]{1,0:T(8,128)(2,1)S(1)}, u32[]{:S(2)}, u32[]{:S(2)}) collective-permute-start(bf16[540,128]{1,0:T(8,128)(2,1)S(1)} %get-tuple-element.26), channel_id=1, source_target_pairs={{0,16},{16,0},{1,17},{17,1},{2,18},{18,2},{3,19},{19,3},{4,20},{20... | collective-permute-start | bytes 414728 | tf_op jit(solution)/shard_map/ppermute | solution.py:419
  7.6 7.2 %collective-permute-start.1 = (bf16[16,135]{1,0:T(8,128)(2,1)S(1)}, bf16[16,135]{1,0:T(8,128)(2,1)S(1)}, u32[]{:S(2)}, u32[]{:S(2)}) collective-permute-start(bf16[16,135]{1,0:T(8,128)(2,1)S(1)} %get-tuple-element.27), channel_id=1, source_target_pairs={{0,1},{1,0},{2,3},{3,2},{4,5},{5,4},{6,7},{7,6},{8,9},{9,8},{10,11... | collective-permute-start | bytes 12968 | tf_op jit(solution)/shard_map/ppermute | solution.py:419
  7.8 7.1 %collective-permute-start.2 = (bf16[16,135]{1,0:T(8,128)(2,1)S(1)}, bf16[16,135]{1,0:T(8,128)(2,1)S(1)}, u32[]{:S(2)}, u32[]{:S(2)}) collective-permute-start(bf16[16,135]{1,0:T(8,128)(2,1)S(1)} %get-tuple-element.28), channel_id=1, source_target_pairs={{1,2},{2,1},{5,6},{6,5},{9,10},{10,9},{13,14},{14,13},{17,18},{18,... | collective-permute-start | bytes 12968 | tf_op jit(solution)/shard_map/ppermute | solution.py:419
  16.8 2.0 %collective-permute-start.5 = (f32[135,512]{1,0:T(8,128)S(1)}, f32[135,512]{1,0:T(8,128)S(1)}, u32[]{:S(2)}, u32[]{:S(2)}) collective-permute-start(f32[135,512]{1,0:T(8,128)S(1)} %get-tuple-element.36), channel_id=1, source_target_pairs={{0,16},{16,0},{1,17},{17,1},{2,18},{18,2},{3,19},{19,3},{4,20},{20... | collective-permute-start | bytes 829448 | tf_op jit(solution)/shard_map/ppermute | solution.py:419

commit v6 on v5

--- a/solution.py
+++ b/solution.py
@@ -299,7 +299,7 @@
             rests[z, :, window] = rest_of(value, head, count)
     wide_right[0:rows, :] = right[...].astype(F32)
     wide_follow[0:block, :] = jnp.where(has_next, follow[...].astype(F32), 0.0)
-    even, odd = side_even[...].astype(F32), side_odd[...].astype(F32)
+    even, odd = side_even[...].astype(F32), without_wrap(side_odd[...].astype(F32), "cy")
     total = bands * across
     sides[0:total, 0:count] = jnp.where(odd_y, even, odd)
     sides[total : 2 * total, 0:count] = jnp.where(odd_y, odd, even)
@@ -357,9 +357,17 @@
     last_band[...] = apply_halves(reach[...], (high_stack[...], low_stack[...]), count)
 
 
+def without_wrap(value, axis):
+    size = lax.axis_size(axis)
+    if size % 2:
+        return value
+    index = lax.axis_index(axis)
+    return jnp.where((index > 0) & (index < size - 1), value, 0.0)
+
+
 def edges_of(face_even, face_odd, z):
     odd_x = lax.axis_index("cx") % 2 == 1
-    even, odd = face_even[z].astype(F32), face_odd[z].astype(F32)
+    even, odd = face_even[z].astype(F32), without_wrap(face_odd[z].astype(F32), "cx")
     return jnp.where(odd_x, even, odd), jnp.where(odd_x, odd, even)
 
 
@@ -413,9 +421,11 @@
 
 
 def swapped(value, axis, first):
+    size = lax.axis_size(axis)
     pairs = []
-    for left in range(first, lax.axis_size(axis) - 1, 2):
-        pairs += [(left, left + 1), (left + 1, left)]
+    for left in range(first, size - 1 + first * (1 - size % 2), 2):
+        right = (left + 1) % size
+        pairs += [(left, right), (right, left)]
     return lax.ppermute(value, axis, pairs)
 
 

time: 20.4 us -> 18.6 us (0.912)
  the two profiles are of different devices: /device:TPU:11 before, /device:TPU:0 now
where the time goes in v6:
time: 18.6 us; the launch traced here: 18.4 us
  Pallas kernels  9.23 us (50%)
  starting transfers between devices  8.65 us (47%)
  waiting for transfers between devices  0.5 us (3%)
    ppermute x6, starting transfers between devices, swapped(): return lax.ppermute(value, axis, pairs)  8.65 us
    pallas_call x1, Pallas kernels, on_device(): call(functools.partial(matrix_kernel, bands, count), (field, shape((bands...  2.73 us
    pallas_call x1, Pallas kernels, on_device(): call(functools.partial(local_kernel, bands, count, across), (shape((bands...  1.92 us
    pallas_call x1, Pallas kernels, on_device(): call(functools.partial(pack_kernel, bands, count, across), (field, face,...  1.9 us
    pallas_call x1, Pallas kernels, on_device(): call(functools.partial(finish_kernel, bands, count, across), shape((rows,...  1.4 us
    pallas_call x1, Pallas kernels, on_device(): call(functools.partial(sweep_kernel, bands, count), shape((bands, count,...  1.27 us
    ppermute x6, waiting for transfers between devices, swapped(): return lax.ppermute(value, axis, pairs)  0.5 us
  transfers between devices with their start and end apart: 6, of which 2 were waited for; matrix products, arithmetic and copies ran while one was open for 0% of the time, Pallas kernels for 22%

profile of v6, /device:TPU:0, one launch (start us, length us, event | category | flops | bytes accessed | tf_op | source)
XLA Modules:
  0.0 18.4 jit_solution(15361801290710112409)
XLA Ops:
  0.0 1.9 %shard_map.64 = (bf16[2160,128]{1,0:T(8,128)(2,1)S(1)}, bf16[4,136,128]{2,1,0:T(8,128)(2,1)S(1)}, bf16[4,136,128]{2,1,0:T(8,128)(2,1)S(1)}, bf16[16,135]{1,0:T(8...) custom-call(bf16[2160,128]{1,0:T(8,128)(2,1)} %bitcast.8, ...), custom_call_target="tpu_custom_call" | custom-call | bytes 1105920 | tf_op jit(solution)/shard_map/pallas_call | solution.py:468
  1.9 3.0 %collective-permute-start.3 = (bf16[4,136,128]{2,1,0:T(8,128)(2,1)S(1)}, bf16[4,136,128]{2,1,0:T(8,128)(2,1)S(1)}, u32[]{:S(2)}, u32[]{:S(2)}) collective-permute-start(bf16[4,136,128]{2,1,0:T(8,128)(2,1)S(1)} %get-tuple-element.29), channel_id=1, source_target_pairs={{0,4},{4,0},{8,12},{12,8},{1,5},{5,1},{9,13},{13,9},{2,6},{6,2},{1... | collective-permute-start | bytes 417800 | tf_op jit(solution)/shard_map/ppermute | solution.py:429
  4.9 1.5 %collective-permute-start.4 = (bf16[4,136,128]{2,1,0:T(8,128)(2,1)S(1)}, bf16[4,136,128]{2,1,0:T(8,128)(2,1)S(1)}, u32[]{:S(2)}, u32[]{:S(2)}) collective-permute-start(bf16[4,136,128]{2,1,0:T(8,128)(2,1)S(1)} %get-tuple-element.30), channel_id=1, source_target_pairs={{4,8},{8,4},{12,0},{0,12},{5,9},{9,5},{13,1},{1,13},{6,10},{10,6},... | collective-permute-start | bytes 417800 | tf_op jit(solution)/shard_map/ppermute | solution.py:429
  6.4 0.0 collective-permute-start
  6.4 1.6 %collective-permute-start.1 = (bf16[16,135]{1,0:T(8,128)(2,1)S(1)}, bf16[16,135]{1,0:T(8,128)(2,1)S(1)}, u32[]{:S(2)}, u32[]{:S(2)}) collective-permute-start(bf16[16,135]{1,0:T(8,128)(2,1)S(1)} %get-tuple-element.27), channel_id=1, source_target_pairs={{0,1},{1,0},{2,3},{3,2},{4,5},{5,4},{6,7},{7,6},{8,9},{9,8},{10,11... | collective-permute-start | bytes 12968 | tf_op jit(solution)/shard_map/ppermute | solution.py:429
  8.0 2.5 %collective-permute-start.2 = (bf16[16,135]{1,0:T(8,128)(2,1)S(1)}, bf16[16,135]{1,0:T(8,128)(2,1)S(1)}, u32[]{:S(2)}, u32[]{:S(2)}) collective-permute-start(bf16[16,135]{1,0:T(8,128)(2,1)S(1)} %get-tuple-element.28), channel_id=1, source_target_pairs={{1,2},{2,1},{3,0},{0,3},{5,6},{6,5},{7,4},{4,7},{9,10},{10,9},{11,... | collective-permute-start | bytes 12968 | tf_op jit(solution)/shard_map/ppermute | solution.py:429
  10.5 2.7 %shard_map.65 = (bf16[2160,128]{1,0:T(8,128)(2,1)S(1)}, bf16[4,288,768]{2,1,0:T(8,128)(2,1)S(1)}, bf16[4,288,256]{2,1,0:T(8,128)(2,1)S(1)}, bf16[288,640]{1,0:T(8,128)(2,1)S(1)}, bf16[4,288,256]{2,1,0:T(8,128)(2,1)S(1)}) custom-call(s32[4]{0:T(128)} %pattern_far.3, f32[6,135,4,135]{3,2,1,0:T(4,128)} %bitcast.7, bf16[2160,128]{1,0:T(8,128)(2,1)} %bitcast.10, ...), custom_call_target="tpu_custom_call" | custom-call | flops 373248000 | bytes 4194304 | tf_op jit(solution)/shard_map/pallas_call | solution.py:494
  13.2 0.0 collective-permute-done.1.side_even
  13.2 0.2 %collective-permute-done.2.side_odd = bf16[16,135]{1,0:T(8,128)(2,1)S(1)} collective-permute-done((bf16[16,135]{1,0:T(8,128)(2,1)S(1)}, bf16[16,135]{1,0:T(8,128)(2,1)S(1)}, u32[]{:S(2)}, u32[]{:S(2)}) %collective-permute-start.2) | collective-permute-done | bytes 4352 | tf_op jit(solution)/shard_map/ppermute | solution.py:429
  13.5 0.0 collective-permute-done.follow
  13.5 0.0 collective-permute-done.3.face_even
  13.5 0.0 collective-permute-done.4.face_odd
  13.5 1.9 %shard_map.66 = (f32[4,135,512]{2,1,0:T(8,128)S(1)}, f32[135,512]{1,0:T(8,128)S(1)}) custom-call(bf16[2160,128]{1,0:T(8,128)(2,1)S(1)} %get-tuple-element.24.right, bf16[2160,128]{1,0:T(8,128)(2,1)S(1)} %get-tuple-element.25.prev, bf16[540,128]{1,0:T(8,128)(2,1)S(1)} %collective-permute-done.follow, bf16[16,135]{1,0:T(8,128)(2,1)S(1)} %collective-permute-done.1.side_even, ...), custom_call_target="tpu_custom_call" | custom-call | flops 970444800 | bytes 1048576 | tf_op jit(solution)/shard_map/pallas_call | solution.py:515
  15.4 0.1 collective-permute-start.5
  15.5 1.3 %shard_map.67.states = f32[4,135,512]{2,1,0:T(8,128)S(1)} custom-call(f32[4,135,512]{2,1,0:T(8,128)S(1)} %get-tuple-element.33.base, f32[12,512]{1,0:T(8,128)S(1)} %get-tuple-element.21.masks, bf16[4,288,256]{2,1,0:T(8,128)(2,1)S(1)} %get-tuple-element.22.inverse_maps, bf16[4,288,256]{2,1,0:T(8,128)(2,1)S(1)} %get-tuple-element.34.step_maps), custom_call_target="tpu_custom_call" | custom-call | flops 522547200 | bytes 1048576 | tf_op jit(solution)/shard_map/pallas_call | solution.py:534
  16.8 0.3 %collective-permute-done.5.incoming = f32[135,512]{1,0:T(8,128)S(1)} collective-permute-done((f32[135,512]{1,0:T(8,128)S(1)}, f32[135,512]{1,0:T(8,128)S(1)}, u32[]{:S(2)}, u32[]{:S(2)}) %collective-permute-start.5) | collective-permute-done | bytes 276512 | tf_op jit(solution)/shard_map/ppermute | solution.py:429
  17.0 1.4 %shard_map.68 = f32[2160,128]{1,0:T(8,128)} custom-call(f32[12,512]{1,0:T(8,128)S(1)} %get-tuple-element.21.masks, f32[4,135,512]{2,1,0:T(8,128)S(1)} %shard_map.67.states, bf16[4,288,256]{2,1,0:T(8,128)(2,1)S(1)} %get-tuple-element.35.chains, f32[135,512]{1,0:T(8,128)S(1)} %collective-permute-done.5.incoming), custom_call_target="tpu_custom_call" | custom-call | flops 223948800 | bytes 1048576 | tf_op jit(solution)/shard_map/pallas_call | solution.py:553
Async XLA Ops:
  1.9 11.6 %collective-permute-start.3 = (bf16[4,136,128]{2,1,0:T(8,128)(2,1)S(1)}, bf16[4,136,128]{2,1,0:T(8,128)(2,1)S(1)}, u32[]{:S(2)}, u32[]{:S(2)}) collective-permute-start(bf16[4,136,128]{2,1,0:T(8,128)(2,1)S(1)} %get-tuple-element.29), channel_id=1, source_target_pairs={{0,4},{4,0},{8,12},{12,8},{1,5},{5,1},{9,13},{13,9},{2,6},{6,2},{1... | collective-permute-start | bytes 417800 | tf_op jit(solution)/shard_map/ppermute | solution.py:429
  4.9 8.5 %collective-permute-start.4 = (bf16[4,136,128]{2,1,0:T(8,128)(2,1)S(1)}, bf16[4,136,128]{2,1,0:T(8,128)(2,1)S(1)}, u32[]{:S(2)}, u32[]{:S(2)}) collective-permute-start(bf16[4,136,128]{2,1,0:T(8,128)(2,1)S(1)} %get-tuple-element.30), channel_id=1, source_target_pairs={{4,8},{8,4},{12,0},{0,12},{5,9},{9,5},{13,1},{1,13},{6,10},{10,6},... | collective-permute-start | bytes 417800 | tf_op jit(solution)/shard_map/ppermute | solution.py:429
  6.4 7.0 %collective-permute-start = (bf16[540,128]{1,0:T(8,128)(2,1)S(1)}, bf16[540,128]{1,0:T(8,128)(2,1)S(1)}, u32[]{:S(2)}, u32[]{:S(2)}) collective-permute-start(bf16[540,128]{1,0:T(8,128)(2,1)S(1)} %get-tuple-element.26), channel_id=1, source_target_pairs={{0,16},{16,0},{1,17},{17,1},{2,18},{18,2},{3,19},{19,3},{4,20},{20... | collective-permute-start | bytes 414728 | tf_op jit(solution)/shard_map/ppermute | solution.py:429
  6.4 6.8 %collective-permute-start.1 = (bf16[16,135]{1,0:T(8,128)(2,1)S(1)}, bf16[16,135]{1,0:T(8,128)(2,1)S(1)}, u32[]{:S(2)}, u32[]{:S(2)}) collective-permute-start(bf16[16,135]{1,0:T(8,128)(2,1)S(1)} %get-tuple-element.27), channel_id=1, source_target_pairs={{0,1},{1,0},{2,3},{3,2},{4,5},{5,4},{6,7},{7,6},{8,9},{9,8},{10,11... | collective-permute-start | bytes 12968 | tf_op jit(solution)/shard_map/ppermute | solution.py:429
  8.0 5.4 %collective-permute-start.2 = (bf16[16,135]{1,0:T(8,128)(2,1)S(1)}, bf16[16,135]{1,0:T(8,128)(2,1)S(1)}, u32[]{:S(2)}, u32[]{:S(2)}) collective-permute-start(bf16[16,135]{1,0:T(8,128)(2,1)S(1)} %get-tuple-element.28), channel_id=1, source_target_pairs={{1,2},{2,1},{3,0},{0,3},{5,6},{6,5},{7,4},{4,7},{9,10},{10,9},{11,... | collective-permute-start | bytes 12968 | tf_op jit(solution)/shard_map/ppermute | solution.py:429
  15.4 1.6 %collective-permute-start.5 = (f32[135,512]{1,0:T(8,128)S(1)}, f32[135,512]{1,0:T(8,128)S(1)}, u32[]{:S(2)}, u32[]{:S(2)}) collective-permute-start(f32[135,512]{1,0:T(8,128)S(1)} %get-tuple-element.36), channel_id=1, source_target_pairs={{0,16},{16,0},{1,17},{17,1},{2,18},{18,2},{3,19},{19,3},{4,20},{20... | collective-permute-start | bytes 829448 | tf_op jit(solution)/shard_map/ppermute | solution.py:429

commit v7 on v5

--- a/solution.py
+++ b/solution.py
@@ -91,8 +91,8 @@
 
 def pack_kernel(
     bands, count, across, prev, pattern_far, live_far, faces, inverses,
-    kept, face_even, face_odd, side_even, side_odd, first, inverse_maps, upstream_maps, masks,
-    wide, rows_even, rows_odd, main, tail, inverse_main, inverse_tail, staged, pattern, live, sems,
+    kept, face_up, face_down, side_up, side_down, first, inverse_maps, upstream_maps, masks,
+    wide, rows_up, rows_down, main, tail, inverse_main, inverse_tail, staged, pattern, live, sems,
 ):
     along = prev.shape[-1]
     rows = prev.shape[0]
@@ -117,13 +117,9 @@
         copy.start()
     staged[...] = jnp.zeros(staged.shape, F32)
     wide[rows:, :] = jnp.zeros((wide.shape[0] - rows, along), F32)
-    odd_x = lax.axis_index("cx") % 2 == 1
-    odd_y = lax.axis_index("cy") % 2 == 1
     row = lax.broadcasted_iota(jnp.int32, (8, along), 0)
     lane = lax.broadcasted_iota(jnp.int32, (8, along), 1)
-    last = along - 1
-    even_lane, odd_lane = jnp.where(odd_y, 0, last), jnp.where(odd_y, last, 0)
-    chosen = jnp.where(row == 0, even_lane, odd_lane)
+    chosen = jnp.where(row == 0, along - 1, 0)
     pick = jnp.where(lane == chosen, 1.0, 0.0).astype(BF16)
     size = rows // len(copies)
     done = 0
@@ -135,18 +131,18 @@
             done += 1
         blocks = lane_blocks(wide, z * count * across, rest_rows(count), across)
         low, high = blocks[0], blocks[-1]
-        face_even[z] = jnp.where(odd_x, low, high).astype(BF16)
-        face_odd[z] = jnp.where(odd_x, high, low).astype(BF16)
+        face_up[z] = high.astype(BF16)
+        face_down[z] = low.astype(BF16)
         for i in range(across):
             found = lax.dot_general(
                 pick, blocks[i][0:count].astype(BF16), (((1,), (1,)), ((), ())), preferred_element_type=F32
             )
             at = z * across + i
-            rows_even[at : at + 1, :] = found[0:1]
-            rows_odd[at : at + 1, :] = found[1:2]
+            rows_up[at : at + 1, :] = found[0:1]
+            rows_down[at : at + 1, :] = found[1:2]
     first[...] = kept[0 : count * across, :]
-    side_even[...] = rows_even[...].astype(BF16)
-    side_odd[...] = rows_odd[...].astype(BF16)
+    side_up[...] = rows_up[...].astype(BF16)
+    side_down[...] = rows_down[...].astype(BF16)
     for copy in small:
         copy.wait()
     slot = lax.broadcasted_iota(jnp.int32, (1, masks.shape[-1]), 1)
@@ -281,7 +277,7 @@
 
 
 def local_kernel(
-    bands, count, across, right, prev, follow, side_even, side_odd, face_even, face_odd, maps, reach, masks,
+    bands, count, across, right, prev, follow, side_up, side_down, face_up, face_down, maps, reach, masks,
     base, last_band, heads, rests, wide, wide_right, wide_follow, sides, shifted, rest_stacks, high_stack, low_stack,
 ):
     rows, along = right.shape
@@ -289,7 +285,6 @@
     deep = rest_rows(count)
     head = count // 128 * 128
     edge = (across - 1) * along
-    odd_y = lax.axis_index("cy") % 2 == 1
     has_next = lax.axis_index("sweep") < lax.axis_size("sweep") - 1
     wide[0:rows, :] = prev[...].astype(F32)
     for z in range(bands):
@@ -299,10 +294,10 @@
             rests[z, :, window] = rest_of(value, head, count)
     wide_right[0:rows, :] = right[...].astype(F32)
     wide_follow[0:block, :] = jnp.where(has_next, follow[...].astype(F32), 0.0)
-    even, odd = side_even[...].astype(F32), side_odd[...].astype(F32)
+    minus, plus = between(side_up[...], side_down[...], "cy")
     total = bands * across
-    sides[0:total, 0:count] = jnp.where(odd_y, even, odd)
-    sides[total : 2 * total, 0:count] = jnp.where(odd_y, odd, even)
+    sides[0:total, 0:count] = minus
+    sides[total : 2 * total, 0:count] = plus
     columns = sides[...].T
     lane = lax.broadcasted_iota(jnp.int32, (deep, along), 1)
     beyond = lane_blocks(wide_follow, 0, deep, across)
@@ -310,7 +305,7 @@
     beyond_rest = jnp.concatenate([rest_of(value, head, count) for value in beyond], axis=1)
     final_rests = []
     for z in range(bands):
-        minus, plus = edges_of(face_even, face_odd, z)
+        minus, plus = between(face_up[z], face_down[z], "cx")
         behind_rests, ahead_rests = [], []
         for i in range(across):
             window = slice(i * along, (i + 1) * along)
@@ -357,10 +352,10 @@
     last_band[...] = apply_halves(reach[...], (high_stack[...], low_stack[...]), count)
 
 
-def edges_of(face_even, face_odd, z):
-    odd_x = lax.axis_index("cx") % 2 == 1
-    even, odd = face_even[z].astype(F32), face_odd[z].astype(F32)
-    return jnp.where(odd_x, even, odd), jnp.where(odd_x, odd, even)
+def between(upward, downward, axis):
+    index = lax.axis_index(axis)
+    minus = jnp.where(index > 0, upward.astype(F32), 0.0)
+    return minus, jnp.where(index < lax.axis_size(axis) - 1, downward.astype(F32), 0.0)
 
 
 def sweep_kernel(bands, count, base, masks, inverse_maps, step_maps, states):
@@ -412,17 +407,15 @@
     return pltpu.with_memory_space_constraint(value, pltpu.HBM)
 
 
-def swapped(value, axis, first):
-    pairs = []
-    for left in range(first, lax.axis_size(axis) - 1, 2):
-        pairs += [(left, left + 1), (left + 1, left)]
-    return lax.ppermute(value, axis, pairs)
+def around(value, axis, steps):
+    size = lax.axis_size(axis)
+    return lax.ppermute(value, axis, [(i, (i + steps) % size) for i in range(size)])
 
 
 def passed_along(value, axis, steps):
     count = lax.axis_size(axis)
     if count == 2:
-        return swapped(value, axis, 0)
+        return around(value, axis, steps)
     first, last = (max(0, -steps), min(count, count - steps))
     return lax.ppermute(value, axis, [(source, source + steps) for source in range(first, last)])
 
@@ -454,7 +447,7 @@
     ]
     small_room = pltpu.SMEM((bands,), jnp.int32)
     (
-        kept, face_even, face_odd, side_even, side_odd, first, inverse_maps, upstream_maps, masks
+        kept, face_up, face_down, side_up, side_down, first, inverse_maps, upstream_maps, masks
     ) = call(
         functools.partial(pack_kernel, bands, count, across),
         (
@@ -474,11 +467,11 @@
         + [pltpu.VMEM((2 * bands, pads // 2, lanes), F32), small_room, small_room, pltpu.SemaphoreType.DMA((8,))],
         moved=rows * along * 4,
     )(prev, pattern, live, faces, inverses)
-    side_even = swapped(side_even, "cy", 0)
-    side_odd = swapped(side_odd, "cy", 1)
+    side_up = around(side_up, "cy", 1)
+    side_down = around(side_down, "cy", -1)
     follow = passed_along(first, "sweep", -1)
-    face_odd = swapped(face_odd, "cx", 1)
-    face_even = swapped(face_even, "cx", 0)
+    face_down = around(face_down, "cx", -1)
+    face_up = around(face_up, "cx", 1)
     step_flops = count * count * cells * 2
     used = face_total - 1
     right_kept, maps, step_maps, reach, chains = call(
@@ -520,7 +513,7 @@
         ],
         flops=bands * 13 * step_flops,
         moved=2**20,
-    )(right_kept, kept, follow, side_even, side_odd, face_even, face_odd, maps, reach, masks)
+    )(right_kept, kept, follow, side_up, side_down, face_up, face_down, maps, reach, masks)
     states = call(
         functools.partial(sweep_kernel, bands, count),
         shape((bands, count, cells), F32),

time: 20.4 us -> 17.9 us (0.88)
  the two profiles are of different devices: /device:TPU:11 before, /device:TPU:0 now
where the time goes in v7:
time: 17.9 us; the launch traced here: 17.7 us
  Pallas kernels  9.22 us (52%)
  starting transfers between devices  8.33 us (47%)
    ppermute x6, starting transfers between devices, around(): lax.ppermute(value, axis, [(i, (i + steps) % size) for i in range(size)])  8.33 us
    pallas_call x1, Pallas kernels, on_device(): call(functools.partial(matrix_kernel, bands, count), (field, shape((bands...  2.73 us
    pallas_call x1, Pallas kernels, on_device(): call(functools.partial(pack_kernel, bands, count, across), (field, face,...  1.93 us
    pallas_call x1, Pallas kernels, on_device(): call(functools.partial(local_kernel, bands, count, across), (shape((bands...  1.9 us
    pallas_call x1, Pallas kernels, on_device(): call(functools.partial(finish_kernel, bands, count, across), shape((rows,...  1.4 us
    pallas_call x1, Pallas kernels, on_device(): call(functools.partial(sweep_kernel, bands, count), shape((bands, count,...  1.26 us
  transfers between devices with their start and end apart: 6, of which 1 were waited for; matrix products, arithmetic and copies ran while one was open for 0% of the time, Pallas kernels for 23%

profile of v7, /device:TPU:0, one launch (start us, length us, event | category | flops | bytes accessed | tf_op | source)
XLA Modules:
  0.0 17.7 jit_solution(16216797374907448611)
XLA Ops:
  0.0 1.9 %shard_map.64 = (bf16[2160,128]{1,0:T(8,128)(2,1)S(1)}, bf16[4,136,128]{2,1,0:T(8,128)(2,1)S(1)}, bf16[4,136,128]{2,1,0:T(8,128)(2,1)S(1)}, bf16[16,135]{1,0:T(8...) custom-call(bf16[2160,128]{1,0:T(8,128)(2,1)} %bitcast.8, ...), custom_call_target="tpu_custom_call" | custom-call | bytes 1105920 | tf_op jit(solution)/shard_map/pallas_call | solution.py:451
  1.9 3.0 %collective-permute-start.3 = (bf16[4,136,128]{2,1,0:T(8,128)(2,1)S(1)}, bf16[4,136,128]{2,1,0:T(8,128)(2,1)S(1)}, u32[]{:S(2)}, u32[]{:S(2)}) collective-permute-start(bf16[4,136,128]{2,1,0:T(8,128)(2,1)S(1)} %get-tuple-element.29), channel_id=1, source_target_pairs={{0,4},{4,8},{8,12},{12,0},{1,5},{5,9},{9,13},{13,1},{2,6},{6,10},{... | collective-permute-start | bytes 417800 | tf_op jit(solution)/shard_map/ppermute | solution.py:412
  5.0 1.0 %collective-permute-start.4 = (bf16[4,136,128]{2,1,0:T(8,128)(2,1)S(1)}, bf16[4,136,128]{2,1,0:T(8,128)(2,1)S(1)}, u32[]{:S(2)}, u32[]{:S(2)}) collective-permute-start(bf16[4,136,128]{2,1,0:T(8,128)(2,1)S(1)} %get-tuple-element.30), channel_id=1, source_target_pairs={{0,12},{4,0},{8,4},{12,8},{1,13},{5,1},{9,5},{13,9},{2,14},{6,2},{... | collective-permute-start | bytes 417800 | tf_op jit(solution)/shard_map/ppermute | solution.py:412
  6.0 0.0 collective-permute-start
  6.0 2.0 %collective-permute-start.1 = (bf16[16,135]{1,0:T(8,128)(2,1)S(1)}, bf16[16,135]{1,0:T(8,128)(2,1)S(1)}, u32[]{:S(2)}, u32[]{:S(2)}) collective-permute-start(bf16[16,135]{1,0:T(8,128)(2,1)S(1)} %get-tuple-element.27), channel_id=1, source_target_pairs={{0,1},{1,2},{2,3},{3,0},{4,5},{5,6},{6,7},{7,4},{8,9},{9,10},{10,1... | collective-permute-start | bytes 12968 | tf_op jit(solution)/shard_map/ppermute | solution.py:412
  8.0 2.0 %collective-permute-start.2 = (bf16[16,135]{1,0:T(8,128)(2,1)S(1)}, bf16[16,135]{1,0:T(8,128)(2,1)S(1)}, u32[]{:S(2)}, u32[]{:S(2)}) collective-permute-start(bf16[16,135]{1,0:T(8,128)(2,1)S(1)} %get-tuple-element.28), channel_id=1, source_target_pairs={{0,3},{1,0},{2,1},{3,2},{4,7},{5,4},{6,5},{7,6},{8,11},{9,8},{10,9... | collective-permute-start | bytes 12968 | tf_op jit(solution)/shard_map/ppermute | solution.py:412
  10.0 2.7 %shard_map.65 = (bf16[2160,128]{1,0:T(8,128)(2,1)S(1)}, bf16[4,288,768]{2,1,0:T(8,128)(2,1)S(1)}, bf16[4,288,256]{2,1,0:T(8,128)(2,1)S(1)}, bf16[288,640]{1,0:T(8,128)(2,1)S(1)}, bf16[4,288,256]{2,1,0:T(8,128)(2,1)S(1)}) custom-call(s32[4]{0:T(128)} %pattern_far.3, f32[6,135,4,135]{3,2,1,0:T(4,128)} %bitcast.7, bf16[2160,128]{1,0:T(8,128)(2,1)} %bitcast.10, ...), custom_call_target="tpu_custom_call" | custom-call | flops 373248000 | bytes 4194304 | tf_op jit(solution)/shard_map/pallas_call | solution.py:477
  12.7 0.0 collective-permute-done.1.side_up
  12.7 0.0 collective-permute-done.2.side_down
  12.8 0.0 collective-permute-done.follow
  12.8 0.0 collective-permute-done.3.face_up
  12.8 0.0 collective-permute-done.4.face_down
  12.8 1.9 %shard_map.66 = (f32[4,135,512]{2,1,0:T(8,128)S(1)}, f32[135,512]{1,0:T(8,128)S(1)}) custom-call(bf16[2160,128]{1,0:T(8,128)(2,1)S(1)} %get-tuple-element.24.right, bf16[2160,128]{1,0:T(8,128)(2,1)S(1)} %get-tuple-element.25.prev, bf16[540,128]{1,0:T(8,128)(2,1)S(1)} %collective-permute-done.follow, bf16[16,135]{1,0:T(8,128)(2,1)S(1)} %collective-permute-done.1.side_up, ...), custom_call_target="tpu_custom_call" | custom-call | flops 970444800 | bytes 1048576 | tf_op jit(solution)/shard_map/pallas_call | solution.py:498
  14.7 0.3 %collective-permute-start.5 = (f32[135,512]{1,0:T(8,128)S(1)}, f32[135,512]{1,0:T(8,128)S(1)}, u32[]{:S(2)}, u32[]{:S(2)}) collective-permute-start(f32[135,512]{1,0:T(8,128)S(1)} %get-tuple-element.36), channel_id=1, source_target_pairs={{0,16},{16,0},{1,17},{17,1},{2,18},{18,2},{3,19},{19,3},{4,20},{20... | collective-permute-start | bytes 829448 | tf_op jit(solution)/shard_map/ppermute | solution.py:412
  15.0 1.3 %shard_map.67.states = f32[4,135,512]{2,1,0:T(8,128)S(1)} custom-call(f32[4,135,512]{2,1,0:T(8,128)S(1)} %get-tuple-element.33.base, f32[12,512]{1,0:T(8,128)S(1)} %get-tuple-element.21.masks, bf16[4,288,256]{2,1,0:T(8,128)(2,1)S(1)} %get-tuple-element.22.inverse_maps, bf16[4,288,256]{2,1,0:T(8,128)(2,1)S(1)} %get-tuple-element.34.step_maps), custom_call_target="tpu_custom_call" | custom-call | flops 522547200 | bytes 1048576 | tf_op jit(solution)/shard_map/pallas_call | solution.py:517
  16.3 0.1 collective-permute-done.5.incoming
  16.3 1.4 %shard_map.68 = f32[2160,128]{1,0:T(8,128)} custom-call(f32[12,512]{1,0:T(8,128)S(1)} %get-tuple-element.21.masks, f32[4,135,512]{2,1,0:T(8,128)S(1)} %shard_map.67.states, bf16[4,288,256]{2,1,0:T(8,128)(2,1)S(1)} %get-tuple-element.35.chains, f32[135,512]{1,0:T(8,128)S(1)} %collective-permute-done.5.incoming), custom_call_target="tpu_custom_call" | custom-call | flops 223948800 | bytes 1048576 | tf_op jit(solution)/shard_map/pallas_call | solution.py:536
Async XLA Ops:
  1.9 10.8 %collective-permute-start.3 = (bf16[4,136,128]{2,1,0:T(8,128)(2,1)S(1)}, bf16[4,136,128]{2,1,0:T(8,128)(2,1)S(1)}, u32[]{:S(2)}, u32[]{:S(2)}) collective-permute-start(bf16[4,136,128]{2,1,0:T(8,128)(2,1)S(1)} %get-tuple-element.29), channel_id=1, source_target_pairs={{0,4},{4,8},{8,12},{12,0},{1,5},{5,9},{9,13},{13,1},{2,6},{6,10},{... | collective-permute-start | bytes 417800 | tf_op jit(solution)/shard_map/ppermute | solution.py:412
  5.0 7.9 %collective-permute-start.4 = (bf16[4,136,128]{2,1,0:T(8,128)(2,1)S(1)}, bf16[4,136,128]{2,1,0:T(8,128)(2,1)S(1)}, u32[]{:S(2)}, u32[]{:S(2)}) collective-permute-start(bf16[4,136,128]{2,1,0:T(8,128)(2,1)S(1)} %get-tuple-element.30), channel_id=1, source_target_pairs={{0,12},{4,0},{8,4},{12,8},{1,13},{5,1},{9,5},{13,9},{2,14},{6,2},{... | collective-permute-start | bytes 417800 | tf_op jit(solution)/shard_map/ppermute | solution.py:412
  6.0 6.8 %collective-permute-start = (bf16[540,128]{1,0:T(8,128)(2,1)S(1)}, bf16[540,128]{1,0:T(8,128)(2,1)S(1)}, u32[]{:S(2)}, u32[]{:S(2)}) collective-permute-start(bf16[540,128]{1,0:T(8,128)(2,1)S(1)} %get-tuple-element.26), channel_id=1, source_target_pairs={{0,16},{16,0},{1,17},{17,1},{2,18},{18,2},{3,19},{19,3},{4,20},{20... | collective-permute-start | bytes 414728 | tf_op jit(solution)/shard_map/ppermute | solution.py:412
  6.0 6.8 %collective-permute-start.1 = (bf16[16,135]{1,0:T(8,128)(2,1)S(1)}, bf16[16,135]{1,0:T(8,128)(2,1)S(1)}, u32[]{:S(2)}, u32[]{:S(2)}) collective-permute-start(bf16[16,135]{1,0:T(8,128)(2,1)S(1)} %get-tuple-element.27), channel_id=1, source_target_pairs={{0,1},{1,2},{2,3},{3,0},{4,5},{5,6},{6,7},{7,4},{8,9},{9,10},{10,1... | collective-permute-start | bytes 12968 | tf_op jit(solution)/shard_map/ppermute | solution.py:412
  8.0 4.8 %collective-permute-start.2 = (bf16[16,135]{1,0:T(8,128)(2,1)S(1)}, bf16[16,135]{1,0:T(8,128)(2,1)S(1)}, u32[]{:S(2)}, u32[]{:S(2)}) collective-permute-start(bf16[16,135]{1,0:T(8,128)(2,1)S(1)} %get-tuple-element.28), channel_id=1, source_target_pairs={{0,3},{1,0},{2,1},{3,2},{4,7},{5,4},{6,5},{7,6},{8,11},{9,8},{10,9... | collective-permute-start | bytes 12968 | tf_op jit(solution)/shard_map/ppermute | solution.py:412
  14.7 1.6 %collective-permute-start.5 = (f32[135,512]{1,0:T(8,128)S(1)}, f32[135,512]{1,0:T(8,128)S(1)}, u32[]{:S(2)}, u32[]{:S(2)}) collective-permute-start(f32[135,512]{1,0:T(8,128)S(1)} %get-tuple-element.36), channel_id=1, source_target_pairs={{0,16},{16,0},{1,17},{17,1},{2,18},{18,2},{3,19},{19,3},{4,20},{20... | collective-permute-start | bytes 829448 | tf_op jit(solution)/shard_map/ppermute | solution.py:412
